TPU v7x, 256 devices: a whole 4x4x8 slice. The times are simulated.
256 devices in a mesh: section: 4 (over x_hi, core), fsdp: 64 (over z, x_lo, y).
Axes of the slice: x: 4 (x_hi: 2, x_lo: 2; x = x_hi * 2 + x_lo), y: 4, z: 8, core: 2. Of those that a mesh axis runs over, the one named last changes fastest.
Arguments:
- signals: bfloat16 [16384, 1536], P('fsdp', 'section'), may hold values from -6 to 6
- conv_weight: bfloat16 [768, 9, 1536], P('fsdp', None, 'section'), may hold values from -0.078125 to 0.078125
- buckets: int32 [2, 2], replicated, may hold values from 0 to 8, as said below
Outputs:
- results: bfloat16 [16384, 1536], P('fsdp', 'section')
- grad_weight: float32 [768, 9, 1536], P('fsdp', None, 'section')
Inputs may be any that keep to these rules, and one draw needn't show every extreme that they name: `buckets`: a bucket b means 16 + 2 b live pixels along that side, in the top left of each sample's grid; microbatch 0 has a height bucket of 5 or more; some entry is 8.
All inputs are finite; a program needn't handle non-finite values.
Results may differ from a plain program's by a relative error of at most 0.0054.
Values may be sent and summed in bfloat16 or wider, within the bound.
No kernel may reach another device: no remote copies, remote signals or barrier semaphores. Data moves between devices by JAX's collectives and lax.ppermute only.
A program may use at most 128 MiB of HBM per device.

v0:
```python
import jax
import jax.numpy as jnp
from jax import lax
from jax.experimental import pallas as pl
from jax.experimental.pallas import tpu as pltpu
from jax.sharding import Mesh
from jax.sharding import PartitionSpec as P


AX = ("xh", "core", "z", "xl", "y")
SIZES = (2, 2, 8, 2, 4)
WEIGHT_GROUP = ("z", "xl")
GROUP_WIDTH = 24
OWN = 96
PIX = 1024
SIDE = 32
TAPS = 9
PAIR = 2 * OWN
QUAD = 4 * OWN
LANES = TAPS * PAIR
EPS = 1e-05
F32 = jnp.float32
BF16 = jnp.bfloat16


def flat(xh, core, z, xl, y):
    return (((xh * 2 + core) * 8 + z) * 2 + xl) * 4 + y


def every():
    for xh in range(2):
        for core in range(2):
            for z in range(8):
                for xl in range(2):
                    for y in range(4):
                        yield xh, core, z, xl, y


def pixel_pairs(turn):
    pairs = []
    for xh, core, z, xl, y in every():
        slot = ((z * 2 + xl) * 4 + y + 1) % 64
        sample, piece = slot // 4, slot % 4
        u = (piece + turn) % 4
        pairs.append(
            (flat(xh, core, z, xl, y), flat(xh, u % 2, sample // 2, sample % 2, 2 * core + u // 2))
        )
    return pairs


def weight_pairs(second):
    pairs = []
    for xh, core, z, xl, y in every():
        b = (y & 1) ^ second
        if xh == 0:
            target = (0, z % 2, 2 * (z // 2) + xl, y >> 1, 2 * core + b)
        else:
            target = (1, b, 4 * core + 2 * (z % 2) + xl, y >> 1, z // 2)
        pairs.append((flat(xh, core, z, xl, y), flat(*target)))
    return pairs


def back(pairs):
    return [(b, a) for a, b in pairs]


def swap(value, axis):
    return lax.ppermute(value, axis, [(0, 1), (1, 0)])


def turn_y(value, d):
    return lax.ppermute(value, "y", [(i, (i + d) % 4) for i in range(4)])


def pixels():
    p = lax.broadcasted_iota(jnp.int32, (1, PIX), 1)
    return p >> 5, p & 31


def live(prm):
    row, col = pixels()
    return ((row < prm[3]) & (col < prm[4])).astype(F32)


def offsets(tap):
    return tap // 3 - 1, tap % 3 - 1


def moved(field, dr, dc):
    off = dr * SIDE + dc
    if off == 0:
        return field
    row, col = pixels()
    ok = (row + dr >= 0) & (row + dr < SIDE) & (col + dc >= 0) & (col + dc < SIDE)
    return jnp.where(ok, pltpu.roll(field, (-off) % PIX, 1), 0.0)


def group_sum(field):
    return jnp.sum(field.reshape(OWN // GROUP_WIDTH, GROUP_WIDTH, PIX), axis=(1, 2), keepdims=True)


def spread(stat):
    return jnp.broadcast_to(stat, (OWN // GROUP_WIDTH, GROUP_WIDTH, PIX)).reshape(OWN, PIX)


def normed_of(values, mask, count):
    masked = values * mask
    mean = group_sum(masked) / count
    var = group_sum(masked * masked) / count - mean * mean
    scale = spread(lax.rsqrt(var + EPS))
    return (values - spread(mean)) * scale, scale


def count_of(prm):
    return (prm[3] * prm[4] * GROUP_WIDTH).astype(F32)


def silu_slope(u, s):
    return s * (1.0 + u * (1.0 - s))


def input_slope(e, xhat, scale, mask, count):
    m1 = spread(group_sum(e) / count)
    m2 = spread(group_sum(e * xhat) / count)
    return mask * (e - m1 - xhat * m2) * scale


def rows(k, n=OWN):
    return pl.ds(pl.multiple_of(k * n, n), n)


def split_kernel(prm, x_ref, *refs):
    outs, scratch = refs[:4], refs[4]
    scratch[...] = x_ref[...].astype(F32).T.astype(BF16)
    for v in range(4):
        outs[v][...] = scratch[rows((prm[5] + v) % 4), :]


def join_kernel(prm, *refs):
    ins, out, scratch = refs[:4], refs[4], refs[5]
    for v in range(4):
        scratch[rows((prm[5] + v) % 4), :] = ins[v][...]
    out[...] = scratch[...].astype(F32).T.astype(BF16)


def start_kernel(prm, *refs):
    ins, x_out, a_out = refs[:4], refs[4], refs[5]
    u = 2 * (prm[2] % 2) + prm[1]
    for v in range(4):
        t = (u - v + 4) % 4
        x_out[:, pl.ds(pl.multiple_of(t * 256, 256), 256)] = ins[v][...]
    mask = live(prm)
    values = x_out[...].astype(F32) * mask
    xhat, _ = normed_of(values, mask, count_of(prm))
    act = mask * (xhat * jax.nn.sigmoid(xhat))
    a_out[...] = jnp.where(prm[0] == 0, act, values).astype(BF16)


def convolve(w, act):
    acc = jnp.zeros((PAIR, PIX), F32)
    for tap in range(0, TAPS, 2):
        n = min(2, TAPS - tap)
        part = lax.dot_general(
            w[:, tap * PAIR : (tap + n) * PAIR],
            act,
            (((0,), (0,)), ((), ())),
            preferred_element_type=F32,
        )
        for k in range(n):
            acc = acc + moved(part[k * PAIR : (k + 1) * PAIR], *offsets(tap + k))
    return acc


def build_moved(act, d_ref):
    act = act.astype(F32)
    for tap in range(TAPS):
        dr, dc = offsets(tap)
        d_ref[tap * PAIR : (tap + 1) * PAIR, :] = moved(act, -dr, -dc).astype(BF16)


def gather_chunks(prm, own, others, full):
    full[rows(prm[2]), :] = own[...]
    for d, ref in enumerate(others, 1):
        full[rows((prm[2] + 4 - d) % 4), :] = ref[...]


def first_kernel(prm, w, g, a0, a1, a2, a3, full, keep, send, d_ref, res):
    gather_chunks(prm, a0, (a1, a2, a3), full)

    @pl.when(prm[0] == 0)
    def _():
        res[...] = convolve(w[...], full[...])

    @pl.when(prm[0] == 1)
    def _():
        for k in range(2):
            build_moved(full[k * PAIR : (k + 1) * PAIR, :], d_ref)
            part = jnp.dot(
                w[k * PAIR : (k + 1) * PAIR, :], d_ref[...], preferred_element_type=F32
            )
            if k == 0:
                res[...] = part
            else:
                res[...] += part

    keep[...] = res[rows(prm[1]), :]
    send[...] = res[rows(1 - prm[1]), :]


def middle_kernel(prm, x, keep, got, out):
    mask = live(prm)
    total = keep[...] + got[...]
    values = x[...].astype(F32) * mask
    out[...] = jnp.where(prm[0] == 0, values + mask * total, total).astype(BF16)


def turn_kernel(prm, mine, theirs, g, b_out, q_out):
    mask = live(prm)
    count = count_of(prm)
    down = prm[0] == 0
    hidden = jnp.where(down, mine[...].astype(F32), theirs[...].astype(F32))
    xhat, scale = normed_of(hidden, mask, count)
    s = jax.nn.sigmoid(xhat)

    @pl.when(down)
    def _():
        e = mask * theirs[...].astype(F32) * silu_slope(xhat, s)
        dv = (g[...].astype(F32) + input_slope(e, xhat, scale, mask, count)).astype(BF16)
        q_out[...] = dv
        b_out[...] = (dv.astype(F32) * mask).astype(BF16)

    @pl.when(jnp.logical_not(down))
    def _():
        q_out[...] = theirs[...]
        b_out[...] = (mask * (xhat * s)).astype(BF16)


def pair_up(prm, own, other, pair):
    pair[rows(prm[1]), :] = own[...]
    pair[rows(1 - prm[1]), :] = other[...]


def weight_slope_kernel(prm, full, b_own, b_other, dw, pair, d_ref):
    pair_up(prm, b_own, b_other, pair)

    def product(lhs):
        return lax.dot_general(
            lhs, d_ref[...], (((1,), (1,)), ((), ())), preferred_element_type=F32
        ).astype(BF16)

    @pl.when(prm[0] == 0)
    def _():
        build_moved(pair[...], d_ref)
        dw[...] = product(full[...])

    @pl.when(prm[0] == 1)
    def _():
        for k in range(2):
            build_moved(full[k * PAIR : (k + 1) * PAIR, :], d_ref)
            dw[k * PAIR : (k + 1) * PAIR, :] = product(pair[...])


def second_kernel(prm, w, b_own, b_other, keep, s1, s2, s3, pair, d_ref, res):
    pair_up(prm, b_own, b_other, pair)

    @pl.when(prm[0] == 0)
    def _():
        build_moved(pair[...], d_ref)
        res[...] = jnp.dot(w[...], d_ref[...], preferred_element_type=F32)

    @pl.when(prm[0] == 1)
    def _():
        for k in range(2):
            res[k * PAIR : (k + 1) * PAIR, :] = convolve(
                w[k * PAIR : (k + 1) * PAIR, :], pair[...]
            )

    keep[...] = res[rows(prm[2]), :]
    for d, ref in enumerate((s1, s2, s3), 1):
        ref[...] = res[rows((prm[2] + d) % 4), :].astype(BF16)


def last_kernel(prm, x, q, keep, r1, r2, r3, *refs):
    outs, scratch = refs[:4], refs[4]
    mask = live(prm)
    count = count_of(prm)
    total = keep[...] + r1[...].astype(F32) + r2[...].astype(F32) + r3[...].astype(F32)
    carried = q[...].astype(F32)

    @pl.when(prm[0] == 0)
    def _():
        xhat, scale = normed_of(x[...].astype(F32) * mask, mask, count)
        e = mask * total * silu_slope(xhat, jax.nn.sigmoid(xhat))
        slope = input_slope(e, xhat, scale, mask, count)
        scratch[...] = (mask * (carried + slope)).astype(BF16)

    @pl.when(prm[0] == 1)
    def _():
        scratch[...] = (carried + mask * total).astype(BF16)

    u = 2 * (prm[2] % 2) + prm[1]
    for v in range(4):
        t = (u - v + 4) % 4
        outs[v][...] = scratch[:, pl.ds(pl.multiple_of(t * 256, 256), 256)]


def call(kernel, outs, scratch, prm, *args, grant=8):
    vmem = pl.BlockSpec(memory_space=pltpu.VMEM)
    return pl.pallas_call(
        kernel,
        out_shape=[jax.ShapeDtypeStruct(s, d) for s, d in outs],
        in_specs=[pl.BlockSpec(memory_space=pltpu.SMEM)] + [vmem] * len(args),
        out_specs=[vmem] * len(outs),
        scratch_shapes=[pltpu.VMEM(s, d) for s, d in scratch],
        compiler_params=pltpu.CompilerParams(vmem_limit_bytes=grant << 20),
    )(prm, *args)


def step(signals, conv_weight, buckets):
    xh, core, z, _, y = (lax.axis_index(a) for a in AX)
    micro = z // 4
    own_bucket = jnp.where(micro == 0, buckets[0], buckets[1])
    size = 16 + 2 * own_bucket
    piece = (y + 1) % 4
    prm = jnp.stack([xh, core, y, size[0], size[1], piece]).astype(jnp.int32)
    own = ((OWN, PIX), BF16)
    own32 = ((OWN, PIX), F32)

    cut = conv_weight.reshape(12, TAPS, 4, OWN)
    low = jnp.where(xh == 0, cut[:, :, 0:2], cut[:, :, 0::2]).reshape(12, LANES)
    high = jnp.where(xh == 0, cut[:, :, 2:4], cut[:, :, 1::2]).reshape(12, LANES)
    odd = y % 2 == 1
    got = [
        lax.ppermute(jnp.where(odd, high, low), AX, weight_pairs(0)),
        lax.ppermute(jnp.where(odd, low, high), AX, weight_pairs(1)),
    ]
    flip = jnp.where(xh == 0, y % 2, core) == 1
    part = jnp.concatenate([jnp.where(flip, got[1], got[0]), jnp.where(flip, got[0], got[1])], 0)
    copies = jnp.broadcast_to(part, (16, 24, LANES))
    w = lax.all_to_all(copies, WEIGHT_GROUP, 0, 0, tiled=True).reshape(QUAD, LANES)

    blocks = call(
        split_kernel, [((OWN, 256), BF16)] * 4, [((QUAD, 256), BF16)], prm, signals
    )
    blocks = [lax.ppermute(b, AX, pixel_pairs(v)) for v, b in enumerate(blocks)]
    x, a = call(start_kernel, [own, own], [], prm, *blocks)
    others = [turn_y(a, d) for d in (1, 2, 3)]
    g = swap(x, "xh")

    full, keep, send = call(
        first_kernel,
        [((QUAD, PIX), BF16), own32, own32],
        [((LANES, PIX), BF16), ((PAIR, PIX), F32)],
        prm,
        w,
        g,
        a,
        *others,
        grant=24,
    )
    (mine,) = call(middle_kernel, [own], [], prm, x, keep, swap(send, "core"))
    theirs = swap(mine, "xh")
    b, q = call(turn_kernel, [own, own], [], prm, mine, theirs, g)
    b_other = swap(b, "core")
    (dw,) = call(
        weight_slope_kernel,
        [((QUAD, LANES), BF16)],
        [((PAIR, PIX), BF16), ((LANES, PIX), BF16)],
        prm,
        full,
        b,
        b_other,
        grant=24,
    )
    keep, *sends = call(
        second_kernel,
        [own32, own, own, own],
        [((PAIR, PIX), BF16), ((LANES, PIX), BF16), ((QUAD, PIX), F32)],
        prm,
        w,
        b,
        b_other,
        grant=24,
    )
    got = [turn_y(s, d) for d, s in enumerate(sends, 1)]
    blocks = call(last_kernel, [((OWN, 256), BF16)] * 4, [own], prm, x, q, keep, *got)
    blocks = [lax.ppermute(b, AX, back(pixel_pairs(v))) for v, b in enumerate(blocks)]
    (results,) = call(
        join_kernel, [((256, QUAD), BF16)], [((QUAD, 256), BF16)], prm, *blocks
    )

    shares = lax.all_to_all(dw.reshape(16, 24, LANES), WEIGHT_GROUP, 0, 0, tiled=True)
    total = jnp.sum(shares.astype(F32), axis=0)
    first, second = total[:12], total[12:]
    low_high = [
        lax.ppermute(jnp.where(flip, second, first), AX, back(weight_pairs(0))),
        lax.ppermute(jnp.where(flip, first, second), AX, back(weight_pairs(1))),
    ]
    low = jnp.where(odd, low_high[1], low_high[0]).reshape(12, TAPS, 2, OWN)
    high = jnp.where(odd, low_high[0], low_high[1]).reshape(12, TAPS, 2, OWN)
    apart = jnp.concatenate([low, high], axis=2)
    woven = jnp.stack([low, high], axis=3).reshape(12, TAPS, 4, OWN)
    grad_weight = jnp.where(xh == 0, apart, woven).reshape(12, TAPS, QUAD)
    return results, grad_weight


def solution(mesh):
    finer = Mesh(mesh.devices.reshape(SIZES), AX)
    section, fsdp = ("xh", "core"), ("z", "xl", "y")
    placed = (P(fsdp, section), P(fsdp, None, section), P())
    return jax.shard_map(
        step,
        mesh=finer,
        in_specs=placed,
        out_specs=(P(fsdp, section), P(fsdp, None, section)),
        check_vma=False,
    )
```

profile of v0, /device:TPU:94, one launch (start us, length us, event | category | flops | bytes accessed | tf_op | source)
XLA Modules:
  0.0 168.8 jit_solution(10252044968738428224)
XLA Ops:
  0.6 1.0 reshape.37
  2.7 0.9 collective-permute-start.4
  3.7 7.2 %collective-permute-start.5 = (bf16[12,1728]{1,0:T(8,128)(2,1)S(1)}, bf16[12,1728]{1,0:T(8,128)(2,1)S(1)}, u32[]{:S(2)}, u32[]{:S(2)}) collective-permute-start(bf16[12,1728]{1,0:T(8,128)(2,1)S(1)} %select_n.112), channel_id=1, source_target_pairs={{0,0},{1,1},{2,4},{3,5},{4,8},{5,9},{6,12},{7,13},{8,64},{9,65},{1... | collective-permute-start | bytes 124424 | tf_op jit(solution)/shard_map/ppermute | solution.py:334
  10.9 1.0 collective-permute-done.4
  11.9 2.9 %collective-permute-done.5 = bf16[12,1728]{1,0:T(8,128)(2,1)S(1)} collective-permute-done((bf16[12,1728]{1,0:T(8,128)(2,1)S(1)}, bf16[12,1728]{1,0:T(8,128)(2,1)S(1)}, u32[]{:S(2)}, u32[]{:S(2)}) %collective-permute-start.5) | collective-permute-done | bytes 41504 | tf_op jit(solution)/shard_map/ppermute | solution.py:334
  14.8 1.2 broadcast_in_dim.3
  16.0 9.1 %all-to-all-start = ((bf16[16,24,1728]{2,1,0:T(8,128)(2,1)}), bf16[16,24,1728]{2,1,0:T(8,128)(2,1)S(1)}, u32[]{:S(2)}, u32[]{:S(2)}) async-start(bf16[16,24,1728]{2,1,0:T(8,128)(2,1)} %broadcast_in_dim.3), calls=%async_computation | async-start | bytes 2752512 | tf_op jit(solution)/shard_map/all_to_all | solution.py:340
  25.2 0.7 shard_map.50
  25.9 5.5 %collective-permute-start = (bf16[96,256]{1,0:T(8,128)(2,1)S(1)}, bf16[96,256]{1,0:T(8,128)(2,1)S(1)}, u32[]{:S(2)}, u32[]{:S(2)}) collective-permute-start(bf16[96,256]{1,0:T(8,128)(2,1)S(1)} %get-tuple-element.21), channel_id=1, source_target_pairs={{0,64},{1,1},{2,65},{3,4},{4,68},{5,5},{6,69},{7,8},{8,72},{9,9},{... | collective-permute-start | bytes 147464 | tf_op jit(solution)/shard_map/ppermute | solution.py:345
  31.6 2.8 %collective-permute-start.2 = (bf16[96,256]{1,0:T(8,128)(2,1)S(1)}, bf16[96,256]{1,0:T(8,128)(2,1)S(1)}, u32[]{:S(2)}, u32[]{:S(2)}) collective-permute-start(bf16[96,256]{1,0:T(8,128)(2,1)S(1)} %get-tuple-element.23), channel_id=1, source_target_pairs={{0,65},{1,0},{2,64},{3,5},{4,69},{5,4},{6,68},{7,9},{8,73},{9,8},{... | collective-permute-start | bytes 147464 | tf_op jit(solution)/shard_map/ppermute | solution.py:345
  34.3 4.1 %collective-permute-start.3 = (bf16[96,256]{1,0:T(8,128)(2,1)S(1)}, bf16[96,256]{1,0:T(8,128)(2,1)S(1)}, u32[]{:S(2)}, u32[]{:S(2)}) collective-permute-start(bf16[96,256]{1,0:T(8,128)(2,1)S(1)} %get-tuple-element.24), channel_id=1, source_target_pairs={{0,0},{1,64},{2,1},{3,69},{4,4},{5,68},{6,5},{7,73},{8,8},{9,72},{... | collective-permute-start | bytes 147464 | tf_op jit(solution)/shard_map/ppermute | solution.py:345
  38.4 17.3 %collective-permute-done.refs_0_ = bf16[96,256]{1,0:T(8,128)(2,1)S(1)} collective-permute-done((bf16[96,256]{1,0:T(8,128)(2,1)S(1)}, bf16[96,256]{1,0:T(8,128)(2,1)S(1)}, u32[]{:S(2)}, u32[]{:S(2)}) %collective-permute-start) | collective-permute-done | bytes 49184 | tf_op jit(solution)/shard_map/ppermute | solution.py:345
  55.8 1.2 collective-permute-done.1.refs_1_
  56.9 1.9 %collective-permute-done.2.refs_2_ = bf16[96,256]{1,0:T(8,128)(2,1)S(1)} collective-permute-done((bf16[96,256]{1,0:T(8,128)(2,1)S(1)}, bf16[96,256]{1,0:T(8,128)(2,1)S(1)}, u32[]{:S(2)}, u32[]{:S(2)}) %collective-permute-start.2) | collective-permute-done | bytes 49184 | tf_op jit(solution)/shard_map/ppermute | solution.py:345
  58.8 2.0 %collective-permute-done.3.refs_3_ = bf16[96,256]{1,0:T(8,128)(2,1)S(1)} collective-permute-done((bf16[96,256]{1,0:T(8,128)(2,1)S(1)}, bf16[96,256]{1,0:T(8,128)(2,1)S(1)}, u32[]{:S(2)}, u32[]{:S(2)}) %collective-permute-start.3) | collective-permute-done | bytes 49184 | tf_op jit(solution)/shard_map/ppermute | solution.py:345
  60.8 0.8 shard_map.51
  62.0 1.9 %collective-permute-start.9 = (bf16[96,1024]{1,0:T(8,128)(2,1)S(1)}, bf16[96,1024]{1,0:T(8,128)(2,1)S(1)}, u32[]{:S(2)}, u32[]{:S(2)}) collective-permute-start(bf16[96,1024]{1,0:T(8,128)(2,1)S(1)} %get-tuple-element.26.a0), channel_id=1, source_target_pairs={{0,3},{1,0},{2,1},{3,2},{4,7},{5,4},{6,5},{7,6},{8,11},{9,8},{10,9... | collective-permute-start | bytes 589832 | tf_op jit(solution)/shard_map/ppermute | solution.py:72
  63.9 7.0 %collective-permute-done.6.g = bf16[96,1024]{1,0:T(8,128)(2,1)S(1)} collective-permute-done((bf16[96,1024]{1,0:T(8,128)(2,1)S(1)}, bf16[96,1024]{1,0:T(8,128)(2,1)S(1)}, u32[]{:S(2)}, u32[]{:S(2)}) %collective-permute-start.6) | collective-permute-done | bytes 196640 | tf_op jit(solution)/shard_map/ppermute | solution.py:68
  71.1 4.3 %collective-permute-done.9.a3 = bf16[96,1024]{1,0:T(8,128)(2,1)S(1)} collective-permute-done((bf16[96,1024]{1,0:T(8,128)(2,1)S(1)}, bf16[96,1024]{1,0:T(8,128)(2,1)S(1)}, u32[]{:S(2)}, u32[]{:S(2)}) %collective-permute-start.9) | collective-permute-done | bytes 196640 | tf_op jit(solution)/shard_map/ppermute | solution.py:72
  75.4 3.3 %shard_map.52 = (bf16[384,1024]{1,0:T(8,128)(2,1)S(1)}, f32[96,1024]{1,0:T(8,128)S(1)}, f32[96,1024]{1,0:T(8,128)S(1)}) custom-call(s32[6]{0:T(128)S(1)} %stack.22.prm, bf16[384,1728]{1,0:T(8,128)(2,1)S(1)} %bitcast.14, bf16[96,1024]{1,0:T(8,128)(2,1)S(1)} %collective-permute-done.6.g, bf16[96,1024]{1,0:T(8,128)(2,1)S(1)} %get-tuple-element.26.a0, ...), custom_call_target="tpu_custom_call" | custom-call | tf_op jit(solution)/shard_map/pallas_call | solution.py:309
  78.7 0.4 collective-permute-start.10
  79.1 1.6 collective-permute-done.10.got
  80.7 0.6 shard_map.53.mine
  81.3 3.4 %collective-permute-start.11 = (bf16[96,1024]{1,0:T(8,128)(2,1)S(1)}, bf16[96,1024]{1,0:T(8,128)(2,1)S(1)}, u32[]{:S(2)}, u32[]{:S(2)}) collective-permute-start(bf16[96,1024]{1,0:T(8,128)(2,1)S(1)} %shard_map.53.mine), channel_id=1, source_target_pairs={{0,128},{128,0},{1,129},{129,1},{2,130},{130,2},{3,131},{131,3},{4... | collective-permute-start | bytes 589832 | tf_op jit(solution)/shard_map/ppermute | solution.py:68
  84.7 5.2 %collective-permute-done.11.theirs = bf16[96,1024]{1,0:T(8,128)(2,1)S(1)} collective-permute-done((bf16[96,1024]{1,0:T(8,128)(2,1)S(1)}, bf16[96,1024]{1,0:T(8,128)(2,1)S(1)}, u32[]{:S(2)}, u32[]{:S(2)}) %collective-permute-start.11) | collective-permute-done | bytes 196640 | tf_op jit(solution)/shard_map/ppermute | solution.py:68
  89.9 0.9 shard_map.54
  90.9 1.4 collective-permute-done.12.b_other
  92.3 4.7 %shard_map.58 = bf16[384,1728]{1,0:T(8,128)(2,1)} custom-call(s32[6]{0:T(128)S(1)} %stack.22.prm, bf16[384,1024]{1,0:T(8,128)(2,1)S(1)} %get-tuple-element.39.full, bf16[96,1024]{1,0:T(8,128)(2,1)S(1)} %get-tuple-element.30.b_own, bf16[96,1024]{1,0:T(8,128)(2,1)S(1)} %collective-permute-done.12.b_other), custom_call_target="tpu_custom_call" | custom-call | tf_op jit(solution)/shard_map/pallas_call | solution.py:309
  97.1 7.3 %all-to-all-start.1 = ((bf16[16,24,1728]{2,1,0:T(8,128)(2,1)}), bf16[16,24,1728]{2,1,0:T(8,128)(2,1)}, u32[]{:S(2)}, u32[]{:S(2)}) async-start(bf16[16,24,1728]{2,1,0:T(8,128)(2,1)} %bitcast.6), calls=%async_computation.1 | async-start | bytes 2752512 | tf_op jit(solution)/shard_map/all_to_all | solution.py:392
  104.3 5.0 %shard_map.55 = (f32[96,1024]{1,0:T(8,128)S(1)}, bf16[96,1024]{1,0:T(8,128)(2,1)S(1)}, bf16[96,1024]{1,0:T(8,128)(2,1)S(1)}, bf16[96,1024]{1,0:T(8,128)(2,1)S(1)}) custom-call(s32[6]{0:T(128)S(1)} %stack.22.prm, bf16[384,1728]{1,0:T(8,128)(2,1)S(1)} %bitcast.15, bf16[96,1024]{1,0:T(8,128)(2,1)S(1)} %get-tuple-element.30.b_own, ...), custom_call_target="tpu_custom_call" | custom-call | tf_op jit(solution)/shard_map/pallas_call | solution.py:309
  109.4 1.2 collective-permute-start.13
  110.5 1.7 collective-permute-start.14
  112.2 0.4 collective-permute-start.15
  112.6 4.6 %collective-permute-done.13.r1 = bf16[96,1024]{1,0:T(8,128)(2,1)S(1)} collective-permute-done((bf16[96,1024]{1,0:T(8,128)(2,1)S(1)}, bf16[96,1024]{1,0:T(8,128)(2,1)S(1)}, u32[]{:S(2)}, u32[]{:S(2)}) %collective-permute-start.13) | collective-permute-done | bytes 196640 | tf_op jit(solution)/shard_map/ppermute | solution.py:72
  117.2 2.6 %collective-permute-done.14.r2 = bf16[96,1024]{1,0:T(8,128)(2,1)S(1)} collective-permute-done((bf16[96,1024]{1,0:T(8,128)(2,1)S(1)}, bf16[96,1024]{1,0:T(8,128)(2,1)S(1)}, u32[]{:S(2)}, u32[]{:S(2)}) %collective-permute-start.14) | collective-permute-done | bytes 196640 | tf_op jit(solution)/shard_map/ppermute | solution.py:72
  119.8 2.5 %collective-permute-done.15.r3 = bf16[96,1024]{1,0:T(8,128)(2,1)S(1)} collective-permute-done((bf16[96,1024]{1,0:T(8,128)(2,1)S(1)}, bf16[96,1024]{1,0:T(8,128)(2,1)S(1)}, u32[]{:S(2)}, u32[]{:S(2)}) %collective-permute-start.15) | collective-permute-done | bytes 196640 | tf_op jit(solution)/shard_map/ppermute | solution.py:72
  122.4 0.8 shard_map.56
  123.1 3.3 %collective-permute-start.16 = (bf16[96,256]{1,0:T(8,128)(2,1)S(1)}, bf16[96,256]{1,0:T(8,128)(2,1)S(1)}, u32[]{:S(2)}, u32[]{:S(2)}) collective-permute-start(bf16[96,256]{1,0:T(8,128)(2,1)S(1)} %get-tuple-element.35), channel_id=1, source_target_pairs={{64,0},{1,1},{65,2},{4,3},{68,4},{5,5},{69,6},{8,7},{72,8},{9,9},{... | collective-permute-start | bytes 147464 | tf_op jit(solution)/shard_map/ppermute | solution.py:387
  126.5 10.6 %all-to-all-done.1 = bf16[16,24,1728]{2,1,0:T(8,128)(2,1)} async-done(((bf16[16,24,1728]{2,1,0:T(8,128)(2,1)}), bf16[16,24,1728]{2,1,0:T(8,128)(2,1)}, u32[]{:S(2)}, u32[]{:S(2)}) %all-to-all-start.1) | async-done | bytes 1327136 | tf_op jit(solution)/shard_map/all_to_all | solution.py:392
  137.1 1.5 convert_reduce_fusion
  138.7 1.7 collective-permute-start.20
  140.3 4.5 %collective-permute-start.21 = (f32[12,1728]{1,0:T(8,128)S(1)}, f32[12,1728]{1,0:T(8,128)S(1)}, u32[]{:S(2)}, u32[]{:S(2)}) collective-permute-start(f32[12,1728]{1,0:T(8,128)S(1)} %get-tuple-element.45), channel_id=1, source_target_pairs={{0,0},{1,1},{4,2},{5,3},{8,4},{9,5},{12,6},{13,7},{64,8},{65,9},{6... | collective-permute-start | bytes 248840 | tf_op jit(solution)/shard_map/ppermute | solution.py:396
  144.8 4.1 %collective-permute-start.17 = (bf16[96,256]{1,0:T(8,128)(2,1)S(1)}, bf16[96,256]{1,0:T(8,128)(2,1)S(1)}, u32[]{:S(2)}, u32[]{:S(2)}) collective-permute-start(bf16[96,256]{1,0:T(8,128)(2,1)S(1)} %get-tuple-element.36), channel_id=1, source_target_pairs={{1,0},{65,1},{0,2},{68,3},{5,4},{69,5},{4,6},{72,7},{9,8},{73,9},{... | collective-permute-start | bytes 147464 | tf_op jit(solution)/shard_map/ppermute | solution.py:387
  149.0 1.9 %collective-permute-start.18 = (bf16[96,256]{1,0:T(8,128)(2,1)S(1)}, bf16[96,256]{1,0:T(8,128)(2,1)S(1)}, u32[]{:S(2)}, u32[]{:S(2)}) collective-permute-start(bf16[96,256]{1,0:T(8,128)(2,1)S(1)} %get-tuple-element.37), channel_id=1, source_target_pairs={{65,0},{0,1},{64,2},{5,3},{69,4},{4,5},{68,6},{9,7},{73,8},{8,9},{... | collective-permute-start | bytes 147464 | tf_op jit(solution)/shard_map/ppermute | solution.py:387
  150.9 1.9 %collective-permute-start.19 = (bf16[96,256]{1,0:T(8,128)(2,1)S(1)}, bf16[96,256]{1,0:T(8,128)(2,1)S(1)}, u32[]{:S(2)}, u32[]{:S(2)}) collective-permute-start(bf16[96,256]{1,0:T(8,128)(2,1)S(1)} %get-tuple-element.38), channel_id=1, source_target_pairs={{0,0},{64,1},{1,2},{69,3},{4,4},{68,5},{5,6},{73,7},{8,8},{72,9},{... | collective-permute-start | bytes 147464 | tf_op jit(solution)/shard_map/ppermute | solution.py:387
  152.8 12.4 %collective-permute-done.18.refs_2_ = bf16[96,256]{1,0:T(8,128)(2,1)S(1)} collective-permute-done((bf16[96,256]{1,0:T(8,128)(2,1)S(1)}, bf16[96,256]{1,0:T(8,128)(2,1)S(1)}, u32[]{:S(2)}, u32[]{:S(2)}) %collective-permute-start.18) | collective-permute-done | bytes 49184 | tf_op jit(solution)/shard_map/ppermute | solution.py:387
  165.3 1.4 shard_map.57
  168.1 0.7 broadcast_select_fusion
  (39 shorter events, 3.5 us)
Async XLA Ops:
  2.7 9.2 %collective-permute-start.4 = (bf16[12,1728]{1,0:T(8,128)(2,1)S(1)}, bf16[12,1728]{1,0:T(8,128)(2,1)S(1)}, u32[]{:S(2)}, u32[]{:S(2)}) collective-permute-start(bf16[12,1728]{1,0:T(8,128)(2,1)S(1)} %select_n.110), channel_id=1, source_target_pairs={{0,1},{1,0},{2,5},{3,4},{4,9},{5,8},{6,13},{7,12},{8,65},{9,64},{1... | collective-permute-start | bytes 124424 | tf_op jit(solution)/shard_map/ppermute | solution.py:335
  3.7 11.1 %collective-permute-start.5 = (bf16[12,1728]{1,0:T(8,128)(2,1)S(1)}, bf16[12,1728]{1,0:T(8,128)(2,1)S(1)}, u32[]{:S(2)}, u32[]{:S(2)}) collective-permute-start(bf16[12,1728]{1,0:T(8,128)(2,1)S(1)} %select_n.112), channel_id=1, source_target_pairs={{0,0},{1,1},{2,4},{3,5},{4,8},{5,9},{6,12},{7,13},{8,64},{9,65},{1... | collective-permute-start | bytes 124424 | tf_op jit(solution)/shard_map/ppermute | solution.py:334
  16.0 9.1 %copy-start.1 = (s32[2,2]{1,0:T(2,128)S(1)}, s32[2,2]{1,0:T(2,128)}, u32[]{:S(2)}) copy-start(s32[2,2]{1,0:T(2,128)} %param.5) | copy-start | bytes 52
  16.0 9.2 %copy-start = (bf16[256,384]{1,0:T(8,128)(2,1)S(1)}, bf16[256,384]{1,0:T(8,128)(2,1)}, u32[]{:S(2)}) copy-start(bf16[256,384]{1,0:T(8,128)(2,1)} %x_ref.1) | copy-start | bytes 589828
  16.0 59.4 %all-to-all-start = ((bf16[16,24,1728]{2,1,0:T(8,128)(2,1)}), bf16[16,24,1728]{2,1,0:T(8,128)(2,1)S(1)}, u32[]{:S(2)}, u32[]{:S(2)}) async-start(bf16[16,24,1728]{2,1,0:T(8,128)(2,1)} %broadcast_in_dim.3), calls=%async_computation | async-start | bytes 2752512 | tf_op jit(solution)/shard_map/all_to_all | solution.py:340
  25.9 29.9 %collective-permute-start = (bf16[96,256]{1,0:T(8,128)(2,1)S(1)}, bf16[96,256]{1,0:T(8,128)(2,1)S(1)}, u32[]{:S(2)}, u32[]{:S(2)}) collective-permute-start(bf16[96,256]{1,0:T(8,128)(2,1)S(1)} %get-tuple-element.21), channel_id=1, source_target_pairs={{0,64},{1,1},{2,65},{3,4},{4,68},{5,5},{6,69},{7,8},{8,72},{9,9},{... | collective-permute-start | bytes 147464 | tf_op jit(solution)/shard_map/ppermute | solution.py:345
  31.4 25.6 %collective-permute-start.1 = (bf16[96,256]{1,0:T(8,128)(2,1)S(1)}, bf16[96,256]{1,0:T(8,128)(2,1)S(1)}, u32[]{:S(2)}, u32[]{:S(2)}) collective-permute-start(bf16[96,256]{1,0:T(8,128)(2,1)S(1)} %get-tuple-element.22), channel_id=1, source_target_pairs={{0,1},{1,65},{2,0},{3,68},{4,5},{5,69},{6,4},{7,72},{8,9},{9,73},{... | collective-permute-start | bytes 147464 | tf_op jit(solution)/shard_map/ppermute | solution.py:345
  31.6 27.3 %collective-permute-start.2 = (bf16[96,256]{1,0:T(8,128)(2,1)S(1)}, bf16[96,256]{1,0:T(8,128)(2,1)S(1)}, u32[]{:S(2)}, u32[]{:S(2)}) collective-permute-start(bf16[96,256]{1,0:T(8,128)(2,1)S(1)} %get-tuple-element.23), channel_id=1, source_target_pairs={{0,65},{1,0},{2,64},{3,5},{4,69},{5,4},{6,68},{7,9},{8,73},{9,8},{... | collective-permute-start | bytes 147464 | tf_op jit(solution)/shard_map/ppermute | solution.py:345
  34.3 26.5 %collective-permute-start.3 = (bf16[96,256]{1,0:T(8,128)(2,1)S(1)}, bf16[96,256]{1,0:T(8,128)(2,1)S(1)}, u32[]{:S(2)}, u32[]{:S(2)}) collective-permute-start(bf16[96,256]{1,0:T(8,128)(2,1)S(1)} %get-tuple-element.24), channel_id=1, source_target_pairs={{0,0},{1,64},{2,1},{3,69},{4,4},{5,68},{6,5},{7,73},{8,8},{9,72},{... | collective-permute-start | bytes 147464 | tf_op jit(solution)/shard_map/ppermute | solution.py:345
  61.7 9.2 %collective-permute-start.6 = (bf16[96,1024]{1,0:T(8,128)(2,1)S(1)}, bf16[96,1024]{1,0:T(8,128)(2,1)S(1)}, u32[]{:S(2)}, u32[]{:S(2)}) collective-permute-start(bf16[96,1024]{1,0:T(8,128)(2,1)S(1)} %get-tuple-element.25.x), channel_id=1, source_target_pairs={{0,128},{128,0},{1,129},{129,1},{2,130},{130,2},{3,131},{131,3},{4... | collective-permute-start | bytes 589832 | tf_op jit(solution)/shard_map/ppermute | solution.py:68
  61.8 9.1 %collective-permute-start.7 = (bf16[96,1024]{1,0:T(8,128)(2,1)S(1)}, bf16[96,1024]{1,0:T(8,128)(2,1)S(1)}, u32[]{:S(2)}, u32[]{:S(2)}) collective-permute-start(bf16[96,1024]{1,0:T(8,128)(2,1)S(1)} %get-tuple-element.26.a0), channel_id=1, source_target_pairs={{0,1},{1,2},{2,3},{3,0},{4,5},{5,6},{6,7},{7,4},{8,9},{9,10},{10,1... | collective-permute-start | bytes 589832 | tf_op jit(solution)/shard_map/ppermute | solution.py:72
  61.9 9.3 %collective-permute-start.8 = (bf16[96,1024]{1,0:T(8,128)(2,1)S(1)}, bf16[96,1024]{1,0:T(8,128)(2,1)S(1)}, u32[]{:S(2)}, u32[]{:S(2)}) collective-permute-start(bf16[96,1024]{1,0:T(8,128)(2,1)S(1)} %get-tuple-element.26.a0), channel_id=1, source_target_pairs={{0,2},{1,3},{2,0},{3,1},{4,6},{5,7},{6,4},{7,5},{8,10},{9,11},{10,... | collective-permute-start | bytes 589832 | tf_op jit(solution)/shard_map/ppermute | solution.py:72
  62.0 13.5 %collective-permute-start.9 = (bf16[96,1024]{1,0:T(8,128)(2,1)S(1)}, bf16[96,1024]{1,0:T(8,128)(2,1)S(1)}, u32[]{:S(2)}, u32[]{:S(2)}) collective-permute-start(bf16[96,1024]{1,0:T(8,128)(2,1)S(1)} %get-tuple-element.26.a0), channel_id=1, source_target_pairs={{0,3},{1,0},{2,1},{3,2},{4,7},{5,4},{6,5},{7,6},{8,11},{9,8},{10,9... | collective-permute-start | bytes 589832 | tf_op jit(solution)/shard_map/ppermute | solution.py:72
  78.7 2.0 %collective-permute-start.10 = (f32[96,1024]{1,0:T(8,128)S(1)}, f32[96,1024]{1,0:T(8,128)S(1)}, u32[]{:S(2)}, u32[]{:S(2)}) collective-permute-start(f32[96,1024]{1,0:T(8,128)S(1)} %get-tuple-element.28), channel_id=1, source_target_pairs={{0,64},{64,0},{1,65},{65,1},{2,66},{66,2},{3,67},{67,3},{4,68},{68... | collective-permute-start | bytes 1179656 | tf_op jit(solution)/shard_map/ppermute | solution.py:68
  81.3 8.6 %collective-permute-start.11 = (bf16[96,1024]{1,0:T(8,128)(2,1)S(1)}, bf16[96,1024]{1,0:T(8,128)(2,1)S(1)}, u32[]{:S(2)}, u32[]{:S(2)}) collective-permute-start(bf16[96,1024]{1,0:T(8,128)(2,1)S(1)} %shard_map.53.mine), channel_id=1, source_target_pairs={{0,128},{128,0},{1,129},{129,1},{2,130},{130,2},{3,131},{131,3},{4... | collective-permute-start | bytes 589832 | tf_op jit(solution)/shard_map/ppermute | solution.py:68
  90.8 1.5 collective-permute-start.12
  97.1 40.1 %all-to-all-start.1 = ((bf16[16,24,1728]{2,1,0:T(8,128)(2,1)}), bf16[16,24,1728]{2,1,0:T(8,128)(2,1)}, u32[]{:S(2)}, u32[]{:S(2)}) async-start(bf16[16,24,1728]{2,1,0:T(8,128)(2,1)} %bitcast.6), calls=%async_computation.1 | async-start | bytes 2752512 | tf_op jit(solution)/shard_map/all_to_all | solution.py:392
  109.4 7.9 %collective-permute-start.13 = (bf16[96,1024]{1,0:T(8,128)(2,1)S(1)}, bf16[96,1024]{1,0:T(8,128)(2,1)S(1)}, u32[]{:S(2)}, u32[]{:S(2)}) collective-permute-start(bf16[96,1024]{1,0:T(8,128)(2,1)S(1)} %get-tuple-element.32), channel_id=1, source_target_pairs={{0,1},{1,2},{2,3},{3,0},{4,5},{5,6},{6,7},{7,4},{8,9},{9,10},{10,1... | collective-permute-start | bytes 589832 | tf_op jit(solution)/shard_map/ppermute | solution.py:72
  110.5 9.3 %collective-permute-start.14 = (bf16[96,1024]{1,0:T(8,128)(2,1)S(1)}, bf16[96,1024]{1,0:T(8,128)(2,1)S(1)}, u32[]{:S(2)}, u32[]{:S(2)}) collective-permute-start(bf16[96,1024]{1,0:T(8,128)(2,1)S(1)} %get-tuple-element.33), channel_id=1, source_target_pairs={{0,2},{1,3},{2,0},{3,1},{4,6},{5,7},{6,4},{7,5},{8,10},{9,11},{10,... | collective-permute-start | bytes 589832 | tf_op jit(solution)/shard_map/ppermute | solution.py:72
  112.2 10.1 %collective-permute-start.15 = (bf16[96,1024]{1,0:T(8,128)(2,1)S(1)}, bf16[96,1024]{1,0:T(8,128)(2,1)S(1)}, u32[]{:S(2)}, u32[]{:S(2)}) collective-permute-start(bf16[96,1024]{1,0:T(8,128)(2,1)S(1)} %get-tuple-element.34), channel_id=1, source_target_pairs={{0,3},{1,0},{2,1},{3,2},{4,7},{5,4},{6,5},{7,6},{8,11},{9,8},{10,9... | collective-permute-start | bytes 589832 | tf_op jit(solution)/shard_map/ppermute | solution.py:72
  123.1 27.8 %collective-permute-start.16 = (bf16[96,256]{1,0:T(8,128)(2,1)S(1)}, bf16[96,256]{1,0:T(8,128)(2,1)S(1)}, u32[]{:S(2)}, u32[]{:S(2)}) collective-permute-start(bf16[96,256]{1,0:T(8,128)(2,1)S(1)} %get-tuple-element.35), channel_id=1, source_target_pairs={{64,0},{1,1},{65,2},{4,3},{68,4},{5,5},{69,6},{8,7},{72,8},{9,9},{... | collective-permute-start | bytes 147464 | tf_op jit(solution)/shard_map/ppermute | solution.py:387
  138.7 28.0 %collective-permute-start.20 = (f32[12,1728]{1,0:T(8,128)S(1)}, f32[12,1728]{1,0:T(8,128)S(1)}, u32[]{:S(2)}, u32[]{:S(2)}) collective-permute-start(f32[12,1728]{1,0:T(8,128)S(1)} %get-tuple-element.44), channel_id=1, source_target_pairs={{1,0},{0,1},{5,2},{4,3},{9,4},{8,5},{13,6},{12,7},{65,8},{64,9},{6... | collective-permute-start | bytes 248840 | tf_op jit(solution)/shard_map/ppermute | solution.py:397
  140.3 26.3 %collective-permute-start.21 = (f32[12,1728]{1,0:T(8,128)S(1)}, f32[12,1728]{1,0:T(8,128)S(1)}, u32[]{:S(2)}, u32[]{:S(2)}) collective-permute-start(f32[12,1728]{1,0:T(8,128)S(1)} %get-tuple-element.45), channel_id=1, source_target_pairs={{0,0},{1,1},{4,2},{5,3},{8,4},{9,5},{12,6},{13,7},{64,8},{65,9},{6... | collective-permute-start | bytes 248840 | tf_op jit(solution)/shard_map/ppermute | solution.py:396
  144.8 8.0 %collective-permute-start.17 = (bf16[96,256]{1,0:T(8,128)(2,1)S(1)}, bf16[96,256]{1,0:T(8,128)(2,1)S(1)}, u32[]{:S(2)}, u32[]{:S(2)}) collective-permute-start(bf16[96,256]{1,0:T(8,128)(2,1)S(1)} %get-tuple-element.36), channel_id=1, source_target_pairs={{1,0},{65,1},{0,2},{68,3},{5,4},{69,5},{4,6},{72,7},{9,8},{73,9},{... | collective-permute-start | bytes 147464 | tf_op jit(solution)/shard_map/ppermute | solution.py:387
  149.0 16.2 %collective-permute-start.18 = (bf16[96,256]{1,0:T(8,128)(2,1)S(1)}, bf16[96,256]{1,0:T(8,128)(2,1)S(1)}, u32[]{:S(2)}, u32[]{:S(2)}) collective-permute-start(bf16[96,256]{1,0:T(8,128)(2,1)S(1)} %get-tuple-element.37), channel_id=1, source_target_pairs={{65,0},{0,1},{64,2},{5,3},{69,4},{4,5},{68,6},{9,7},{73,8},{8,9},{... | collective-permute-start | bytes 147464 | tf_op jit(solution)/shard_map/ppermute | solution.py:387
  150.9 14.4 %collective-permute-start.19 = (bf16[96,256]{1,0:T(8,128)(2,1)S(1)}, bf16[96,256]{1,0:T(8,128)(2,1)S(1)}, u32[]{:S(2)}, u32[]{:S(2)}) collective-permute-start(bf16[96,256]{1,0:T(8,128)(2,1)S(1)} %get-tuple-element.38), channel_id=1, source_target_pairs={{0,0},{64,1},{1,2},{69,3},{4,4},{68,5},{5,6},{73,7},{8,8},{72,9},{... | collective-permute-start | bytes 147464 | tf_op jit(solution)/shard_map/ppermute | solution.py:387
where the time goes:
time: 169 us
  waiting for transfers between devices  79 us (47%)
  starting transfers between devices  63.6 us (38%)
  Pallas kernels  18.2 us (11%)
  local copies, waits for them, and re-layouts  4.33 us (3%)
  other arithmetic  2.71 us (2%)
    ppermute x4, waiting for transfers between devices, step(): blocks = [lax.ppermute(b, AX, pixel_pairs(v)) for v, b in enumerate(blocks)]  22.4 us
    pallas_call x9, Pallas kernels, call(): pl.pallas_call(kernel, out_shape=[jax.ShapeDtypeStruct(s, d) for s, d in...  18.2 us
    ppermute x4, waiting for transfers between devices, swap(): return lax.ppermute(value, axis, [(0, 1), (1, 0)])  15.2 us
    ppermute x6, waiting for transfers between devices, turn_y(): return lax.ppermute(value, 'y', [(i, (i + d) % 4) for i in range(4)])  14.3 us
    ppermute x4, starting transfers between devices, step(): blocks = [lax.ppermute(b, AX, pixel_pairs(v)) for v, b in enumerate(blocks)]  12.5 us
    ppermute x4, waiting for transfers between devices, step(): lax.ppermute(b, AX, back(pixel_pairs(v)))  12.5 us
    ppermute x4, starting transfers between devices, step(): lax.ppermute(b, AX, back(pixel_pairs(v)))  11.3 us
    all_to_all x1, waiting for transfers between devices, step(): lax.all_to_all(dw.reshape(16, 24, LANES), WEIGHT_GROUP, 0, 0, tiled=True)  10.6 us
  transfers between devices with their start and end apart: 24, of which 18 were waited for; matrix products, arithmetic and copies ran while one was open for 1% of the time, Pallas kernels for 5%

commit v1 on v0

--- a/solution.py
+++ b/solution.py
@@ -10,6 +10,7 @@
 AX = ("xh", "core", "z", "xl", "y")
 SIZES = (2, 2, 8, 2, 4)
 WEIGHT_GROUP = ("z", "xl")
+FSDP = ("z", "xl", "y")
 GROUP_WIDTH = 24
 OWN = 96
 PIX = 1024
@@ -36,10 +37,10 @@
                         yield xh, core, z, xl, y
 
 
-def pixel_pairs(turn):
+def pixel_pairs(turn, ahead):
     pairs = []
     for xh, core, z, xl, y in every():
-        slot = ((z * 2 + xl) * 4 + y + 1) % 64
+        slot = ((z * 2 + xl) * 4 + y + ahead) % 64
         sample, piece = slot // 4, slot % 4
         u = (piece + turn) % 4
         pairs.append(
@@ -92,7 +93,7 @@
         return field
     row, col = pixels()
     ok = (row + dr >= 0) & (row + dr < SIDE) & (col + dc >= 0) & (col + dc < SIDE)
-    return jnp.where(ok, pltpu.roll(field, (-off) % PIX, 1), 0.0)
+    return pltpu.roll(field, (-off) % PIX, 1) * ok.astype(F32).astype(field.dtype)
 
 
 def group_sum(field):
@@ -133,7 +134,7 @@
     outs, scratch = refs[:4], refs[4]
     scratch[...] = x_ref[...].astype(F32).T.astype(BF16)
     for v in range(4):
-        outs[v][...] = scratch[rows((prm[5] + v) % 4), :]
+        outs[v][...] = scratch[rows((prm[2] + v) % 4), :]
 
 
 def join_kernel(prm, *refs):
@@ -172,10 +173,9 @@
 
 
 def build_moved(act, d_ref):
-    act = act.astype(F32)
     for tap in range(TAPS):
         dr, dc = offsets(tap)
-        d_ref[tap * PAIR : (tap + 1) * PAIR, :] = moved(act, -dr, -dc).astype(BF16)
+        d_ref[tap * PAIR : (tap + 1) * PAIR, :] = moved(act, -dr, -dc)
 
 
 def gather_chunks(prm, own, others, full):
@@ -339,10 +339,11 @@
     copies = jnp.broadcast_to(part, (16, 24, LANES))
     w = lax.all_to_all(copies, WEIGHT_GROUP, 0, 0, tiled=True).reshape(QUAD, LANES)
 
+    shifted = lax.ppermute(signals, FSDP, [(i, (i + 1) % 64) for i in range(64)])
     blocks = call(
-        split_kernel, [((OWN, 256), BF16)] * 4, [((QUAD, 256), BF16)], prm, signals
-    )
-    blocks = [lax.ppermute(b, AX, pixel_pairs(v)) for v, b in enumerate(blocks)]
+        split_kernel, [((OWN, 256), BF16)] * 4, [((QUAD, 256), BF16)], prm, shifted
+    )
+    blocks = [lax.ppermute(b, AX, pixel_pairs(v, 0)) for v, b in enumerate(blocks)]
     x, a = call(start_kernel, [own, own], [], prm, *blocks)
     others = [turn_y(a, d) for d in (1, 2, 3)]
     g = swap(x, "xh")
@@ -384,13 +385,13 @@
     )
     got = [turn_y(s, d) for d, s in enumerate(sends, 1)]
     blocks = call(last_kernel, [((OWN, 256), BF16)] * 4, [own], prm, x, q, keep, *got)
-    blocks = [lax.ppermute(b, AX, back(pixel_pairs(v))) for v, b in enumerate(blocks)]
+    blocks = [lax.ppermute(b, AX, back(pixel_pairs(v, 1))) for v, b in enumerate(blocks)]
     (results,) = call(
         join_kernel, [((256, QUAD), BF16)], [((QUAD, 256), BF16)], prm, *blocks
     )
 
     shares = lax.all_to_all(dw.reshape(16, 24, LANES), WEIGHT_GROUP, 0, 0, tiled=True)
-    total = jnp.sum(shares.astype(F32), axis=0)
+    total = jnp.sum(shares.astype(F32), axis=0).astype(BF16)
     first, second = total[:12], total[12:]
     low_high = [
         lax.ppermute(jnp.where(flip, second, first), AX, back(weight_pairs(0))),
@@ -400,7 +401,7 @@
     high = jnp.where(odd, low_high[0], low_high[1]).reshape(12, TAPS, 2, OWN)
     apart = jnp.concatenate([low, high], axis=2)
     woven = jnp.stack([low, high], axis=3).reshape(12, TAPS, 4, OWN)
-    grad_weight = jnp.where(xh == 0, apart, woven).reshape(12, TAPS, QUAD)
+    grad_weight = jnp.where(xh == 0, apart, woven).reshape(12, TAPS, QUAD).astype(F32)
     return results, grad_weight
 
 

time: 169 us -> 173 us (1.024)
  the two profiles are of different devices: /device:TPU:94 before, /device:TPU:21 now
where the time goes in v1:
time: 173 us
  starting transfers between devices  74.5 us (43%)
  waiting for transfers between devices  73.4 us (42%)
  Pallas kernels  16.9 us (10%)
  local copies, waits for them, and re-layouts  4.21 us (2%)
  other arithmetic  2.78 us (2%)
    ppermute x4, waiting for transfers between devices, step(): lax.ppermute(b, AX, pixel_pairs(v, 0))  32.2 us
    pallas_call x9, Pallas kernels, call(): pl.pallas_call(kernel, out_shape=[jax.ShapeDtypeStruct(s, d) for s, d in...  16.9 us
    ppermute x4, starting transfers between devices, step(): lax.ppermute(b, AX, back(pixel_pairs(v, 1)))  16.3 us
    ppermute x6, waiting for transfers between devices, turn_y(): return lax.ppermute(value, 'y', [(i, (i + d) % 4) for i in range(4)])  15.3 us
    ppermute x6, starting transfers between devices, turn_y(): return lax.ppermute(value, 'y', [(i, (i + d) % 4) for i in range(4)])  13 us
    ppermute x4, starting transfers between devices, step(): lax.ppermute(b, AX, pixel_pairs(v, 0))  7.68 us
    ppermute x1, waiting for transfers between devices, step(): lax.ppermute(jnp.where(flip, second, first), AX, back(weight_pairs(0)))  7.42 us
    ppermute x1, starting transfers between devices, step(): lax.ppermute(jnp.where(odd, low, high), AX, weight_pairs(1))  7.4 us
  transfers between devices with their start and end apart: 25, of which 13 were waited for; matrix products, arithmetic and copies ran while one was open for 1% of the time, Pallas kernels for 5%

profile of v1, /device:TPU:21, one launch (start us, length us, event | category | flops | bytes accessed | tf_op | source)
XLA Modules:
  0.0 172.8 jit_solution(1029107042606887654)
XLA Ops:
  0.6 1.0 reshape.37
  2.1 0.3 slice.32
  2.7 7.4 %collective-permute-start.5 = (bf16[12,1728]{1,0:T(8,128)(2,1)S(1)}, bf16[12,1728]{1,0:T(8,128)(2,1)S(1)}, u32[]{:S(2)}, u32[]{:S(2)}) collective-permute-start(bf16[12,1728]{1,0:T(8,128)(2,1)S(1)} %select_n.108), channel_id=1, source_target_pairs={{0,1},{1,0},{2,5},{3,4},{4,9},{5,8},{6,13},{7,12},{8,65},{9,64},{1... | collective-permute-start | bytes 124424 | tf_op jit(solution)/shard_map/ppermute | solution.py:335
  10.2 4.0 %collective-permute-start.6 = (bf16[12,1728]{1,0:T(8,128)(2,1)S(1)}, bf16[12,1728]{1,0:T(8,128)(2,1)S(1)}, u32[]{:S(2)}, u32[]{:S(2)}) collective-permute-start(bf16[12,1728]{1,0:T(8,128)(2,1)S(1)} %select_n.110), channel_id=1, source_target_pairs={{0,0},{1,1},{2,4},{3,5},{4,8},{5,9},{6,12},{7,13},{8,64},{9,65},{1... | collective-permute-start | bytes 124424 | tf_op jit(solution)/shard_map/ppermute | solution.py:334
  14.2 6.4 %collective-permute-done.6 = bf16[12,1728]{1,0:T(8,128)(2,1)S(1)} collective-permute-done((bf16[12,1728]{1,0:T(8,128)(2,1)S(1)}, bf16[12,1728]{1,0:T(8,128)(2,1)S(1)}, u32[]{:S(2)}, u32[]{:S(2)}) %collective-permute-start.6) | collective-permute-done | bytes 41504 | tf_op jit(solution)/shard_map/ppermute | solution.py:334
  20.6 1.2 broadcast_in_dim.3
  21.8 3.8 %all-to-all-start = ((bf16[16,24,1728]{2,1,0:T(8,128)(2,1)}), bf16[16,24,1728]{2,1,0:T(8,128)(2,1)S(1)}, u32[]{:S(2)}, u32[]{:S(2)}) async-start(bf16[16,24,1728]{2,1,0:T(8,128)(2,1)} %broadcast_in_dim.3), calls=%async_computation | async-start | bytes 2752512 | tf_op jit(solution)/shard_map/all_to_all | solution.py:340
  25.7 3.7 %collective-permute-start = (bf16[256,384]{1,0:T(8,128)(2,1)S(1)}, bf16[256,384]{1,0:T(8,128)(2,1)S(1)}, u32[]{:S(2)}, u32[]{:S(2)}) collective-permute-start(bf16[256,384]{1,0:T(8,128)(2,1)S(1)} %copy-done.1), channel_id=1, source_target_pairs={{0,1},{1,2},{2,3},{3,4},{4,5},{5,6},{6,7},{7,8},{8,9},{9,10},{10,1... | collective-permute-start | bytes 589832 | tf_op jit(solution)/shard_map/ppermute | solution.py:342
  29.5 3.2 %collective-permute-done.x_ref = bf16[256,384]{1,0:T(8,128)(2,1)S(1)} collective-permute-done((bf16[256,384]{1,0:T(8,128)(2,1)S(1)}, bf16[256,384]{1,0:T(8,128)(2,1)S(1)}, u32[]{:S(2)}, u32[]{:S(2)}) %collective-permute-start) | collective-permute-done | bytes 196640 | tf_op jit(solution)/shard_map/ppermute | solution.py:342
  32.7 0.7 shard_map.50
  33.4 5.0 %collective-permute-start.1 = (bf16[96,256]{1,0:T(8,128)(2,1)S(1)}, bf16[96,256]{1,0:T(8,128)(2,1)S(1)}, u32[]{:S(2)}, u32[]{:S(2)}) collective-permute-start(bf16[96,256]{1,0:T(8,128)(2,1)S(1)} %get-tuple-element.21), channel_id=1, source_target_pairs={{0,0},{1,64},{2,1},{3,65},{4,4},{5,68},{6,5},{7,69},{8,8},{9,72},{... | collective-permute-start | bytes 147464 | tf_op jit(solution)/shard_map/ppermute | solution.py:346
  38.4 1.9 %collective-permute-start.2 = (bf16[96,256]{1,0:T(8,128)(2,1)S(1)}, bf16[96,256]{1,0:T(8,128)(2,1)S(1)}, u32[]{:S(2)}, u32[]{:S(2)}) collective-permute-start(bf16[96,256]{1,0:T(8,128)(2,1)S(1)} %get-tuple-element.22), channel_id=1, source_target_pairs={{0,64},{1,1},{2,65},{3,0},{4,68},{5,5},{6,69},{7,4},{8,72},{9,9},{... | collective-permute-start | bytes 147464 | tf_op jit(solution)/shard_map/ppermute | solution.py:346
  40.4 0.7 collective-permute-start.4
  41.1 32.2 %collective-permute-done.2.refs_1_ = bf16[96,256]{1,0:T(8,128)(2,1)S(1)} collective-permute-done((bf16[96,256]{1,0:T(8,128)(2,1)S(1)}, bf16[96,256]{1,0:T(8,128)(2,1)S(1)}, u32[]{:S(2)}, u32[]{:S(2)}) %collective-permute-start.2) | collective-permute-done | bytes 49184 | tf_op jit(solution)/shard_map/ppermute | solution.py:346
  73.3 0.8 shard_map.51
  74.3 4.2 %collective-permute-start.8 = (bf16[96,1024]{1,0:T(8,128)(2,1)S(1)}, bf16[96,1024]{1,0:T(8,128)(2,1)S(1)}, u32[]{:S(2)}, u32[]{:S(2)}) collective-permute-start(bf16[96,1024]{1,0:T(8,128)(2,1)S(1)} %get-tuple-element.26.a0), channel_id=1, source_target_pairs={{0,1},{1,2},{2,3},{3,0},{4,5},{5,6},{6,7},{7,4},{8,9},{9,10},{10,1... | collective-permute-start | bytes 589832 | tf_op jit(solution)/shard_map/ppermute | solution.py:73
  78.5 2.7 %collective-permute-start.9 = (bf16[96,1024]{1,0:T(8,128)(2,1)S(1)}, bf16[96,1024]{1,0:T(8,128)(2,1)S(1)}, u32[]{:S(2)}, u32[]{:S(2)}) collective-permute-start(bf16[96,1024]{1,0:T(8,128)(2,1)S(1)} %get-tuple-element.26.a0), channel_id=1, source_target_pairs={{0,2},{1,3},{2,0},{3,1},{4,6},{5,7},{6,4},{7,5},{8,10},{9,11},{10,... | collective-permute-start | bytes 589832 | tf_op jit(solution)/shard_map/ppermute | solution.py:73
  81.3 2.0 %collective-permute-start.10 = (bf16[96,1024]{1,0:T(8,128)(2,1)S(1)}, bf16[96,1024]{1,0:T(8,128)(2,1)S(1)}, u32[]{:S(2)}, u32[]{:S(2)}) collective-permute-start(bf16[96,1024]{1,0:T(8,128)(2,1)S(1)} %get-tuple-element.26.a0), channel_id=1, source_target_pairs={{0,3},{1,0},{2,1},{3,2},{4,7},{5,4},{6,5},{7,6},{8,11},{9,8},{10,9... | collective-permute-start | bytes 589832 | tf_op jit(solution)/shard_map/ppermute | solution.py:73
  83.2 7.2 %collective-permute-done.9.a2 = bf16[96,1024]{1,0:T(8,128)(2,1)S(1)} collective-permute-done((bf16[96,1024]{1,0:T(8,128)(2,1)S(1)}, bf16[96,1024]{1,0:T(8,128)(2,1)S(1)}, u32[]{:S(2)}, u32[]{:S(2)}) %collective-permute-start.9) | collective-permute-done | bytes 196640 | tf_op jit(solution)/shard_map/ppermute | solution.py:73
  90.7 2.8 %shard_map.52 = (bf16[384,1024]{1,0:T(8,128)(2,1)S(1)}, f32[96,1024]{1,0:T(8,128)S(1)}, f32[96,1024]{1,0:T(8,128)S(1)}) custom-call(s32[6]{0:T(128)S(1)} %stack.22.prm, bf16[384,1728]{1,0:T(8,128)(2,1)S(1)} %bitcast.14, bf16[96,1024]{1,0:T(8,128)(2,1)S(1)} %collective-permute-done.7.g, bf16[96,1024]{1,0:T(8,128)(2,1)S(1)} %get-tuple-element.26.a0, ...), custom_call_target="tpu_custom_call" | custom-call | tf_op jit(solution)/shard_map/pallas_call | solution.py:309
  93.5 1.6 collective-permute-start.11
  95.1 1.3 collective-permute-done.11.got
  96.4 0.6 shard_map.53.mine
  97.1 3.5 %collective-permute-start.12 = (bf16[96,1024]{1,0:T(8,128)(2,1)S(1)}, bf16[96,1024]{1,0:T(8,128)(2,1)S(1)}, u32[]{:S(2)}, u32[]{:S(2)}) collective-permute-start(bf16[96,1024]{1,0:T(8,128)(2,1)S(1)} %shard_map.53.mine), channel_id=1, source_target_pairs={{0,128},{128,0},{1,129},{129,1},{2,130},{130,2},{3,131},{131,3},{4... | collective-permute-start | bytes 589832 | tf_op jit(solution)/shard_map/ppermute | solution.py:69
  100.5 4.9 %collective-permute-done.12.theirs = bf16[96,1024]{1,0:T(8,128)(2,1)S(1)} collective-permute-done((bf16[96,1024]{1,0:T(8,128)(2,1)S(1)}, bf16[96,1024]{1,0:T(8,128)(2,1)S(1)}, u32[]{:S(2)}, u32[]{:S(2)}) %collective-permute-start.12) | collective-permute-done | bytes 196640 | tf_op jit(solution)/shard_map/ppermute | solution.py:69
  105.4 0.9 shard_map.54
  106.3 1.1 collective-permute-start.13
  107.3 1.1 collective-permute-done.13.b_other
  108.4 4.2 %shard_map.58 = bf16[384,1728]{1,0:T(8,128)(2,1)} custom-call(s32[6]{0:T(128)S(1)} %stack.22.prm, bf16[384,1024]{1,0:T(8,128)(2,1)S(1)} %get-tuple-element.39.full, bf16[96,1024]{1,0:T(8,128)(2,1)S(1)} %get-tuple-element.30.b_own, bf16[96,1024]{1,0:T(8,128)(2,1)S(1)} %collective-permute-done.13.b_other), custom_call_target="tpu_custom_call" | custom-call | tf_op jit(solution)/shard_map/pallas_call | solution.py:309
  112.6 4.6 %all-to-all-start.1 = ((bf16[16,24,1728]{2,1,0:T(8,128)(2,1)}), bf16[16,24,1728]{2,1,0:T(8,128)(2,1)}, u32[]{:S(2)}, u32[]{:S(2)}) async-start(bf16[16,24,1728]{2,1,0:T(8,128)(2,1)} %bitcast.6), calls=%async_computation.1 | async-start | bytes 2752512 | tf_op jit(solution)/shard_map/all_to_all | solution.py:393
  117.3 4.7 %shard_map.55 = (f32[96,1024]{1,0:T(8,128)S(1)}, bf16[96,1024]{1,0:T(8,128)(2,1)S(1)}, bf16[96,1024]{1,0:T(8,128)(2,1)S(1)}, bf16[96,1024]{1,0:T(8,128)(2,1)S(1)}) custom-call(s32[6]{0:T(128)S(1)} %stack.22.prm, bf16[384,1728]{1,0:T(8,128)(2,1)S(1)} %bitcast.15, bf16[96,1024]{1,0:T(8,128)(2,1)S(1)} %get-tuple-element.30.b_own, ...), custom_call_target="tpu_custom_call" | custom-call | tf_op jit(solution)/shard_map/pallas_call | solution.py:309
  122.0 2.5 %collective-permute-start.14 = (bf16[96,1024]{1,0:T(8,128)(2,1)S(1)}, bf16[96,1024]{1,0:T(8,128)(2,1)S(1)}, u32[]{:S(2)}, u32[]{:S(2)}) collective-permute-start(bf16[96,1024]{1,0:T(8,128)(2,1)S(1)} %get-tuple-element.32), channel_id=1, source_target_pairs={{0,1},{1,2},{2,3},{3,0},{4,5},{5,6},{6,7},{7,4},{8,9},{9,10},{10,1... | collective-permute-start | bytes 589832 | tf_op jit(solution)/shard_map/ppermute | solution.py:73
  124.5 1.5 collective-permute-start.16
  126.0 2.1 %collective-permute-done.14.r1 = bf16[96,1024]{1,0:T(8,128)(2,1)S(1)} collective-permute-done((bf16[96,1024]{1,0:T(8,128)(2,1)S(1)}, bf16[96,1024]{1,0:T(8,128)(2,1)S(1)}, u32[]{:S(2)}, u32[]{:S(2)}) %collective-permute-start.14) | collective-permute-done | bytes 196640 | tf_op jit(solution)/shard_map/ppermute | solution.py:73
  128.1 4.9 %collective-permute-done.15.r2 = bf16[96,1024]{1,0:T(8,128)(2,1)S(1)} collective-permute-done((bf16[96,1024]{1,0:T(8,128)(2,1)S(1)}, bf16[96,1024]{1,0:T(8,128)(2,1)S(1)}, u32[]{:S(2)}, u32[]{:S(2)}) %collective-permute-start.15) | collective-permute-done | bytes 196640 | tf_op jit(solution)/shard_map/ppermute | solution.py:73
  133.0 0.8 collective-permute-done.16.r3
  133.9 0.8 shard_map.56
  134.6 4.2 %collective-permute-start.17 = (bf16[96,256]{1,0:T(8,128)(2,1)S(1)}, bf16[96,256]{1,0:T(8,128)(2,1)S(1)}, u32[]{:S(2)}, u32[]{:S(2)}) collective-permute-start(bf16[96,256]{1,0:T(8,128)(2,1)S(1)} %get-tuple-element.35), channel_id=1, source_target_pairs={{64,0},{1,1},{65,2},{4,3},{68,4},{5,5},{69,6},{8,7},{72,8},{9,9},{... | collective-permute-start | bytes 147464 | tf_op jit(solution)/shard_map/ppermute | solution.py:388
  138.8 4.5 %collective-permute-start.18 = (bf16[96,256]{1,0:T(8,128)(2,1)S(1)}, bf16[96,256]{1,0:T(8,128)(2,1)S(1)}, u32[]{:S(2)}, u32[]{:S(2)}) collective-permute-start(bf16[96,256]{1,0:T(8,128)(2,1)S(1)} %get-tuple-element.36), channel_id=1, source_target_pairs={{1,0},{65,1},{0,2},{68,3},{5,4},{69,5},{4,6},{72,7},{9,8},{73,9},{... | collective-permute-start | bytes 147464 | tf_op jit(solution)/shard_map/ppermute | solution.py:388
  143.4 0.7 collective-permute-start.19
  144.0 7.0 %collective-permute-start.20 = (bf16[96,256]{1,0:T(8,128)(2,1)S(1)}, bf16[96,256]{1,0:T(8,128)(2,1)S(1)}, u32[]{:S(2)}, u32[]{:S(2)}) collective-permute-start(bf16[96,256]{1,0:T(8,128)(2,1)S(1)} %get-tuple-element.38), channel_id=1, source_target_pairs={{0,0},{64,1},{1,2},{69,3},{4,4},{68,5},{5,6},{73,7},{8,8},{72,9},{... | collective-permute-start | bytes 147464 | tf_op jit(solution)/shard_map/ppermute | solution.py:388
  151.0 1.5 reduce_sum.12
  152.6 5.4 %collective-permute-start.21 = (bf16[12,1728]{1,0:T(8,128)(2,1)S(1)}, bf16[12,1728]{1,0:T(8,128)(2,1)S(1)}, u32[]{:S(2)}, u32[]{:S(2)}) collective-permute-start(bf16[12,1728]{1,0:T(8,128)(2,1)S(1)} %get-tuple-element.48), channel_id=1, source_target_pairs={{1,0},{0,1},{5,2},{4,3},{9,4},{8,5},{13,6},{12,7},{65,8},{64,9},{6... | collective-permute-start | bytes 124424 | tf_op jit(solution)/shard_map/ppermute | solution.py:398
  158.0 2.4 %collective-permute-start.22 = (bf16[12,1728]{1,0:T(8,128)(2,1)S(1)}, bf16[12,1728]{1,0:T(8,128)(2,1)S(1)}, u32[]{:S(2)}, u32[]{:S(2)}) collective-permute-start(bf16[12,1728]{1,0:T(8,128)(2,1)S(1)} %get-tuple-element.49), channel_id=1, source_target_pairs={{0,0},{1,1},{4,2},{5,3},{8,4},{9,5},{12,6},{13,7},{64,8},{65,9},{6... | collective-permute-start | bytes 124424 | tf_op jit(solution)/shard_map/ppermute | solution.py:397
  160.4 1.4 shard_map.57
  161.7 1.6 collective-permute-done.21
  163.3 7.4 %collective-permute-done.22 = bf16[12,1728]{1,0:T(8,128)(2,1)S(1)} collective-permute-done((bf16[12,1728]{1,0:T(8,128)(2,1)S(1)}, bf16[12,1728]{1,0:T(8,128)(2,1)S(1)}, u32[]{:S(2)}, u32[]{:S(2)}) %collective-permute-start.22) | collective-permute-done | bytes 41504 | tf_op jit(solution)/shard_map/ppermute | solution.py:397
  172.1 0.7 select_convert_fusion
  (41 shorter events, 2.7 us)
Async XLA Ops:
  2.7 11.5 %collective-permute-start.5 = (bf16[12,1728]{1,0:T(8,128)(2,1)S(1)}, bf16[12,1728]{1,0:T(8,128)(2,1)S(1)}, u32[]{:S(2)}, u32[]{:S(2)}) collective-permute-start(bf16[12,1728]{1,0:T(8,128)(2,1)S(1)} %select_n.108), channel_id=1, source_target_pairs={{0,1},{1,0},{2,5},{3,4},{4,9},{5,8},{6,13},{7,12},{8,65},{9,64},{1... | collective-permute-start | bytes 124424 | tf_op jit(solution)/shard_map/ppermute | solution.py:335
  10.2 10.4 %collective-permute-start.6 = (bf16[12,1728]{1,0:T(8,128)(2,1)S(1)}, bf16[12,1728]{1,0:T(8,128)(2,1)S(1)}, u32[]{:S(2)}, u32[]{:S(2)}) collective-permute-start(bf16[12,1728]{1,0:T(8,128)(2,1)S(1)} %select_n.110), channel_id=1, source_target_pairs={{0,0},{1,1},{2,4},{3,5},{4,8},{5,9},{6,12},{7,13},{8,64},{9,65},{1... | collective-permute-start | bytes 124424 | tf_op jit(solution)/shard_map/ppermute | solution.py:334
  21.8 3.8 %copy-start.1 = (bf16[256,384]{1,0:T(8,128)(2,1)S(1)}, bf16[256,384]{1,0:T(8,128)(2,1)}, u32[]{:S(2)}) copy-start(bf16[256,384]{1,0:T(8,128)(2,1)} %param.3) | copy-start | bytes 589828
  21.8 7.6 %copy-start = (s32[2,2]{1,0:T(2,128)S(1)}, s32[2,2]{1,0:T(2,128)}, u32[]{:S(2)}) copy-start(s32[2,2]{1,0:T(2,128)} %param.5) | copy-start | bytes 52
  21.8 68.9 %all-to-all-start = ((bf16[16,24,1728]{2,1,0:T(8,128)(2,1)}), bf16[16,24,1728]{2,1,0:T(8,128)(2,1)S(1)}, u32[]{:S(2)}, u32[]{:S(2)}) async-start(bf16[16,24,1728]{2,1,0:T(8,128)(2,1)} %broadcast_in_dim.3), calls=%async_computation | async-start | bytes 2752512 | tf_op jit(solution)/shard_map/all_to_all | solution.py:340
  25.7 7.0 %collective-permute-start = (bf16[256,384]{1,0:T(8,128)(2,1)S(1)}, bf16[256,384]{1,0:T(8,128)(2,1)S(1)}, u32[]{:S(2)}, u32[]{:S(2)}) collective-permute-start(bf16[256,384]{1,0:T(8,128)(2,1)S(1)} %copy-done.1), channel_id=1, source_target_pairs={{0,1},{1,2},{2,3},{3,4},{4,5},{5,6},{6,7},{7,8},{8,9},{9,10},{10,1... | collective-permute-start | bytes 589832 | tf_op jit(solution)/shard_map/ppermute | solution.py:342
  33.4 7.7 %collective-permute-start.1 = (bf16[96,256]{1,0:T(8,128)(2,1)S(1)}, bf16[96,256]{1,0:T(8,128)(2,1)S(1)}, u32[]{:S(2)}, u32[]{:S(2)}) collective-permute-start(bf16[96,256]{1,0:T(8,128)(2,1)S(1)} %get-tuple-element.21), channel_id=1, source_target_pairs={{0,0},{1,64},{2,1},{3,65},{4,4},{5,68},{6,5},{7,69},{8,8},{9,72},{... | collective-permute-start | bytes 147464 | tf_op jit(solution)/shard_map/ppermute | solution.py:346
  38.4 34.9 %collective-permute-start.2 = (bf16[96,256]{1,0:T(8,128)(2,1)S(1)}, bf16[96,256]{1,0:T(8,128)(2,1)S(1)}, u32[]{:S(2)}, u32[]{:S(2)}) collective-permute-start(bf16[96,256]{1,0:T(8,128)(2,1)S(1)} %get-tuple-element.22), channel_id=1, source_target_pairs={{0,64},{1,1},{2,65},{3,0},{4,68},{5,5},{6,69},{7,4},{8,72},{9,9},{... | collective-permute-start | bytes 147464 | tf_op jit(solution)/shard_map/ppermute | solution.py:346
  40.3 33.0 %collective-permute-start.3 = (bf16[96,256]{1,0:T(8,128)(2,1)S(1)}, bf16[96,256]{1,0:T(8,128)(2,1)S(1)}, u32[]{:S(2)}, u32[]{:S(2)}) collective-permute-start(bf16[96,256]{1,0:T(8,128)(2,1)S(1)} %get-tuple-element.23), channel_id=1, source_target_pairs={{0,1},{1,65},{2,0},{3,64},{4,5},{5,69},{6,4},{7,68},{8,9},{9,73},{... | collective-permute-start | bytes 147464 | tf_op jit(solution)/shard_map/ppermute | solution.py:346
  40.4 32.9 %collective-permute-start.4 = (bf16[96,256]{1,0:T(8,128)(2,1)S(1)}, bf16[96,256]{1,0:T(8,128)(2,1)S(1)}, u32[]{:S(2)}, u32[]{:S(2)}) collective-permute-start(bf16[96,256]{1,0:T(8,128)(2,1)S(1)} %get-tuple-element.24), channel_id=1, source_target_pairs={{0,65},{1,0},{2,64},{3,1},{4,69},{5,4},{6,68},{7,5},{8,73},{9,8},{... | collective-permute-start | bytes 147464 | tf_op jit(solution)/shard_map/ppermute | solution.py:346
  74.2 9.0 %collective-permute-start.7 = (bf16[96,1024]{1,0:T(8,128)(2,1)S(1)}, bf16[96,1024]{1,0:T(8,128)(2,1)S(1)}, u32[]{:S(2)}, u32[]{:S(2)}) collective-permute-start(bf16[96,1024]{1,0:T(8,128)(2,1)S(1)} %get-tuple-element.25.x), channel_id=1, source_target_pairs={{0,128},{128,0},{1,129},{129,1},{2,130},{130,2},{3,131},{131,3},{4... | collective-permute-start | bytes 589832 | tf_op jit(solution)/shard_map/ppermute | solution.py:69
  74.3 8.9 %collective-permute-start.8 = (bf16[96,1024]{1,0:T(8,128)(2,1)S(1)}, bf16[96,1024]{1,0:T(8,128)(2,1)S(1)}, u32[]{:S(2)}, u32[]{:S(2)}) collective-permute-start(bf16[96,1024]{1,0:T(8,128)(2,1)S(1)} %get-tuple-element.26.a0), channel_id=1, source_target_pairs={{0,1},{1,2},{2,3},{3,0},{4,5},{5,6},{6,7},{7,4},{8,9},{9,10},{10,1... | collective-permute-start | bytes 589832 | tf_op jit(solution)/shard_map/ppermute | solution.py:73
  78.5 11.9 %collective-permute-start.9 = (bf16[96,1024]{1,0:T(8,128)(2,1)S(1)}, bf16[96,1024]{1,0:T(8,128)(2,1)S(1)}, u32[]{:S(2)}, u32[]{:S(2)}) collective-permute-start(bf16[96,1024]{1,0:T(8,128)(2,1)S(1)} %get-tuple-element.26.a0), channel_id=1, source_target_pairs={{0,2},{1,3},{2,0},{3,1},{4,6},{5,7},{6,4},{7,5},{8,10},{9,11},{10,... | collective-permute-start | bytes 589832 | tf_op jit(solution)/shard_map/ppermute | solution.py:73
  81.3 9.5 %collective-permute-start.10 = (bf16[96,1024]{1,0:T(8,128)(2,1)S(1)}, bf16[96,1024]{1,0:T(8,128)(2,1)S(1)}, u32[]{:S(2)}, u32[]{:S(2)}) collective-permute-start(bf16[96,1024]{1,0:T(8,128)(2,1)S(1)} %get-tuple-element.26.a0), channel_id=1, source_target_pairs={{0,3},{1,0},{2,1},{3,2},{4,7},{5,4},{6,5},{7,6},{8,11},{9,8},{10,9... | collective-permute-start | bytes 589832 | tf_op jit(solution)/shard_map/ppermute | solution.py:73
  93.5 2.9 %collective-permute-start.11 = (f32[96,1024]{1,0:T(8,128)S(1)}, f32[96,1024]{1,0:T(8,128)S(1)}, u32[]{:S(2)}, u32[]{:S(2)}) collective-permute-start(f32[96,1024]{1,0:T(8,128)S(1)} %get-tuple-element.28), channel_id=1, source_target_pairs={{0,64},{64,0},{1,65},{65,1},{2,66},{66,2},{3,67},{67,3},{4,68},{68... | collective-permute-start | bytes 1179656 | tf_op jit(solution)/shard_map/ppermute | solution.py:69
  97.1 8.4 %collective-permute-start.12 = (bf16[96,1024]{1,0:T(8,128)(2,1)S(1)}, bf16[96,1024]{1,0:T(8,128)(2,1)S(1)}, u32[]{:S(2)}, u32[]{:S(2)}) collective-permute-start(bf16[96,1024]{1,0:T(8,128)(2,1)S(1)} %shard_map.53.mine), channel_id=1, source_target_pairs={{0,128},{128,0},{1,129},{129,1},{2,130},{130,2},{3,131},{131,3},{4... | collective-permute-start | bytes 589832 | tf_op jit(solution)/shard_map/ppermute | solution.py:69
  106.3 2.1 %collective-permute-start.13 = (bf16[96,1024]{1,0:T(8,128)(2,1)S(1)}, bf16[96,1024]{1,0:T(8,128)(2,1)S(1)}, u32[]{:S(2)}, u32[]{:S(2)}) collective-permute-start(bf16[96,1024]{1,0:T(8,128)(2,1)S(1)} %get-tuple-element.30.b_own), channel_id=1, source_target_pairs={{0,64},{64,0},{1,65},{65,1},{2,66},{66,2},{3,67},{67,3},{4,68},{68... | collective-permute-start | bytes 589832 | tf_op jit(solution)/shard_map/ppermute | solution.py:69
  112.6 38.4 %all-to-all-start.1 = ((bf16[16,24,1728]{2,1,0:T(8,128)(2,1)}), bf16[16,24,1728]{2,1,0:T(8,128)(2,1)}, u32[]{:S(2)}, u32[]{:S(2)}) async-start(bf16[16,24,1728]{2,1,0:T(8,128)(2,1)} %bitcast.6), calls=%async_computation.1 | async-start | bytes 2752512 | tf_op jit(solution)/shard_map/all_to_all | solution.py:393
  122.0 6.2 %collective-permute-start.14 = (bf16[96,1024]{1,0:T(8,128)(2,1)S(1)}, bf16[96,1024]{1,0:T(8,128)(2,1)S(1)}, u32[]{:S(2)}, u32[]{:S(2)}) collective-permute-start(bf16[96,1024]{1,0:T(8,128)(2,1)S(1)} %get-tuple-element.32), channel_id=1, source_target_pairs={{0,1},{1,2},{2,3},{3,0},{4,5},{5,6},{6,7},{7,4},{8,9},{9,10},{10,1... | collective-permute-start | bytes 589832 | tf_op jit(solution)/shard_map/ppermute | solution.py:73
  124.5 8.5 %collective-permute-start.15 = (bf16[96,1024]{1,0:T(8,128)(2,1)S(1)}, bf16[96,1024]{1,0:T(8,128)(2,1)S(1)}, u32[]{:S(2)}, u32[]{:S(2)}) collective-permute-start(bf16[96,1024]{1,0:T(8,128)(2,1)S(1)} %get-tuple-element.33), channel_id=1, source_target_pairs={{0,2},{1,3},{2,0},{3,1},{4,6},{5,7},{6,4},{7,5},{8,10},{9,11},{10,... | collective-permute-start | bytes 589832 | tf_op jit(solution)/shard_map/ppermute | solution.py:73
  124.5 9.4 %collective-permute-start.16 = (bf16[96,1024]{1,0:T(8,128)(2,1)S(1)}, bf16[96,1024]{1,0:T(8,128)(2,1)S(1)}, u32[]{:S(2)}, u32[]{:S(2)}) collective-permute-start(bf16[96,1024]{1,0:T(8,128)(2,1)S(1)} %get-tuple-element.34), channel_id=1, source_target_pairs={{0,3},{1,0},{2,1},{3,2},{4,7},{5,4},{6,5},{7,6},{8,11},{9,8},{10,9... | collective-permute-start | bytes 589832 | tf_op jit(solution)/shard_map/ppermute | solution.py:73
  134.6 23.3 %collective-permute-start.17 = (bf16[96,256]{1,0:T(8,128)(2,1)S(1)}, bf16[96,256]{1,0:T(8,128)(2,1)S(1)}, u32[]{:S(2)}, u32[]{:S(2)}) collective-permute-start(bf16[96,256]{1,0:T(8,128)(2,1)S(1)} %get-tuple-element.35), channel_id=1, source_target_pairs={{64,0},{1,1},{65,2},{4,3},{68,4},{5,5},{69,6},{8,7},{72,8},{9,9},{... | collective-permute-start | bytes 147464 | tf_op jit(solution)/shard_map/ppermute | solution.py:388
  138.8 21.5 %collective-permute-start.18 = (bf16[96,256]{1,0:T(8,128)(2,1)S(1)}, bf16[96,256]{1,0:T(8,128)(2,1)S(1)}, u32[]{:S(2)}, u32[]{:S(2)}) collective-permute-start(bf16[96,256]{1,0:T(8,128)(2,1)S(1)} %get-tuple-element.36), channel_id=1, source_target_pairs={{1,0},{65,1},{0,2},{68,3},{5,4},{69,5},{4,6},{72,7},{9,8},{73,9},{... | collective-permute-start | bytes 147464 | tf_op jit(solution)/shard_map/ppermute | solution.py:388
  143.4 17.0 %collective-permute-start.19 = (bf16[96,256]{1,0:T(8,128)(2,1)S(1)}, bf16[96,256]{1,0:T(8,128)(2,1)S(1)}, u32[]{:S(2)}, u32[]{:S(2)}) collective-permute-start(bf16[96,256]{1,0:T(8,128)(2,1)S(1)} %get-tuple-element.37), channel_id=1, source_target_pairs={{65,0},{0,1},{64,2},{5,3},{69,4},{4,5},{68,6},{9,7},{73,8},{8,9},{... | collective-permute-start | bytes 147464 | tf_op jit(solution)/shard_map/ppermute | solution.py:388
  144.0 16.3 %collective-permute-start.20 = (bf16[96,256]{1,0:T(8,128)(2,1)S(1)}, bf16[96,256]{1,0:T(8,128)(2,1)S(1)}, u32[]{:S(2)}, u32[]{:S(2)}) collective-permute-start(bf16[96,256]{1,0:T(8,128)(2,1)S(1)} %get-tuple-element.38), channel_id=1, source_target_pairs={{0,0},{64,1},{1,2},{69,3},{4,4},{68,5},{5,6},{73,7},{8,8},{72,9},{... | collective-permute-start | bytes 147464 | tf_op jit(solution)/shard_map/ppermute | solution.py:388
  152.6 10.8 %collective-permute-start.21 = (bf16[12,1728]{1,0:T(8,128)(2,1)S(1)}, bf16[12,1728]{1,0:T(8,128)(2,1)S(1)}, u32[]{:S(2)}, u32[]{:S(2)}) collective-permute-start(bf16[12,1728]{1,0:T(8,128)(2,1)S(1)} %get-tuple-element.48), channel_id=1, source_target_pairs={{1,0},{0,1},{5,2},{4,3},{9,4},{8,5},{13,6},{12,7},{65,8},{64,9},{6... | collective-permute-start | bytes 124424 | tf_op jit(solution)/shard_map/ppermute | solution.py:398
  158.0 12.8 %collective-permute-start.22 = (bf16[12,1728]{1,0:T(8,128)(2,1)S(1)}, bf16[12,1728]{1,0:T(8,128)(2,1)S(1)}, u32[]{:S(2)}, u32[]{:S(2)}) collective-permute-start(bf16[12,1728]{1,0:T(8,128)(2,1)S(1)} %get-tuple-element.49), channel_id=1, source_target_pairs={{0,0},{1,1},{4,2},{5,3},{8,4},{9,5},{12,6},{13,7},{64,8},{65,9},{6... | collective-permute-start | bytes 124424 | tf_op jit(solution)/shard_map/ppermute | solution.py:397

commit v2 on v1

--- a/solution.py
+++ b/solution.py
@@ -56,7 +56,8 @@
         if xh == 0:
             target = (0, z % 2, 2 * (z // 2) + xl, y >> 1, 2 * core + b)
         else:
-            target = (1, b, 4 * core + 2 * (z % 2) + xl, y >> 1, z // 2)
+            far = 2 * core + (y >> 1)
+            target = (1, b, (z + (far if z % 2 else -far)) % 8, xl, z // 2)
         pairs.append((flat(xh, core, z, xl, y), flat(*target)))
     return pairs
 
@@ -184,7 +185,14 @@
         full[rows((prm[2] + 4 - d) % 4), :] = ref[...]
 
 
-def first_kernel(prm, w, g, a0, a1, a2, a3, full, keep, send, d_ref, res):
+def parts_in_order(prm):
+    for k in range(16):
+        far, odd, xl = 2 * (k >> 3) + (k & 1), (k >> 2) & 1, (k >> 1) & 1
+        plane = (2 * prm[2] + (1 + far if odd else 8 - far)) % 8
+        yield k, rows(2 * plane + xl, 24)
+
+
+def first_kernel(prm, w, g, a0, a1, a2, a3, full, keep, send, sorted_w, d_ref, res):
     gather_chunks(prm, a0, (a1, a2, a3), full)
 
     @pl.when(prm[0] == 0)
@@ -193,10 +201,12 @@
 
     @pl.when(prm[0] == 1)
     def _():
+        for k, place in parts_in_order(prm):
+            sorted_w[k * 24 : (k + 1) * 24, :] = w[place, :]
         for k in range(2):
             build_moved(full[k * PAIR : (k + 1) * PAIR, :], d_ref)
             part = jnp.dot(
-                w[k * PAIR : (k + 1) * PAIR, :], d_ref[...], preferred_element_type=F32
+                sorted_w[k * PAIR : (k + 1) * PAIR, :], d_ref[...], preferred_element_type=F32
             )
             if k == 0:
                 res[...] = part
@@ -246,21 +256,24 @@
     def product(lhs):
         return lax.dot_general(
             lhs, d_ref[...], (((1,), (1,)), ((), ())), preferred_element_type=F32
-        ).astype(BF16)
+        )
 
     @pl.when(prm[0] == 0)
     def _():
         build_moved(pair[...], d_ref)
-        dw[...] = product(full[...])
+        dw[...] = product(full[...]).astype(BF16)
 
     @pl.when(prm[0] == 1)
     def _():
         for k in range(2):
             build_moved(full[k * PAIR : (k + 1) * PAIR, :], d_ref)
-            dw[k * PAIR : (k + 1) * PAIR, :] = product(pair[...])
-
-
-def second_kernel(prm, w, b_own, b_other, keep, s1, s2, s3, pair, d_ref, res):
+            part = product(pair[...])
+            for m, place in parts_in_order(prm):
+                if m // 8 == k:
+                    dw[place, :] = part[m % 8 * 24 : (m % 8 + 1) * 24, :].astype(BF16)
+
+
+def second_kernel(prm, w, sorted_w, b_own, b_other, keep, s1, s2, s3, pair, d_ref, res):
     pair_up(prm, b_own, b_other, pair)
 
     @pl.when(prm[0] == 0)
@@ -272,7 +285,7 @@
     def _():
         for k in range(2):
             res[k * PAIR : (k + 1) * PAIR, :] = convolve(
-                w[k * PAIR : (k + 1) * PAIR, :], pair[...]
+                sorted_w[k * PAIR : (k + 1) * PAIR, :], pair[...]
             )
 
     keep[...] = res[rows(prm[2]), :]
@@ -348,9 +361,9 @@
     others = [turn_y(a, d) for d in (1, 2, 3)]
     g = swap(x, "xh")
 
-    full, keep, send = call(
+    full, keep, send, sorted_w = call(
         first_kernel,
-        [((QUAD, PIX), BF16), own32, own32],
+        [((QUAD, PIX), BF16), own32, own32, ((QUAD, LANES), BF16)],
         [((LANES, PIX), BF16), ((PAIR, PIX), F32)],
         prm,
         w,
@@ -379,6 +392,7 @@
         [((PAIR, PIX), BF16), ((LANES, PIX), BF16), ((QUAD, PIX), F32)],
         prm,
         w,
+        sorted_w,
         b,
         b_other,
         grant=24,

time: 173 us -> 175 us (1.012)
  the two profiles are of different devices: /device:TPU:21 before, /device:TPU:1 now
where the time goes in v2:
time: 175 us; the launch traced here: 172 us
  waiting for transfers between devices  73 us (42%)
  starting transfers between devices  72.2 us (41%)
  Pallas kernels  15.1 us (9%)
  local copies, waits for them, and re-layouts  7.43 us (4%)
  other arithmetic  2.78 us (2%)
    ppermute x1, waiting for transfers between devices, step(): lax.ppermute(signals, FSDP, [(i, (i + 1) % 64) for i in range(64)])  35.9 us
    ppermute x6, waiting for transfers between devices, turn_y(): return lax.ppermute(value, 'y', [(i, (i + d) % 4) for i in range(4)])  16.1 us
    pallas_call x9, Pallas kernels, call(): pl.pallas_call(kernel, out_shape=[jax.ShapeDtypeStruct(s, d) for s, d in...  15.1 us
    ppermute x4, starting transfers between devices, step(): lax.ppermute(b, AX, back(pixel_pairs(v, 1)))  14.7 us
    ppermute x4, waiting for transfers between devices, swap(): return lax.ppermute(value, axis, [(0, 1), (1, 0)])  12.1 us
    all_to_all x1, starting transfers between devices, step(): lax.all_to_all(copies, WEIGHT_GROUP, 0, 0, tiled=True).reshape(QUAD, LANES)  11.9 us
    ppermute x4, starting transfers between devices, step(): lax.ppermute(b, AX, pixel_pairs(v, 0))  8.88 us
    ppermute x4, starting transfers between devices, swap(): return lax.ppermute(value, axis, [(0, 1), (1, 0)])  7.84 us
  transfers between devices with their start and end apart: 25, of which 16 were waited for; matrix products, arithmetic and copies ran while one was open for 1% of the time, Pallas kernels for 4%

profile of v2, /device:TPU:1, one launch (start us, length us, event | category | flops | bytes accessed | tf_op | source)
XLA Modules:
  0.0 171.6 jit_solution(10601625447721027488)
XLA Ops:
  0.6 1.0 reshape.37
  2.7 6.2 %collective-permute-start.6 = (bf16[12,1728]{1,0:T(8,128)(2,1)S(1)}, bf16[12,1728]{1,0:T(8,128)(2,1)S(1)}, u32[]{:S(2)}, u32[]{:S(2)}) collective-permute-start(bf16[12,1728]{1,0:T(8,128)(2,1)S(1)} %select_n.110), channel_id=1, source_target_pairs={{0,0},{1,1},{2,4},{3,5},{4,8},{5,9},{6,12},{7,13},{8,64},{9,65},{1... | collective-permute-start | bytes 124424 | tf_op jit(solution)/shard_map/ppermute | solution.py:347
  9.0 3.9 %collective-permute-start.5 = (bf16[12,1728]{1,0:T(8,128)(2,1)S(1)}, bf16[12,1728]{1,0:T(8,128)(2,1)S(1)}, u32[]{:S(2)}, u32[]{:S(2)}) collective-permute-start(bf16[12,1728]{1,0:T(8,128)(2,1)S(1)} %select_n.108), channel_id=1, source_target_pairs={{0,1},{1,0},{2,5},{3,4},{4,9},{5,8},{6,13},{7,12},{8,65},{9,64},{1... | collective-permute-start | bytes 124424 | tf_op jit(solution)/shard_map/ppermute | solution.py:348
  12.9 2.5 %collective-permute-done.5 = bf16[12,1728]{1,0:T(8,128)(2,1)S(1)} collective-permute-done((bf16[12,1728]{1,0:T(8,128)(2,1)S(1)}, bf16[12,1728]{1,0:T(8,128)(2,1)S(1)}, u32[]{:S(2)}, u32[]{:S(2)}) %collective-permute-start.5) | collective-permute-done | bytes 41504 | tf_op jit(solution)/shard_map/ppermute | solution.py:348
  15.4 1.2 broadcast_in_dim.3
  16.7 11.9 %all-to-all-start = ((bf16[16,24,1728]{2,1,0:T(8,128)(2,1)}), bf16[16,24,1728]{2,1,0:T(8,128)(2,1)S(1)}, u32[]{:S(2)}, u32[]{:S(2)}) async-start(bf16[16,24,1728]{2,1,0:T(8,128)(2,1)} %broadcast_in_dim.3), calls=%async_computation | async-start | bytes 2752512 | tf_op jit(solution)/shard_map/all_to_all | solution.py:353
  28.8 35.9 %collective-permute-done.x_ref = bf16[256,384]{1,0:T(8,128)(2,1)S(1)} collective-permute-done((bf16[256,384]{1,0:T(8,128)(2,1)S(1)}, bf16[256,384]{1,0:T(8,128)(2,1)S(1)}, u32[]{:S(2)}, u32[]{:S(2)}) %collective-permute-start) | collective-permute-done | bytes 196640 | tf_op jit(solution)/shard_map/ppermute | solution.py:355
  64.7 0.7 shard_map.50
  65.4 1.9 %collective-permute-start.1 = (bf16[96,256]{1,0:T(8,128)(2,1)S(1)}, bf16[96,256]{1,0:T(8,128)(2,1)S(1)}, u32[]{:S(2)}, u32[]{:S(2)}) collective-permute-start(bf16[96,256]{1,0:T(8,128)(2,1)S(1)} %get-tuple-element.22), channel_id=1, source_target_pairs={{0,0},{1,64},{2,1},{3,65},{4,4},{5,68},{6,5},{7,69},{8,8},{9,72},{... | collective-permute-start | bytes 147464 | tf_op jit(solution)/shard_map/ppermute | solution.py:359
  67.3 1.9 %collective-permute-start.2 = (bf16[96,256]{1,0:T(8,128)(2,1)S(1)}, bf16[96,256]{1,0:T(8,128)(2,1)S(1)}, u32[]{:S(2)}, u32[]{:S(2)}) collective-permute-start(bf16[96,256]{1,0:T(8,128)(2,1)S(1)} %get-tuple-element.23), channel_id=1, source_target_pairs={{0,64},{1,1},{2,65},{3,0},{4,68},{5,5},{6,69},{7,4},{8,72},{9,9},{... | collective-permute-start | bytes 147464 | tf_op jit(solution)/shard_map/ppermute | solution.py:359
  69.2 3.1 %collective-permute-start.3 = (bf16[96,256]{1,0:T(8,128)(2,1)S(1)}, bf16[96,256]{1,0:T(8,128)(2,1)S(1)}, u32[]{:S(2)}, u32[]{:S(2)}) collective-permute-start(bf16[96,256]{1,0:T(8,128)(2,1)S(1)} %get-tuple-element.24), channel_id=1, source_target_pairs={{0,1},{1,65},{2,0},{3,64},{4,5},{5,69},{6,4},{7,68},{8,9},{9,73},{... | collective-permute-start | bytes 147464 | tf_op jit(solution)/shard_map/ppermute | solution.py:359
  72.4 1.9 %collective-permute-start.4 = (bf16[96,256]{1,0:T(8,128)(2,1)S(1)}, bf16[96,256]{1,0:T(8,128)(2,1)S(1)}, u32[]{:S(2)}, u32[]{:S(2)}) collective-permute-start(bf16[96,256]{1,0:T(8,128)(2,1)S(1)} %get-tuple-element.25), channel_id=1, source_target_pairs={{0,65},{1,0},{2,64},{3,1},{4,69},{5,4},{6,68},{7,5},{8,73},{9,8},{... | collective-permute-start | bytes 147464 | tf_op jit(solution)/shard_map/ppermute | solution.py:359
  74.3 0.8 collective-permute-done.3.refs_2_
  75.1 4.2 %collective-permute-done.4.refs_3_ = bf16[96,256]{1,0:T(8,128)(2,1)S(1)} collective-permute-done((bf16[96,256]{1,0:T(8,128)(2,1)S(1)}, bf16[96,256]{1,0:T(8,128)(2,1)S(1)}, u32[]{:S(2)}, u32[]{:S(2)}) %collective-permute-start.4) | collective-permute-done | bytes 49184 | tf_op jit(solution)/shard_map/ppermute | solution.py:359
  79.3 0.8 shard_map.51
  80.1 5.7 %collective-permute-start.7 = (bf16[96,1024]{1,0:T(8,128)(2,1)S(1)}, bf16[96,1024]{1,0:T(8,128)(2,1)S(1)}, u32[]{:S(2)}, u32[]{:S(2)}) collective-permute-start(bf16[96,1024]{1,0:T(8,128)(2,1)S(1)} %get-tuple-element.26.x), channel_id=1, source_target_pairs={{0,128},{128,0},{1,129},{129,1},{2,130},{130,2},{3,131},{131,3},{4... | collective-permute-start | bytes 589832 | tf_op jit(solution)/shard_map/ppermute | solution.py:70
  85.8 1.5 collective-permute-start.8
  87.3 2.1 %collective-permute-done.7.g = bf16[96,1024]{1,0:T(8,128)(2,1)S(1)} collective-permute-done((bf16[96,1024]{1,0:T(8,128)(2,1)S(1)}, bf16[96,1024]{1,0:T(8,128)(2,1)S(1)}, u32[]{:S(2)}, u32[]{:S(2)}) %collective-permute-start.7) | collective-permute-done | bytes 196640 | tf_op jit(solution)/shard_map/ppermute | solution.py:70
  89.3 3.4 %collective-permute-done.10.a3 = bf16[96,1024]{1,0:T(8,128)(2,1)S(1)} collective-permute-done((bf16[96,1024]{1,0:T(8,128)(2,1)S(1)}, bf16[96,1024]{1,0:T(8,128)(2,1)S(1)}, u32[]{:S(2)}, u32[]{:S(2)}) %collective-permute-start.10) | collective-permute-done | bytes 196640 | tf_op jit(solution)/shard_map/ppermute | solution.py:74
  92.7 1.2 collective-permute-done.9.a2
  94.6 2.7 %collective-permute-done.8.a1 = bf16[96,1024]{1,0:T(8,128)(2,1)S(1)} collective-permute-done((bf16[96,1024]{1,0:T(8,128)(2,1)S(1)}, bf16[96,1024]{1,0:T(8,128)(2,1)S(1)}, u32[]{:S(2)}, u32[]{:S(2)}) %collective-permute-start.8) | collective-permute-done | bytes 196640 | tf_op jit(solution)/shard_map/ppermute | solution.py:74
  98.0 0.9 copy-done.1
  99.0 0.9 copy-done.3
  99.9 3.2 %shard_map.52 = (bf16[384,1024]{1,0:T(8,128)(2,1)S(1)}, f32[96,1024]{1,0:T(8,128)S(1)}, f32[96,1024]{1,0:T(8,128)S(1)}, bf16[384,1728]{1,0:T(8,128)(2,1)S(1)}) custom-call(s32[6]{0:T(128)S(1)} %stack.22.prm, bf16[384,1728]{1,0:T(8,128)(2,1)S(1)} %bitcast.14, bf16[96,1024]{1,0:T(8,128)(2,1)S(1)} %collective-permute-done.7.g, ...), custom_call_target="tpu_custom_call" | custom-call | tf_op jit(solution)/shard_map/pallas_call | solution.py:322
  103.7 1.3 collective-permute-done.11.got
  105.9 7.6 %collective-permute-done.12.theirs = bf16[96,1024]{1,0:T(8,128)(2,1)S(1)} collective-permute-done((bf16[96,1024]{1,0:T(8,128)(2,1)S(1)}, bf16[96,1024]{1,0:T(8,128)(2,1)S(1)}, u32[]{:S(2)}, u32[]{:S(2)}) %collective-permute-start.12) | collective-permute-done | bytes 196640 | tf_op jit(solution)/shard_map/ppermute | solution.py:70
  113.5 1.2 shard_map.54
  114.7 1.3 collective-permute-start.13
  116.1 1.1 collective-permute-done.13.b_other
  117.1 3.5 %shard_map.58 = bf16[384,1728]{1,0:T(8,128)(2,1)} custom-call(s32[6]{0:T(128)S(1)} %stack.22.prm, bf16[384,1024]{1,0:T(8,128)(2,1)S(1)} %get-tuple-element.41.full, bf16[96,1024]{1,0:T(8,128)(2,1)S(1)} %get-tuple-element.32.b_own, bf16[96,1024]{1,0:T(8,128)(2,1)S(1)} %collective-permute-done.13.b_other), custom_call_target="tpu_custom_call" | custom-call | tf_op jit(solution)/shard_map/pallas_call | solution.py:322
  120.6 4.4 %all-to-all-start.1 = ((bf16[16,24,1728]{2,1,0:T(8,128)(2,1)}), bf16[16,24,1728]{2,1,0:T(8,128)(2,1)}, u32[]{:S(2)}, u32[]{:S(2)}) async-start(bf16[16,24,1728]{2,1,0:T(8,128)(2,1)} %bitcast.6), calls=%async_computation.1 | async-start | bytes 2752512 | tf_op jit(solution)/shard_map/all_to_all | solution.py:407
  125.0 2.4 %shard_map.55 = (f32[96,1024]{1,0:T(8,128)S(1)}, bf16[96,1024]{1,0:T(8,128)(2,1)S(1)}, bf16[96,1024]{1,0:T(8,128)(2,1)S(1)}, bf16[96,1024]{1,0:T(8,128)(2,1)S(1)}) custom-call(s32[6]{0:T(128)S(1)} %stack.22.prm, bf16[384,1728]{1,0:T(8,128)(2,1)S(1)} %bitcast.15, bf16[384,1728]{1,0:T(8,128)(2,1)S(1)} %get-tuple-element.31.sorted_w, ...), custom_call_target="tpu_custom_call" | custom-call | tf_op jit(solution)/shard_map/pallas_call | solution.py:322
  127.5 2.1 %collective-permute-start.15 = (bf16[96,1024]{1,0:T(8,128)(2,1)S(1)}, bf16[96,1024]{1,0:T(8,128)(2,1)S(1)}, u32[]{:S(2)}, u32[]{:S(2)}) collective-permute-start(bf16[96,1024]{1,0:T(8,128)(2,1)S(1)} %get-tuple-element.35), channel_id=1, source_target_pairs={{0,2},{1,3},{2,0},{3,1},{4,6},{5,7},{6,4},{7,5},{8,10},{9,11},{10,... | collective-permute-start | bytes 589832 | tf_op jit(solution)/shard_map/ppermute | solution.py:74
  129.5 0.9 collective-permute-start.16
  130.5 4.8 %collective-permute-done.14.r1 = bf16[96,1024]{1,0:T(8,128)(2,1)S(1)} collective-permute-done((bf16[96,1024]{1,0:T(8,128)(2,1)S(1)}, bf16[96,1024]{1,0:T(8,128)(2,1)S(1)}, u32[]{:S(2)}, u32[]{:S(2)}) %collective-permute-start.14) | collective-permute-done | bytes 196640 | tf_op jit(solution)/shard_map/ppermute | solution.py:74
  135.2 3.1 %collective-permute-done.15.r2 = bf16[96,1024]{1,0:T(8,128)(2,1)S(1)} collective-permute-done((bf16[96,1024]{1,0:T(8,128)(2,1)S(1)}, bf16[96,1024]{1,0:T(8,128)(2,1)S(1)}, u32[]{:S(2)}, u32[]{:S(2)}) %collective-permute-start.15) | collective-permute-done | bytes 196640 | tf_op jit(solution)/shard_map/ppermute | solution.py:74
  138.3 0.9 collective-permute-done.16.r3
  139.3 1.3 shard_map.56
  140.6 3.5 %collective-permute-start.17 = (bf16[96,256]{1,0:T(8,128)(2,1)S(1)}, bf16[96,256]{1,0:T(8,128)(2,1)S(1)}, u32[]{:S(2)}, u32[]{:S(2)}) collective-permute-start(bf16[96,256]{1,0:T(8,128)(2,1)S(1)} %get-tuple-element.37), channel_id=1, source_target_pairs={{64,0},{1,1},{65,2},{4,3},{68,4},{5,5},{69,6},{8,7},{72,8},{9,9},{... | collective-permute-start | bytes 147464 | tf_op jit(solution)/shard_map/ppermute | solution.py:402
  144.0 5.6 %collective-permute-start.18 = (bf16[96,256]{1,0:T(8,128)(2,1)S(1)}, bf16[96,256]{1,0:T(8,128)(2,1)S(1)}, u32[]{:S(2)}, u32[]{:S(2)}) collective-permute-start(bf16[96,256]{1,0:T(8,128)(2,1)S(1)} %get-tuple-element.38), channel_id=1, source_target_pairs={{1,0},{65,1},{0,2},{68,3},{5,4},{69,5},{4,6},{72,7},{9,8},{73,9},{... | collective-permute-start | bytes 147464 | tf_op jit(solution)/shard_map/ppermute | solution.py:402
  149.7 2.9 %collective-permute-start.19 = (bf16[96,256]{1,0:T(8,128)(2,1)S(1)}, bf16[96,256]{1,0:T(8,128)(2,1)S(1)}, u32[]{:S(2)}, u32[]{:S(2)}) collective-permute-start(bf16[96,256]{1,0:T(8,128)(2,1)S(1)} %get-tuple-element.39), channel_id=1, source_target_pairs={{65,0},{0,1},{64,2},{5,3},{69,4},{4,5},{68,6},{9,7},{73,8},{8,9},{... | collective-permute-start | bytes 147464 | tf_op jit(solution)/shard_map/ppermute | solution.py:402
  152.6 2.7 %collective-permute-start.20 = (bf16[96,256]{1,0:T(8,128)(2,1)S(1)}, bf16[96,256]{1,0:T(8,128)(2,1)S(1)}, u32[]{:S(2)}, u32[]{:S(2)}) collective-permute-start(bf16[96,256]{1,0:T(8,128)(2,1)S(1)} %get-tuple-element.40), channel_id=1, source_target_pairs={{0,0},{64,1},{1,2},{69,3},{4,4},{68,5},{5,6},{73,7},{8,8},{72,9},{... | collective-permute-start | bytes 147464 | tf_op jit(solution)/shard_map/ppermute | solution.py:402
  155.3 1.1 all-to-all-done.1
  156.4 1.5 reduce_sum.12
  158.0 4.4 %collective-permute-start.21 = (bf16[12,1728]{1,0:T(8,128)(2,1)S(1)}, bf16[12,1728]{1,0:T(8,128)(2,1)S(1)}, u32[]{:S(2)}, u32[]{:S(2)}) collective-permute-start(bf16[12,1728]{1,0:T(8,128)(2,1)S(1)} %get-tuple-element.50), channel_id=1, source_target_pairs={{1,0},{0,1},{5,2},{4,3},{9,4},{8,5},{13,6},{12,7},{65,8},{64,9},{6... | collective-permute-start | bytes 124424 | tf_op jit(solution)/shard_map/ppermute | solution.py:412
  162.4 5.4 %collective-permute-start.22 = (bf16[12,1728]{1,0:T(8,128)(2,1)S(1)}, bf16[12,1728]{1,0:T(8,128)(2,1)S(1)}, u32[]{:S(2)}, u32[]{:S(2)}) collective-permute-start(bf16[12,1728]{1,0:T(8,128)(2,1)S(1)} %get-tuple-element.51), channel_id=1, source_target_pairs={{0,0},{1,1},{4,2},{5,3},{8,4},{9,5},{12,6},{13,7},{64,8},{65,9},{6... | collective-permute-start | bytes 124424 | tf_op jit(solution)/shard_map/ppermute | solution.py:411
  167.8 1.4 shard_map.57
  170.9 0.7 select_convert_fusion
  (49 shorter events, 5.9 us)
Async XLA Ops:
  2.7 10.2 %collective-permute-start.6 = (bf16[12,1728]{1,0:T(8,128)(2,1)S(1)}, bf16[12,1728]{1,0:T(8,128)(2,1)S(1)}, u32[]{:S(2)}, u32[]{:S(2)}) collective-permute-start(bf16[12,1728]{1,0:T(8,128)(2,1)S(1)} %select_n.110), channel_id=1, source_target_pairs={{0,0},{1,1},{2,4},{3,5},{4,8},{5,9},{6,12},{7,13},{8,64},{9,65},{1... | collective-permute-start | bytes 124424 | tf_op jit(solution)/shard_map/ppermute | solution.py:347
  9.0 6.4 %collective-permute-start.5 = (bf16[12,1728]{1,0:T(8,128)(2,1)S(1)}, bf16[12,1728]{1,0:T(8,128)(2,1)S(1)}, u32[]{:S(2)}, u32[]{:S(2)}) collective-permute-start(bf16[12,1728]{1,0:T(8,128)(2,1)S(1)} %select_n.108), channel_id=1, source_target_pairs={{0,1},{1,0},{2,5},{3,4},{4,9},{5,8},{6,13},{7,12},{8,65},{9,64},{1... | collective-permute-start | bytes 124424 | tf_op jit(solution)/shard_map/ppermute | solution.py:348
  16.7 11.9 %copy-start.5 = (bf16[256,384]{1,0:T(8,128)(2,1)S(1)}, bf16[256,384]{1,0:T(8,128)(2,1)}, u32[]{:S(2)}) copy-start(bf16[256,384]{1,0:T(8,128)(2,1)} %param.3) | copy-start | bytes 589828
  16.7 12.0 %copy-start.4 = (s32[2,2]{1,0:T(2,128)S(1)}, s32[2,2]{1,0:T(2,128)}, u32[]{:S(2)}) copy-start(s32[2,2]{1,0:T(2,128)} %param.5) | copy-start | bytes 52
  16.7 81.4 %all-to-all-start = ((bf16[16,24,1728]{2,1,0:T(8,128)(2,1)}), bf16[16,24,1728]{2,1,0:T(8,128)(2,1)S(1)}, u32[]{:S(2)}, u32[]{:S(2)}) async-start(bf16[16,24,1728]{2,1,0:T(8,128)(2,1)} %broadcast_in_dim.3), calls=%async_computation | async-start | bytes 2752512 | tf_op jit(solution)/shard_map/all_to_all | solution.py:353
  28.6 36.1 %collective-permute-start = (bf16[256,384]{1,0:T(8,128)(2,1)S(1)}, bf16[256,384]{1,0:T(8,128)(2,1)S(1)}, u32[]{:S(2)}, u32[]{:S(2)}) collective-permute-start(bf16[256,384]{1,0:T(8,128)(2,1)S(1)} %copy-done.5), channel_id=1, source_target_pairs={{0,1},{1,2},{2,3},{3,4},{4,5},{5,6},{6,7},{7,8},{8,9},{9,10},{10,1... | collective-permute-start | bytes 589832 | tf_op jit(solution)/shard_map/ppermute | solution.py:355
  65.4 8.9 %collective-permute-start.1 = (bf16[96,256]{1,0:T(8,128)(2,1)S(1)}, bf16[96,256]{1,0:T(8,128)(2,1)S(1)}, u32[]{:S(2)}, u32[]{:S(2)}) collective-permute-start(bf16[96,256]{1,0:T(8,128)(2,1)S(1)} %get-tuple-element.22), channel_id=1, source_target_pairs={{0,0},{1,64},{2,1},{3,65},{4,4},{5,68},{6,5},{7,69},{8,8},{9,72},{... | collective-permute-start | bytes 147464 | tf_op jit(solution)/shard_map/ppermute | solution.py:359
  67.3 7.0 %collective-permute-start.2 = (bf16[96,256]{1,0:T(8,128)(2,1)S(1)}, bf16[96,256]{1,0:T(8,128)(2,1)S(1)}, u32[]{:S(2)}, u32[]{:S(2)}) collective-permute-start(bf16[96,256]{1,0:T(8,128)(2,1)S(1)} %get-tuple-element.23), channel_id=1, source_target_pairs={{0,64},{1,1},{2,65},{3,0},{4,68},{5,5},{6,69},{7,4},{8,72},{9,9},{... | collective-permute-start | bytes 147464 | tf_op jit(solution)/shard_map/ppermute | solution.py:359
  69.2 5.9 %collective-permute-start.3 = (bf16[96,256]{1,0:T(8,128)(2,1)S(1)}, bf16[96,256]{1,0:T(8,128)(2,1)S(1)}, u32[]{:S(2)}, u32[]{:S(2)}) collective-permute-start(bf16[96,256]{1,0:T(8,128)(2,1)S(1)} %get-tuple-element.24), channel_id=1, source_target_pairs={{0,1},{1,65},{2,0},{3,64},{4,5},{5,69},{6,4},{7,68},{8,9},{9,73},{... | collective-permute-start | bytes 147464 | tf_op jit(solution)/shard_map/ppermute | solution.py:359
  72.4 6.9 %collective-permute-start.4 = (bf16[96,256]{1,0:T(8,128)(2,1)S(1)}, bf16[96,256]{1,0:T(8,128)(2,1)S(1)}, u32[]{:S(2)}, u32[]{:S(2)}) collective-permute-start(bf16[96,256]{1,0:T(8,128)(2,1)S(1)} %get-tuple-element.25), channel_id=1, source_target_pairs={{0,65},{1,0},{2,64},{3,1},{4,69},{5,4},{6,68},{7,5},{8,73},{9,8},{... | collective-permute-start | bytes 147464 | tf_op jit(solution)/shard_map/ppermute | solution.py:359
  80.1 9.2 %collective-permute-start.7 = (bf16[96,1024]{1,0:T(8,128)(2,1)S(1)}, bf16[96,1024]{1,0:T(8,128)(2,1)S(1)}, u32[]{:S(2)}, u32[]{:S(2)}) collective-permute-start(bf16[96,1024]{1,0:T(8,128)(2,1)S(1)} %get-tuple-element.26.x), channel_id=1, source_target_pairs={{0,128},{128,0},{1,129},{129,1},{2,130},{130,2},{3,131},{131,3},{4... | collective-permute-start | bytes 589832 | tf_op jit(solution)/shard_map/ppermute | solution.py:70
  85.8 6.9 %collective-permute-start.10 = (bf16[96,1024]{1,0:T(8,128)(2,1)S(1)}, bf16[96,1024]{1,0:T(8,128)(2,1)S(1)}, u32[]{:S(2)}, u32[]{:S(2)}) collective-permute-start(bf16[96,1024]{1,0:T(8,128)(2,1)S(1)} %get-tuple-element.27.a0), channel_id=1, source_target_pairs={{0,3},{1,0},{2,1},{3,2},{4,7},{5,4},{6,5},{7,6},{8,11},{9,8},{10,9... | collective-permute-start | bytes 589832 | tf_op jit(solution)/shard_map/ppermute | solution.py:74
  85.8 8.1 %collective-permute-start.9 = (bf16[96,1024]{1,0:T(8,128)(2,1)S(1)}, bf16[96,1024]{1,0:T(8,128)(2,1)S(1)}, u32[]{:S(2)}, u32[]{:S(2)}) collective-permute-start(bf16[96,1024]{1,0:T(8,128)(2,1)S(1)} %get-tuple-element.27.a0), channel_id=1, source_target_pairs={{0,2},{1,3},{2,0},{3,1},{4,6},{5,7},{6,4},{7,5},{8,10},{9,11},{10,... | collective-permute-start | bytes 589832 | tf_op jit(solution)/shard_map/ppermute | solution.py:74
  85.8 11.6 %collective-permute-start.8 = (bf16[96,1024]{1,0:T(8,128)(2,1)S(1)}, bf16[96,1024]{1,0:T(8,128)(2,1)S(1)}, u32[]{:S(2)}, u32[]{:S(2)}) collective-permute-start(bf16[96,1024]{1,0:T(8,128)(2,1)S(1)} %get-tuple-element.27.a0), channel_id=1, source_target_pairs={{0,1},{1,2},{2,3},{3,0},{4,5},{5,6},{6,7},{7,4},{8,9},{9,10},{10,1... | collective-permute-start | bytes 589832 | tf_op jit(solution)/shard_map/ppermute | solution.py:74
  93.9 0.7 copy-start
  97.3 0.7 copy-start.2
  98.0 0.9 copy-start.1
  99.0 0.9 copy-start.3
  103.1 1.9 %collective-permute-start.11 = (f32[96,1024]{1,0:T(8,128)S(1)}, f32[96,1024]{1,0:T(8,128)S(1)}, u32[]{:S(2)}, u32[]{:S(2)}) collective-permute-start(f32[96,1024]{1,0:T(8,128)S(1)} %get-tuple-element.29), channel_id=1, source_target_pairs={{0,64},{64,0},{1,65},{65,1},{2,66},{66,2},{3,67},{67,3},{4,68},{68... | collective-permute-start | bytes 1179656 | tf_op jit(solution)/shard_map/ppermute | solution.py:70
  105.7 7.9 %collective-permute-start.12 = (bf16[96,1024]{1,0:T(8,128)(2,1)S(1)}, bf16[96,1024]{1,0:T(8,128)(2,1)S(1)}, u32[]{:S(2)}, u32[]{:S(2)}) collective-permute-start(bf16[96,1024]{1,0:T(8,128)(2,1)S(1)} %shard_map.53.mine), channel_id=1, source_target_pairs={{0,128},{128,0},{1,129},{129,1},{2,130},{130,2},{3,131},{131,3},{4... | collective-permute-start | bytes 589832 | tf_op jit(solution)/shard_map/ppermute | solution.py:70
  114.7 2.4 %collective-permute-start.13 = (bf16[96,1024]{1,0:T(8,128)(2,1)S(1)}, bf16[96,1024]{1,0:T(8,128)(2,1)S(1)}, u32[]{:S(2)}, u32[]{:S(2)}) collective-permute-start(bf16[96,1024]{1,0:T(8,128)(2,1)S(1)} %get-tuple-element.32.b_own), channel_id=1, source_target_pairs={{0,64},{64,0},{1,65},{65,1},{2,66},{66,2},{3,67},{67,3},{4,68},{68... | collective-permute-start | bytes 589832 | tf_op jit(solution)/shard_map/ppermute | solution.py:70
  120.6 35.8 %all-to-all-start.1 = ((bf16[16,24,1728]{2,1,0:T(8,128)(2,1)}), bf16[16,24,1728]{2,1,0:T(8,128)(2,1)}, u32[]{:S(2)}, u32[]{:S(2)}) async-start(bf16[16,24,1728]{2,1,0:T(8,128)(2,1)} %bitcast.6), calls=%async_computation.1 | async-start | bytes 2752512 | tf_op jit(solution)/shard_map/all_to_all | solution.py:407
  127.4 7.9 %collective-permute-start.14 = (bf16[96,1024]{1,0:T(8,128)(2,1)S(1)}, bf16[96,1024]{1,0:T(8,128)(2,1)S(1)}, u32[]{:S(2)}, u32[]{:S(2)}) collective-permute-start(bf16[96,1024]{1,0:T(8,128)(2,1)S(1)} %get-tuple-element.34), channel_id=1, source_target_pairs={{0,1},{1,2},{2,3},{3,0},{4,5},{5,6},{6,7},{7,4},{8,9},{9,10},{10,1... | collective-permute-start | bytes 589832 | tf_op jit(solution)/shard_map/ppermute | solution.py:74
  127.5 10.9 %collective-permute-start.15 = (bf16[96,1024]{1,0:T(8,128)(2,1)S(1)}, bf16[96,1024]{1,0:T(8,128)(2,1)S(1)}, u32[]{:S(2)}, u32[]{:S(2)}) collective-permute-start(bf16[96,1024]{1,0:T(8,128)(2,1)S(1)} %get-tuple-element.35), channel_id=1, source_target_pairs={{0,2},{1,3},{2,0},{3,1},{4,6},{5,7},{6,4},{7,5},{8,10},{9,11},{10,... | collective-permute-start | bytes 589832 | tf_op jit(solution)/shard_map/ppermute | solution.py:74
  129.5 9.7 %collective-permute-start.16 = (bf16[96,1024]{1,0:T(8,128)(2,1)S(1)}, bf16[96,1024]{1,0:T(8,128)(2,1)S(1)}, u32[]{:S(2)}, u32[]{:S(2)}) collective-permute-start(bf16[96,1024]{1,0:T(8,128)(2,1)S(1)} %get-tuple-element.36), channel_id=1, source_target_pairs={{0,3},{1,0},{2,1},{3,2},{4,7},{5,4},{6,5},{7,6},{8,11},{9,8},{10,9... | collective-permute-start | bytes 589832 | tf_op jit(solution)/shard_map/ppermute | solution.py:74
  140.6 21.9 %collective-permute-start.17 = (bf16[96,256]{1,0:T(8,128)(2,1)S(1)}, bf16[96,256]{1,0:T(8,128)(2,1)S(1)}, u32[]{:S(2)}, u32[]{:S(2)}) collective-permute-start(bf16[96,256]{1,0:T(8,128)(2,1)S(1)} %get-tuple-element.37), channel_id=1, source_target_pairs={{64,0},{1,1},{65,2},{4,3},{68,4},{5,5},{69,6},{8,7},{72,8},{9,9},{... | collective-permute-start | bytes 147464 | tf_op jit(solution)/shard_map/ppermute | solution.py:402
  144.0 23.8 %collective-permute-start.18 = (bf16[96,256]{1,0:T(8,128)(2,1)S(1)}, bf16[96,256]{1,0:T(8,128)(2,1)S(1)}, u32[]{:S(2)}, u32[]{:S(2)}) collective-permute-start(bf16[96,256]{1,0:T(8,128)(2,1)S(1)} %get-tuple-element.38), channel_id=1, source_target_pairs={{1,0},{65,1},{0,2},{68,3},{5,4},{69,5},{4,6},{72,7},{9,8},{73,9},{... | collective-permute-start | bytes 147464 | tf_op jit(solution)/shard_map/ppermute | solution.py:402
  149.7 18.1 %collective-permute-start.19 = (bf16[96,256]{1,0:T(8,128)(2,1)S(1)}, bf16[96,256]{1,0:T(8,128)(2,1)S(1)}, u32[]{:S(2)}, u32[]{:S(2)}) collective-permute-start(bf16[96,256]{1,0:T(8,128)(2,1)S(1)} %get-tuple-element.39), channel_id=1, source_target_pairs={{65,0},{0,1},{64,2},{5,3},{69,4},{4,5},{68,6},{9,7},{73,8},{8,9},{... | collective-permute-start | bytes 147464 | tf_op jit(solution)/shard_map/ppermute | solution.py:402
  152.6 15.2 %collective-permute-start.20 = (bf16[96,256]{1,0:T(8,128)(2,1)S(1)}, bf16[96,256]{1,0:T(8,128)(2,1)S(1)}, u32[]{:S(2)}, u32[]{:S(2)}) collective-permute-start(bf16[96,256]{1,0:T(8,128)(2,1)S(1)} %get-tuple-element.40), channel_id=1, source_target_pairs={{0,0},{64,1},{1,2},{69,3},{4,4},{68,5},{5,6},{73,7},{8,8},{72,9},{... | collective-permute-start | bytes 147464 | tf_op jit(solution)/shard_map/ppermute | solution.py:402
  158.0 11.2 %collective-permute-start.21 = (bf16[12,1728]{1,0:T(8,128)(2,1)S(1)}, bf16[12,1728]{1,0:T(8,128)(2,1)S(1)}, u32[]{:S(2)}, u32[]{:S(2)}) collective-permute-start(bf16[12,1728]{1,0:T(8,128)(2,1)S(1)} %get-tuple-element.50), channel_id=1, source_target_pairs={{1,0},{0,1},{5,2},{4,3},{9,4},{8,5},{13,6},{12,7},{65,8},{64,9},{6... | collective-permute-start | bytes 124424 | tf_op jit(solution)/shard_map/ppermute | solution.py:412
  162.4 7.1 %collective-permute-start.22 = (bf16[12,1728]{1,0:T(8,128)(2,1)S(1)}, bf16[12,1728]{1,0:T(8,128)(2,1)S(1)}, u32[]{:S(2)}, u32[]{:S(2)}) collective-permute-start(bf16[12,1728]{1,0:T(8,128)(2,1)S(1)} %get-tuple-element.51), channel_id=1, source_target_pairs={{0,0},{1,1},{4,2},{5,3},{8,4},{9,5},{12,6},{13,7},{64,8},{65,9},{6... | collective-permute-start | bytes 124424 | tf_op jit(solution)/shard_map/ppermute | solution.py:411

commit v3 on v2

--- a/solution.py
+++ b/solution.py
@@ -192,7 +192,7 @@
         yield k, rows(2 * plane + xl, 24)
 
 
-def first_kernel(prm, w, g, a0, a1, a2, a3, full, keep, send, sorted_w, d_ref, res):
+def first_kernel(prm, w, a0, a1, a2, a3, full, keep, send, sorted_w, d_ref, res):
     gather_chunks(prm, a0, (a1, a2, a3), full)
 
     @pl.when(prm[0] == 0)
@@ -273,7 +273,7 @@
                     dw[place, :] = part[m % 8 * 24 : (m % 8 + 1) * 24, :].astype(BF16)
 
 
-def second_kernel(prm, w, sorted_w, b_own, b_other, keep, s1, s2, s3, pair, d_ref, res):
+def second_kernel(prm, w, b_own, b_other, keep, s1, s2, s3, sorted_w, pair, d_ref, res):
     pair_up(prm, b_own, b_other, pair)
 
     @pl.when(prm[0] == 0)
@@ -283,6 +283,8 @@
 
     @pl.when(prm[0] == 1)
     def _():
+        for k, place in parts_in_order(prm):
+            sorted_w[k * 24 : (k + 1) * 24, :] = w[place, :]
         for k in range(2):
             res[k * PAIR : (k + 1) * PAIR, :] = convolve(
                 sorted_w[k * PAIR : (k + 1) * PAIR, :], pair[...]
@@ -361,13 +363,12 @@
     others = [turn_y(a, d) for d in (1, 2, 3)]
     g = swap(x, "xh")
 
-    full, keep, send, sorted_w = call(
+    full, keep, send = call(
         first_kernel,
-        [((QUAD, PIX), BF16), own32, own32, ((QUAD, LANES), BF16)],
-        [((LANES, PIX), BF16), ((PAIR, PIX), F32)],
+        [((QUAD, PIX), BF16), own32, own32],
+        [((QUAD, LANES), BF16), ((LANES, PIX), BF16), ((PAIR, PIX), F32)],
         prm,
         w,
-        g,
         a,
         *others,
         grant=24,
@@ -389,10 +390,14 @@
     keep, *sends = call(
         second_kernel,
         [own32, own, own, own],
-        [((PAIR, PIX), BF16), ((LANES, PIX), BF16), ((QUAD, PIX), F32)],
+        [
+            ((QUAD, LANES), BF16),
+            ((PAIR, PIX), BF16),
+            ((LANES, PIX), BF16),
+            ((QUAD, PIX), F32),
+        ],
         prm,
         w,
-        sorted_w,
         b,
         b_other,
         grant=24,

time: 175 us -> 173 us (0.989)
  the two profiles are of different devices: /device:TPU:1 before, /device:TPU:21 now
where the time goes in v3:
time: 173 us; the launch traced here: 172 us
  waiting for transfers between devices  73.6 us (43%)
  starting transfers between devices  73.3 us (42%)
  Pallas kernels  17.2 us (10%)
  local copies, waits for them, and re-layouts  4.21 us (2%)
  other arithmetic  2.78 us (2%)
    ppermute x4, waiting for transfers between devices, step(): lax.ppermute(b, AX, pixel_pairs(v, 0))  30.6 us
    ppermute x6, waiting for transfers between devices, turn_y(): return lax.ppermute(value, 'y', [(i, (i + d) % 4) for i in range(4)])  17.8 us
    pallas_call x9, Pallas kernels, call(): pl.pallas_call(kernel, out_shape=[jax.ShapeDtypeStruct(s, d) for s, d in...  17.2 us
    ppermute x4, starting transfers between devices, step(): lax.ppermute(b, AX, back(pixel_pairs(v, 1)))  14.5 us
    ppermute x6, starting transfers between devices, turn_y(): return lax.ppermute(value, 'y', [(i, (i + d) % 4) for i in range(4)])  13.2 us
    ppermute x4, waiting for transfers between devices, swap(): return lax.ppermute(value, axis, [(0, 1), (1, 0)])  10.8 us
    ppermute x1, starting transfers between devices, step(): lax.ppermute(jnp.where(odd, low, high), AX, weight_pairs(1))  8.15 us
    ppermute x4, starting transfers between devices, step(): lax.ppermute(b, AX, pixel_pairs(v, 0))  7.89 us
  transfers between devices with their start and end apart: 25, of which 13 were waited for; matrix products, arithmetic and copies ran while one was open for 1% of the time, Pallas kernels for 5%

profile of v3, /device:TPU:21, one launch (start us, length us, event | category | flops | bytes accessed | tf_op | source)
XLA Modules:
  0.0 172.1 jit_solution(17926077524579783531)
XLA Ops:
  0.6 1.0 reshape.37
  2.7 8.1 %collective-permute-start.5 = (bf16[12,1728]{1,0:T(8,128)(2,1)S(1)}, bf16[12,1728]{1,0:T(8,128)(2,1)S(1)}, u32[]{:S(2)}, u32[]{:S(2)}) collective-permute-start(bf16[12,1728]{1,0:T(8,128)(2,1)S(1)} %select_n.108), channel_id=1, source_target_pairs={{0,1},{1,0},{2,5},{3,4},{4,9},{5,8},{6,13},{7,12},{8,65},{9,64},{1... | collective-permute-start | bytes 124424 | tf_op jit(solution)/shard_map/ppermute | solution.py:350
  10.9 5.1 %collective-permute-start.6 = (bf16[12,1728]{1,0:T(8,128)(2,1)S(1)}, bf16[12,1728]{1,0:T(8,128)(2,1)S(1)}, u32[]{:S(2)}, u32[]{:S(2)}) collective-permute-start(bf16[12,1728]{1,0:T(8,128)(2,1)S(1)} %select_n.110), channel_id=1, source_target_pairs={{0,0},{1,1},{2,4},{3,5},{4,8},{5,9},{6,12},{7,13},{8,64},{9,65},{1... | collective-permute-start | bytes 124424 | tf_op jit(solution)/shard_map/ppermute | solution.py:349
  16.1 3.7 %collective-permute-done.6 = bf16[12,1728]{1,0:T(8,128)(2,1)S(1)} collective-permute-done((bf16[12,1728]{1,0:T(8,128)(2,1)S(1)}, bf16[12,1728]{1,0:T(8,128)(2,1)S(1)}, u32[]{:S(2)}, u32[]{:S(2)}) %collective-permute-start.6) | collective-permute-done | bytes 41504 | tf_op jit(solution)/shard_map/ppermute | solution.py:349
  19.9 1.2 broadcast_in_dim.3
  21.1 3.8 %all-to-all-start = ((bf16[16,24,1728]{2,1,0:T(8,128)(2,1)}), bf16[16,24,1728]{2,1,0:T(8,128)(2,1)S(1)}, u32[]{:S(2)}, u32[]{:S(2)}) async-start(bf16[16,24,1728]{2,1,0:T(8,128)(2,1)} %broadcast_in_dim.3), calls=%async_computation | async-start | bytes 2752512 | tf_op jit(solution)/shard_map/all_to_all | solution.py:355
  24.9 1.8 %collective-permute-start = (bf16[256,384]{1,0:T(8,128)(2,1)S(1)}, bf16[256,384]{1,0:T(8,128)(2,1)S(1)}, u32[]{:S(2)}, u32[]{:S(2)}) collective-permute-start(bf16[256,384]{1,0:T(8,128)(2,1)S(1)} %copy-done.1), channel_id=1, source_target_pairs={{0,1},{1,2},{2,3},{3,4},{4,5},{5,6},{6,7},{7,8},{8,9},{9,10},{10,1... | collective-permute-start | bytes 589832 | tf_op jit(solution)/shard_map/ppermute | solution.py:357
  26.9 5.8 %collective-permute-done.x_ref = bf16[256,384]{1,0:T(8,128)(2,1)S(1)} collective-permute-done((bf16[256,384]{1,0:T(8,128)(2,1)S(1)}, bf16[256,384]{1,0:T(8,128)(2,1)S(1)}, u32[]{:S(2)}, u32[]{:S(2)}) %collective-permute-start) | collective-permute-done | bytes 196640 | tf_op jit(solution)/shard_map/ppermute | solution.py:357
  32.7 0.7 shard_map.50
  33.4 5.2 %collective-permute-start.1 = (bf16[96,256]{1,0:T(8,128)(2,1)S(1)}, bf16[96,256]{1,0:T(8,128)(2,1)S(1)}, u32[]{:S(2)}, u32[]{:S(2)}) collective-permute-start(bf16[96,256]{1,0:T(8,128)(2,1)S(1)} %get-tuple-element.21), channel_id=1, source_target_pairs={{0,0},{1,64},{2,1},{3,65},{4,4},{5,68},{6,5},{7,69},{8,8},{9,72},{... | collective-permute-start | bytes 147464 | tf_op jit(solution)/shard_map/ppermute | solution.py:361
  38.6 1.9 %collective-permute-start.2 = (bf16[96,256]{1,0:T(8,128)(2,1)S(1)}, bf16[96,256]{1,0:T(8,128)(2,1)S(1)}, u32[]{:S(2)}, u32[]{:S(2)}) collective-permute-start(bf16[96,256]{1,0:T(8,128)(2,1)S(1)} %get-tuple-element.22), channel_id=1, source_target_pairs={{0,64},{1,1},{2,65},{3,0},{4,68},{5,5},{6,69},{7,4},{8,72},{9,9},{... | collective-permute-start | bytes 147464 | tf_op jit(solution)/shard_map/ppermute | solution.py:361
  40.6 0.7 collective-permute-start.4
  41.3 30.6 %collective-permute-done.2.refs_1_ = bf16[96,256]{1,0:T(8,128)(2,1)S(1)} collective-permute-done((bf16[96,256]{1,0:T(8,128)(2,1)S(1)}, bf16[96,256]{1,0:T(8,128)(2,1)S(1)}, u32[]{:S(2)}, u32[]{:S(2)}) %collective-permute-start.2) | collective-permute-done | bytes 49184 | tf_op jit(solution)/shard_map/ppermute | solution.py:361
  71.9 0.8 shard_map.51
  72.8 6.0 %collective-permute-start.7 = (bf16[96,1024]{1,0:T(8,128)(2,1)S(1)}, bf16[96,1024]{1,0:T(8,128)(2,1)S(1)}, u32[]{:S(2)}, u32[]{:S(2)}) collective-permute-start(bf16[96,1024]{1,0:T(8,128)(2,1)S(1)} %get-tuple-element.26.a0), channel_id=1, source_target_pairs={{0,1},{1,2},{2,3},{3,0},{4,5},{5,6},{6,7},{7,4},{8,9},{9,10},{10,1... | collective-permute-start | bytes 589832 | tf_op jit(solution)/shard_map/ppermute | solution.py:74
  78.8 2.7 %collective-permute-start.8 = (bf16[96,1024]{1,0:T(8,128)(2,1)S(1)}, bf16[96,1024]{1,0:T(8,128)(2,1)S(1)}, u32[]{:S(2)}, u32[]{:S(2)}) collective-permute-start(bf16[96,1024]{1,0:T(8,128)(2,1)S(1)} %get-tuple-element.26.a0), channel_id=1, source_target_pairs={{0,2},{1,3},{2,0},{3,1},{4,6},{5,7},{6,4},{7,5},{8,10},{9,11},{10,... | collective-permute-start | bytes 589832 | tf_op jit(solution)/shard_map/ppermute | solution.py:74
  81.5 2.0 %collective-permute-start.9 = (bf16[96,1024]{1,0:T(8,128)(2,1)S(1)}, bf16[96,1024]{1,0:T(8,128)(2,1)S(1)}, u32[]{:S(2)}, u32[]{:S(2)}) collective-permute-start(bf16[96,1024]{1,0:T(8,128)(2,1)S(1)} %get-tuple-element.26.a0), channel_id=1, source_target_pairs={{0,3},{1,0},{2,1},{3,2},{4,7},{5,4},{6,5},{7,6},{8,11},{9,8},{10,9... | collective-permute-start | bytes 589832 | tf_op jit(solution)/shard_map/ppermute | solution.py:74
  83.5 5.9 %collective-permute-done.8.a2 = bf16[96,1024]{1,0:T(8,128)(2,1)S(1)} collective-permute-done((bf16[96,1024]{1,0:T(8,128)(2,1)S(1)}, bf16[96,1024]{1,0:T(8,128)(2,1)S(1)}, u32[]{:S(2)}, u32[]{:S(2)}) %collective-permute-start.8) | collective-permute-done | bytes 196640 | tf_op jit(solution)/shard_map/ppermute | solution.py:74
  89.4 2.4 %collective-permute-done.9.a3 = bf16[96,1024]{1,0:T(8,128)(2,1)S(1)} collective-permute-done((bf16[96,1024]{1,0:T(8,128)(2,1)S(1)}, bf16[96,1024]{1,0:T(8,128)(2,1)S(1)}, u32[]{:S(2)}, u32[]{:S(2)}) %collective-permute-start.9) | collective-permute-done | bytes 196640 | tf_op jit(solution)/shard_map/ppermute | solution.py:74
  91.8 2.8 %shard_map.52 = (bf16[384,1024]{1,0:T(8,128)(2,1)S(1)}, f32[96,1024]{1,0:T(8,128)S(1)}, f32[96,1024]{1,0:T(8,128)S(1)}) custom-call(s32[6]{0:T(128)S(1)} %stack.22.prm, bf16[384,1728]{1,0:T(8,128)(2,1)S(1)} %bitcast.14, bf16[96,1024]{1,0:T(8,128)(2,1)S(1)} %get-tuple-element.26.a0, bf16[96,1024]{1,0:T(8,128)(2,1)S(1)} %collective-permute-done.7.a1, ...), custom_call_target="tpu_custom_call" | custom-call | tf_op jit(solution)/shard_map/pallas_call | solution.py:324
  94.6 0.7 collective-permute-start.10
  95.3 1.3 collective-permute-done.10.got
  96.7 0.6 shard_map.53.mine
  97.3 1.7 collective-permute-start.11
  99.1 4.2 %collective-permute-done.12.g = bf16[96,1024]{1,0:T(8,128)(2,1)S(1)} collective-permute-done((bf16[96,1024]{1,0:T(8,128)(2,1)S(1)}, bf16[96,1024]{1,0:T(8,128)(2,1)S(1)}, u32[]{:S(2)}, u32[]{:S(2)}) %collective-permute-start.12) | collective-permute-done | bytes 196640 | tf_op jit(solution)/shard_map/ppermute | solution.py:70
  103.2 4.2 %collective-permute-done.11.theirs = bf16[96,1024]{1,0:T(8,128)(2,1)S(1)} collective-permute-done((bf16[96,1024]{1,0:T(8,128)(2,1)S(1)}, bf16[96,1024]{1,0:T(8,128)(2,1)S(1)}, u32[]{:S(2)}, u32[]{:S(2)}) %collective-permute-start.11) | collective-permute-done | bytes 196640 | tf_op jit(solution)/shard_map/ppermute | solution.py:70
  107.4 1.0 shard_map.54
  108.5 1.0 collective-permute-start.13
  109.5 1.1 collective-permute-done.13.b_other
  110.6 4.2 %shard_map.58 = bf16[384,1728]{1,0:T(8,128)(2,1)} custom-call(s32[6]{0:T(128)S(1)} %stack.22.prm, bf16[384,1024]{1,0:T(8,128)(2,1)S(1)} %get-tuple-element.39.full, bf16[96,1024]{1,0:T(8,128)(2,1)S(1)} %get-tuple-element.30.b_own, bf16[96,1024]{1,0:T(8,128)(2,1)S(1)} %collective-permute-done.13.b_other), custom_call_target="tpu_custom_call" | custom-call | tf_op jit(solution)/shard_map/pallas_call | solution.py:324
  114.8 4.4 %all-to-all-start.1 = ((bf16[16,24,1728]{2,1,0:T(8,128)(2,1)}), bf16[16,24,1728]{2,1,0:T(8,128)(2,1)}, u32[]{:S(2)}, u32[]{:S(2)}) async-start(bf16[16,24,1728]{2,1,0:T(8,128)(2,1)} %bitcast.6), calls=%async_computation.1 | async-start | bytes 2752512 | tf_op jit(solution)/shard_map/all_to_all | solution.py:412
  119.2 4.8 %shard_map.55 = (f32[96,1024]{1,0:T(8,128)S(1)}, bf16[96,1024]{1,0:T(8,128)(2,1)S(1)}, bf16[96,1024]{1,0:T(8,128)(2,1)S(1)}, bf16[96,1024]{1,0:T(8,128)(2,1)S(1)}) custom-call(s32[6]{0:T(128)S(1)} %stack.22.prm, bf16[384,1728]{1,0:T(8,128)(2,1)S(1)} %bitcast.15, bf16[96,1024]{1,0:T(8,128)(2,1)S(1)} %get-tuple-element.30.b_own, ...), custom_call_target="tpu_custom_call" | custom-call | tf_op jit(solution)/shard_map/pallas_call | solution.py:324
  124.0 1.2 collective-permute-start.14
  125.2 1.0 collective-permute-start.15
  126.4 3.6 %collective-permute-done.14.r1 = bf16[96,1024]{1,0:T(8,128)(2,1)S(1)} collective-permute-done((bf16[96,1024]{1,0:T(8,128)(2,1)S(1)}, bf16[96,1024]{1,0:T(8,128)(2,1)S(1)}, u32[]{:S(2)}, u32[]{:S(2)}) %collective-permute-start.14) | collective-permute-done | bytes 196640 | tf_op jit(solution)/shard_map/ppermute | solution.py:74
  130.1 4.8 %collective-permute-done.15.r2 = bf16[96,1024]{1,0:T(8,128)(2,1)S(1)} collective-permute-done((bf16[96,1024]{1,0:T(8,128)(2,1)S(1)}, bf16[96,1024]{1,0:T(8,128)(2,1)S(1)}, u32[]{:S(2)}, u32[]{:S(2)}) %collective-permute-start.15) | collective-permute-done | bytes 196640 | tf_op jit(solution)/shard_map/ppermute | solution.py:74
  134.9 1.0 collective-permute-done.16.r3
  135.9 0.8 shard_map.56
  136.7 2.8 %collective-permute-start.17 = (bf16[96,256]{1,0:T(8,128)(2,1)S(1)}, bf16[96,256]{1,0:T(8,128)(2,1)S(1)}, u32[]{:S(2)}, u32[]{:S(2)}) collective-permute-start(bf16[96,256]{1,0:T(8,128)(2,1)S(1)} %get-tuple-element.35), channel_id=1, source_target_pairs={{64,0},{1,1},{65,2},{4,3},{68,4},{5,5},{69,6},{8,7},{72,8},{9,9},{... | collective-permute-start | bytes 147464 | tf_op jit(solution)/shard_map/ppermute | solution.py:407
  139.5 4.1 %collective-permute-start.18 = (bf16[96,256]{1,0:T(8,128)(2,1)S(1)}, bf16[96,256]{1,0:T(8,128)(2,1)S(1)}, u32[]{:S(2)}, u32[]{:S(2)}) collective-permute-start(bf16[96,256]{1,0:T(8,128)(2,1)S(1)} %get-tuple-element.36), channel_id=1, source_target_pairs={{1,0},{65,1},{0,2},{68,3},{5,4},{69,5},{4,6},{72,7},{9,8},{73,9},{... | collective-permute-start | bytes 147464 | tf_op jit(solution)/shard_map/ppermute | solution.py:407
  143.6 0.7 collective-permute-start.19
  144.2 7.0 %collective-permute-start.20 = (bf16[96,256]{1,0:T(8,128)(2,1)S(1)}, bf16[96,256]{1,0:T(8,128)(2,1)S(1)}, u32[]{:S(2)}, u32[]{:S(2)}) collective-permute-start(bf16[96,256]{1,0:T(8,128)(2,1)S(1)} %get-tuple-element.38), channel_id=1, source_target_pairs={{0,0},{64,1},{1,2},{69,3},{4,4},{68,5},{5,6},{73,7},{8,8},{72,9},{... | collective-permute-start | bytes 147464 | tf_op jit(solution)/shard_map/ppermute | solution.py:407
  151.2 1.5 reduce_sum.12
  152.8 6.3 %collective-permute-start.21 = (bf16[12,1728]{1,0:T(8,128)(2,1)S(1)}, bf16[12,1728]{1,0:T(8,128)(2,1)S(1)}, u32[]{:S(2)}, u32[]{:S(2)}) collective-permute-start(bf16[12,1728]{1,0:T(8,128)(2,1)S(1)} %get-tuple-element.48), channel_id=1, source_target_pairs={{1,0},{0,1},{5,2},{4,3},{9,4},{8,5},{13,6},{12,7},{65,8},{64,9},{6... | collective-permute-start | bytes 124424 | tf_op jit(solution)/shard_map/ppermute | solution.py:417
  159.1 4.7 %collective-permute-start.22 = (bf16[12,1728]{1,0:T(8,128)(2,1)S(1)}, bf16[12,1728]{1,0:T(8,128)(2,1)S(1)}, u32[]{:S(2)}, u32[]{:S(2)}) collective-permute-start(bf16[12,1728]{1,0:T(8,128)(2,1)S(1)} %get-tuple-element.49), channel_id=1, source_target_pairs={{0,0},{1,1},{4,2},{5,3},{8,4},{9,5},{12,6},{13,7},{64,8},{65,9},{6... | collective-permute-start | bytes 124424 | tf_op jit(solution)/shard_map/ppermute | solution.py:416
  163.8 1.4 shard_map.57
  165.2 4.8 %collective-permute-done.22 = bf16[12,1728]{1,0:T(8,128)(2,1)S(1)} collective-permute-done((bf16[12,1728]{1,0:T(8,128)(2,1)S(1)}, bf16[12,1728]{1,0:T(8,128)(2,1)S(1)}, u32[]{:S(2)}, u32[]{:S(2)}) %collective-permute-start.22) | collective-permute-done | bytes 41504 | tf_op jit(solution)/shard_map/ppermute | solution.py:416
  171.4 0.7 select_convert_fusion
  (41 shorter events, 2.9 us)
Async XLA Ops:
  2.7 13.4 %collective-permute-start.5 = (bf16[12,1728]{1,0:T(8,128)(2,1)S(1)}, bf16[12,1728]{1,0:T(8,128)(2,1)S(1)}, u32[]{:S(2)}, u32[]{:S(2)}) collective-permute-start(bf16[12,1728]{1,0:T(8,128)(2,1)S(1)} %select_n.108), channel_id=1, source_target_pairs={{0,1},{1,0},{2,5},{3,4},{4,9},{5,8},{6,13},{7,12},{8,65},{9,64},{1... | collective-permute-start | bytes 124424 | tf_op jit(solution)/shard_map/ppermute | solution.py:350
  10.9 8.9 %collective-permute-start.6 = (bf16[12,1728]{1,0:T(8,128)(2,1)S(1)}, bf16[12,1728]{1,0:T(8,128)(2,1)S(1)}, u32[]{:S(2)}, u32[]{:S(2)}) collective-permute-start(bf16[12,1728]{1,0:T(8,128)(2,1)S(1)} %select_n.110), channel_id=1, source_target_pairs={{0,0},{1,1},{2,4},{3,5},{4,8},{5,9},{6,12},{7,13},{8,64},{9,65},{1... | collective-permute-start | bytes 124424 | tf_op jit(solution)/shard_map/ppermute | solution.py:349
  21.1 3.8 %copy-start.1 = (bf16[256,384]{1,0:T(8,128)(2,1)S(1)}, bf16[256,384]{1,0:T(8,128)(2,1)}, u32[]{:S(2)}) copy-start(bf16[256,384]{1,0:T(8,128)(2,1)} %param.3) | copy-start | bytes 589828
  21.1 5.7 %copy-start = (s32[2,2]{1,0:T(2,128)S(1)}, s32[2,2]{1,0:T(2,128)}, u32[]{:S(2)}) copy-start(s32[2,2]{1,0:T(2,128)} %param.5) | copy-start | bytes 52
  21.1 70.7 %all-to-all-start = ((bf16[16,24,1728]{2,1,0:T(8,128)(2,1)}), bf16[16,24,1728]{2,1,0:T(8,128)(2,1)S(1)}, u32[]{:S(2)}, u32[]{:S(2)}) async-start(bf16[16,24,1728]{2,1,0:T(8,128)(2,1)} %broadcast_in_dim.3), calls=%async_computation | async-start | bytes 2752512 | tf_op jit(solution)/shard_map/all_to_all | solution.py:355
  24.9 7.8 %collective-permute-start = (bf16[256,384]{1,0:T(8,128)(2,1)S(1)}, bf16[256,384]{1,0:T(8,128)(2,1)S(1)}, u32[]{:S(2)}, u32[]{:S(2)}) collective-permute-start(bf16[256,384]{1,0:T(8,128)(2,1)S(1)} %copy-done.1), channel_id=1, source_target_pairs={{0,1},{1,2},{2,3},{3,4},{4,5},{5,6},{6,7},{7,8},{8,9},{9,10},{10,1... | collective-permute-start | bytes 589832 | tf_op jit(solution)/shard_map/ppermute | solution.py:357
  33.4 7.9 %collective-permute-start.1 = (bf16[96,256]{1,0:T(8,128)(2,1)S(1)}, bf16[96,256]{1,0:T(8,128)(2,1)S(1)}, u32[]{:S(2)}, u32[]{:S(2)}) collective-permute-start(bf16[96,256]{1,0:T(8,128)(2,1)S(1)} %get-tuple-element.21), channel_id=1, source_target_pairs={{0,0},{1,64},{2,1},{3,65},{4,4},{5,68},{6,5},{7,69},{8,8},{9,72},{... | collective-permute-start | bytes 147464 | tf_op jit(solution)/shard_map/ppermute | solution.py:361
  38.6 33.3 %collective-permute-start.2 = (bf16[96,256]{1,0:T(8,128)(2,1)S(1)}, bf16[96,256]{1,0:T(8,128)(2,1)S(1)}, u32[]{:S(2)}, u32[]{:S(2)}) collective-permute-start(bf16[96,256]{1,0:T(8,128)(2,1)S(1)} %get-tuple-element.22), channel_id=1, source_target_pairs={{0,64},{1,1},{2,65},{3,0},{4,68},{5,5},{6,69},{7,4},{8,72},{9,9},{... | collective-permute-start | bytes 147464 | tf_op jit(solution)/shard_map/ppermute | solution.py:361
  40.5 31.4 %collective-permute-start.3 = (bf16[96,256]{1,0:T(8,128)(2,1)S(1)}, bf16[96,256]{1,0:T(8,128)(2,1)S(1)}, u32[]{:S(2)}, u32[]{:S(2)}) collective-permute-start(bf16[96,256]{1,0:T(8,128)(2,1)S(1)} %get-tuple-element.23), channel_id=1, source_target_pairs={{0,1},{1,65},{2,0},{3,64},{4,5},{5,69},{6,4},{7,68},{8,9},{9,73},{... | collective-permute-start | bytes 147464 | tf_op jit(solution)/shard_map/ppermute | solution.py:361
  40.6 31.3 %collective-permute-start.4 = (bf16[96,256]{1,0:T(8,128)(2,1)S(1)}, bf16[96,256]{1,0:T(8,128)(2,1)S(1)}, u32[]{:S(2)}, u32[]{:S(2)}) collective-permute-start(bf16[96,256]{1,0:T(8,128)(2,1)S(1)} %get-tuple-element.24), channel_id=1, source_target_pairs={{0,65},{1,0},{2,64},{3,1},{4,69},{5,4},{6,68},{7,5},{8,73},{9,8},{... | collective-permute-start | bytes 147464 | tf_op jit(solution)/shard_map/ppermute | solution.py:361
  72.8 10.7 %collective-permute-start.7 = (bf16[96,1024]{1,0:T(8,128)(2,1)S(1)}, bf16[96,1024]{1,0:T(8,128)(2,1)S(1)}, u32[]{:S(2)}, u32[]{:S(2)}) collective-permute-start(bf16[96,1024]{1,0:T(8,128)(2,1)S(1)} %get-tuple-element.26.a0), channel_id=1, source_target_pairs={{0,1},{1,2},{2,3},{3,0},{4,5},{5,6},{6,7},{7,4},{8,9},{9,10},{10,1... | collective-permute-start | bytes 589832 | tf_op jit(solution)/shard_map/ppermute | solution.py:74
  78.8 10.6 %collective-permute-start.8 = (bf16[96,1024]{1,0:T(8,128)(2,1)S(1)}, bf16[96,1024]{1,0:T(8,128)(2,1)S(1)}, u32[]{:S(2)}, u32[]{:S(2)}) collective-permute-start(bf16[96,1024]{1,0:T(8,128)(2,1)S(1)} %get-tuple-element.26.a0), channel_id=1, source_target_pairs={{0,2},{1,3},{2,0},{3,1},{4,6},{5,7},{6,4},{7,5},{8,10},{9,11},{10,... | collective-permute-start | bytes 589832 | tf_op jit(solution)/shard_map/ppermute | solution.py:74
  81.5 10.3 %collective-permute-start.9 = (bf16[96,1024]{1,0:T(8,128)(2,1)S(1)}, bf16[96,1024]{1,0:T(8,128)(2,1)S(1)}, u32[]{:S(2)}, u32[]{:S(2)}) collective-permute-start(bf16[96,1024]{1,0:T(8,128)(2,1)S(1)} %get-tuple-element.26.a0), channel_id=1, source_target_pairs={{0,3},{1,0},{2,1},{3,2},{4,7},{5,4},{6,5},{7,6},{8,11},{9,8},{10,9... | collective-permute-start | bytes 589832 | tf_op jit(solution)/shard_map/ppermute | solution.py:74
  94.6 2.1 %collective-permute-start.10 = (f32[96,1024]{1,0:T(8,128)S(1)}, f32[96,1024]{1,0:T(8,128)S(1)}, u32[]{:S(2)}, u32[]{:S(2)}) collective-permute-start(f32[96,1024]{1,0:T(8,128)S(1)} %get-tuple-element.28), channel_id=1, source_target_pairs={{0,64},{64,0},{1,65},{65,1},{2,66},{66,2},{3,67},{67,3},{4,68},{68... | collective-permute-start | bytes 1179656 | tf_op jit(solution)/shard_map/ppermute | solution.py:70
  95.3 7.9 %collective-permute-start.12 = (bf16[96,1024]{1,0:T(8,128)(2,1)S(1)}, bf16[96,1024]{1,0:T(8,128)(2,1)S(1)}, u32[]{:S(2)}, u32[]{:S(2)}) collective-permute-start(bf16[96,1024]{1,0:T(8,128)(2,1)S(1)} %get-tuple-element.25.x), channel_id=1, source_target_pairs={{0,128},{128,0},{1,129},{129,1},{2,130},{130,2},{3,131},{131,3},{4... | collective-permute-start | bytes 589832 | tf_op jit(solution)/shard_map/ppermute | solution.py:70
  97.3 10.1 %collective-permute-start.11 = (bf16[96,1024]{1,0:T(8,128)(2,1)S(1)}, bf16[96,1024]{1,0:T(8,128)(2,1)S(1)}, u32[]{:S(2)}, u32[]{:S(2)}) collective-permute-start(bf16[96,1024]{1,0:T(8,128)(2,1)S(1)} %shard_map.53.mine), channel_id=1, source_target_pairs={{0,128},{128,0},{1,129},{129,1},{2,130},{130,2},{3,131},{131,3},{4... | collective-permute-start | bytes 589832 | tf_op jit(solution)/shard_map/ppermute | solution.py:70
  108.5 2.1 %collective-permute-start.13 = (bf16[96,1024]{1,0:T(8,128)(2,1)S(1)}, bf16[96,1024]{1,0:T(8,128)(2,1)S(1)}, u32[]{:S(2)}, u32[]{:S(2)}) collective-permute-start(bf16[96,1024]{1,0:T(8,128)(2,1)S(1)} %get-tuple-element.30.b_own), channel_id=1, source_target_pairs={{0,64},{64,0},{1,65},{65,1},{2,66},{66,2},{3,67},{67,3},{4,68},{68... | collective-permute-start | bytes 589832 | tf_op jit(solution)/shard_map/ppermute | solution.py:70
  114.8 36.4 %all-to-all-start.1 = ((bf16[16,24,1728]{2,1,0:T(8,128)(2,1)}), bf16[16,24,1728]{2,1,0:T(8,128)(2,1)}, u32[]{:S(2)}, u32[]{:S(2)}) async-start(bf16[16,24,1728]{2,1,0:T(8,128)(2,1)} %bitcast.6), calls=%async_computation.1 | async-start | bytes 2752512 | tf_op jit(solution)/shard_map/all_to_all | solution.py:412
  124.0 6.1 %collective-permute-start.14 = (bf16[96,1024]{1,0:T(8,128)(2,1)S(1)}, bf16[96,1024]{1,0:T(8,128)(2,1)S(1)}, u32[]{:S(2)}, u32[]{:S(2)}) collective-permute-start(bf16[96,1024]{1,0:T(8,128)(2,1)S(1)} %get-tuple-element.32), channel_id=1, source_target_pairs={{0,1},{1,2},{2,3},{3,0},{4,5},{5,6},{6,7},{7,4},{8,9},{9,10},{10,1... | collective-permute-start | bytes 589832 | tf_op jit(solution)/shard_map/ppermute | solution.py:74
  125.2 9.7 %collective-permute-start.15 = (bf16[96,1024]{1,0:T(8,128)(2,1)S(1)}, bf16[96,1024]{1,0:T(8,128)(2,1)S(1)}, u32[]{:S(2)}, u32[]{:S(2)}) collective-permute-start(bf16[96,1024]{1,0:T(8,128)(2,1)S(1)} %get-tuple-element.33), channel_id=1, source_target_pairs={{0,2},{1,3},{2,0},{3,1},{4,6},{5,7},{6,4},{7,5},{8,10},{9,11},{10,... | collective-permute-start | bytes 589832 | tf_op jit(solution)/shard_map/ppermute | solution.py:74
  126.2 9.7 %collective-permute-start.16 = (bf16[96,1024]{1,0:T(8,128)(2,1)S(1)}, bf16[96,1024]{1,0:T(8,128)(2,1)S(1)}, u32[]{:S(2)}, u32[]{:S(2)}) collective-permute-start(bf16[96,1024]{1,0:T(8,128)(2,1)S(1)} %get-tuple-element.34), channel_id=1, source_target_pairs={{0,3},{1,0},{2,1},{3,2},{4,7},{5,4},{6,5},{7,6},{8,11},{9,8},{10,9... | collective-permute-start | bytes 589832 | tf_op jit(solution)/shard_map/ppermute | solution.py:74
  136.7 22.4 %collective-permute-start.17 = (bf16[96,256]{1,0:T(8,128)(2,1)S(1)}, bf16[96,256]{1,0:T(8,128)(2,1)S(1)}, u32[]{:S(2)}, u32[]{:S(2)}) collective-permute-start(bf16[96,256]{1,0:T(8,128)(2,1)S(1)} %get-tuple-element.35), channel_id=1, source_target_pairs={{64,0},{1,1},{65,2},{4,3},{68,4},{5,5},{69,6},{8,7},{72,8},{9,9},{... | collective-permute-start | bytes 147464 | tf_op jit(solution)/shard_map/ppermute | solution.py:407
  139.5 24.3 %collective-permute-start.18 = (bf16[96,256]{1,0:T(8,128)(2,1)S(1)}, bf16[96,256]{1,0:T(8,128)(2,1)S(1)}, u32[]{:S(2)}, u32[]{:S(2)}) collective-permute-start(bf16[96,256]{1,0:T(8,128)(2,1)S(1)} %get-tuple-element.36), channel_id=1, source_target_pairs={{1,0},{65,1},{0,2},{68,3},{5,4},{69,5},{4,6},{72,7},{9,8},{73,9},{... | collective-permute-start | bytes 147464 | tf_op jit(solution)/shard_map/ppermute | solution.py:407
  143.6 20.2 %collective-permute-start.19 = (bf16[96,256]{1,0:T(8,128)(2,1)S(1)}, bf16[96,256]{1,0:T(8,128)(2,1)S(1)}, u32[]{:S(2)}, u32[]{:S(2)}) collective-permute-start(bf16[96,256]{1,0:T(8,128)(2,1)S(1)} %get-tuple-element.37), channel_id=1, source_target_pairs={{65,0},{0,1},{64,2},{5,3},{69,4},{4,5},{68,6},{9,7},{73,8},{8,9},{... | collective-permute-start | bytes 147464 | tf_op jit(solution)/shard_map/ppermute | solution.py:407
  144.2 19.6 %collective-permute-start.20 = (bf16[96,256]{1,0:T(8,128)(2,1)S(1)}, bf16[96,256]{1,0:T(8,128)(2,1)S(1)}, u32[]{:S(2)}, u32[]{:S(2)}) collective-permute-start(bf16[96,256]{1,0:T(8,128)(2,1)S(1)} %get-tuple-element.38), channel_id=1, source_target_pairs={{0,0},{64,1},{1,2},{69,3},{4,4},{68,5},{5,6},{73,7},{8,8},{72,9},{... | collective-permute-start | bytes 147464 | tf_op jit(solution)/shard_map/ppermute | solution.py:407
  152.8 12.4 %collective-permute-start.21 = (bf16[12,1728]{1,0:T(8,128)(2,1)S(1)}, bf16[12,1728]{1,0:T(8,128)(2,1)S(1)}, u32[]{:S(2)}, u32[]{:S(2)}) collective-permute-start(bf16[12,1728]{1,0:T(8,128)(2,1)S(1)} %get-tuple-element.48), channel_id=1, source_target_pairs={{1,0},{0,1},{5,2},{4,3},{9,4},{8,5},{13,6},{12,7},{65,8},{64,9},{6... | collective-permute-start | bytes 124424 | tf_op jit(solution)/shard_map/ppermute | solution.py:417
  159.1 10.9 %collective-permute-start.22 = (bf16[12,1728]{1,0:T(8,128)(2,1)S(1)}, bf16[12,1728]{1,0:T(8,128)(2,1)S(1)}, u32[]{:S(2)}, u32[]{:S(2)}) collective-permute-start(bf16[12,1728]{1,0:T(8,128)(2,1)S(1)} %get-tuple-element.49), channel_id=1, source_target_pairs={{0,0},{1,1},{4,2},{5,3},{8,4},{9,5},{12,6},{13,7},{64,8},{65,9},{6... | collective-permute-start | bytes 124424 | tf_op jit(solution)/shard_map/ppermute | solution.py:416

commit v4 on v3

--- a/solution.py
+++ b/solution.py
@@ -37,15 +37,11 @@
                         yield xh, core, z, xl, y
 
 
-def pixel_pairs(turn, ahead):
+def pixel_pairs(turn):
     pairs = []
     for xh, core, z, xl, y in every():
-        slot = ((z * 2 + xl) * 4 + y + ahead) % 64
-        sample, piece = slot // 4, slot % 4
-        u = (piece + turn) % 4
-        pairs.append(
-            (flat(xh, core, z, xl, y), flat(xh, u % 2, sample // 2, sample % 2, 2 * core + u // 2))
-        )
+        u = (y + turn) % 4
+        pairs.append((flat(xh, core, z, xl, y), flat(xh, u % 2, z, xl, 2 * core + u // 2)))
     return pairs
 
 
@@ -74,6 +70,10 @@
     return lax.ppermute(value, "y", [(i, (i + d) % 4) for i in range(4)])
 
 
+def shift(value, d):
+    return lax.ppermute(value, FSDP, [(i, (i + d) % 64) for i in range(64)])
+
+
 def pixels():
     p = lax.broadcasted_iota(jnp.int32, (1, PIX), 1)
     return p >> 5, p & 31
@@ -141,7 +141,7 @@
 def join_kernel(prm, *refs):
     ins, out, scratch = refs[:4], refs[4], refs[5]
     for v in range(4):
-        scratch[rows((prm[5] + v) % 4), :] = ins[v][...]
+        scratch[rows((prm[2] + v) % 4), :] = ins[v][...]
     out[...] = scratch[...].astype(F32).T.astype(BF16)
 
 
@@ -336,8 +336,7 @@
     micro = z // 4
     own_bucket = jnp.where(micro == 0, buckets[0], buckets[1])
     size = 16 + 2 * own_bucket
-    piece = (y + 1) % 4
-    prm = jnp.stack([xh, core, y, size[0], size[1], piece]).astype(jnp.int32)
+    prm = jnp.stack([xh, core, y, size[0], size[1]]).astype(jnp.int32)
     own = ((OWN, PIX), BF16)
     own32 = ((OWN, PIX), F32)
 
@@ -354,11 +353,11 @@
     copies = jnp.broadcast_to(part, (16, 24, LANES))
     w = lax.all_to_all(copies, WEIGHT_GROUP, 0, 0, tiled=True).reshape(QUAD, LANES)
 
-    shifted = lax.ppermute(signals, FSDP, [(i, (i + 1) % 64) for i in range(64)])
+    shifted = shift(signals, 1)
     blocks = call(
         split_kernel, [((OWN, 256), BF16)] * 4, [((QUAD, 256), BF16)], prm, shifted
     )
-    blocks = [lax.ppermute(b, AX, pixel_pairs(v, 0)) for v, b in enumerate(blocks)]
+    blocks = [lax.ppermute(b, AX, pixel_pairs(v)) for v, b in enumerate(blocks)]
     x, a = call(start_kernel, [own, own], [], prm, *blocks)
     others = [turn_y(a, d) for d in (1, 2, 3)]
     g = swap(x, "xh")
@@ -404,17 +403,18 @@
     )
     got = [turn_y(s, d) for d, s in enumerate(sends, 1)]
     blocks = call(last_kernel, [((OWN, 256), BF16)] * 4, [own], prm, x, q, keep, *got)
-    blocks = [lax.ppermute(b, AX, back(pixel_pairs(v, 1))) for v, b in enumerate(blocks)]
-    (results,) = call(
+    blocks = [lax.ppermute(b, AX, back(pixel_pairs(v))) for v, b in enumerate(blocks)]
+    (joined,) = call(
         join_kernel, [((256, QUAD), BF16)], [((QUAD, 256), BF16)], prm, *blocks
     )
+    results = shift(joined, -1)
 
     shares = lax.all_to_all(dw.reshape(16, 24, LANES), WEIGHT_GROUP, 0, 0, tiled=True)
     total = jnp.sum(shares.astype(F32), axis=0).astype(BF16)
-    first, second = total[:12], total[12:]
+    pieces = [jnp.where(flip, total[12:], total[:12]), jnp.where(flip, total[:12], total[12:])]
     low_high = [
-        lax.ppermute(jnp.where(flip, second, first), AX, back(weight_pairs(0))),
-        lax.ppermute(jnp.where(flip, first, second), AX, back(weight_pairs(1))),
+        lax.ppermute(pieces[0], AX, back(weight_pairs(0))),
+        lax.ppermute(pieces[1], AX, back(weight_pairs(1))),
     ]
     low = jnp.where(odd, low_high[1], low_high[0]).reshape(12, TAPS, 2, OWN)
     high = jnp.where(odd, low_high[0], low_high[1]).reshape(12, TAPS, 2, OWN)

time: 173 us -> 175 us (1.012)
  the two profiles are of different devices: /device:TPU:21 before, /device:TPU:20 now
where the time goes in v4:
time: 175 us
  starting transfers between devices  94.5 us (54%)
  waiting for transfers between devices  55 us (31%)
  Pallas kernels  16.5 us (9%)
  local copies, waits for them, and re-layouts  4.82 us (3%)
  other arithmetic  2.86 us (2%)
    ppermute x4, starting transfers between devices, step(): blocks = [lax.ppermute(b, AX, pixel_pairs(v)) for v, b in enumerate(blocks)]  43 us
    ppermute x6, waiting for transfers between devices, turn_y(): return lax.ppermute(value, 'y', [(i, (i + d) % 4) for i in range(4)])  20.9 us
    pallas_call x9, Pallas kernels, call(): pl.pallas_call(kernel, out_shape=[jax.ShapeDtypeStruct(s, d) for s, d in...  16.5 us
    ppermute x4, waiting for transfers between devices, swap(): return lax.ppermute(value, axis, [(0, 1), (1, 0)])  11.7 us
    ppermute x4, starting transfers between devices, step(): lax.ppermute(b, AX, back(pixel_pairs(v)))  8.14 us
    ppermute x1, starting transfers between devices, step(): lax.ppermute(pieces[0], AX, back(weight_pairs(0)))  7.8 us
    ppermute x1, starting transfers between devices, step(): lax.ppermute(jnp.where(odd, low, high), AX, weight_pairs(1))  6.98 us
    ppermute x6, starting transfers between devices, turn_y(): return lax.ppermute(value, 'y', [(i, (i + d) % 4) for i in range(4)])  5.9 us
  transfers between devices with their start and end apart: 26, of which 18 were waited for; matrix products, arithmetic and copies ran while one was open for 1% of the time, Pallas kernels for 5%

profile of v4, /device:TPU:20, one launch (start us, length us, event | category | flops | bytes accessed | tf_op | source)
XLA Modules:
  0.0 174.8 jit_solution(4795685765176880951)
XLA Ops:
  0.6 1.0 reshape.37
  2.7 7.0 %collective-permute-start.5 = (bf16[12,1728]{1,0:T(8,128)(2,1)S(1)}, bf16[12,1728]{1,0:T(8,128)(2,1)S(1)}, u32[]{:S(2)}, u32[]{:S(2)}) collective-permute-start(bf16[12,1728]{1,0:T(8,128)(2,1)S(1)} %select_n.103), channel_id=1, source_target_pairs={{0,1},{1,0},{2,5},{3,4},{4,9},{5,8},{6,13},{7,12},{8,65},{9,64},{1... | collective-permute-start | bytes 124424 | tf_op jit(solution)/shard_map/ppermute | solution.py:349
  9.8 4.9 %collective-permute-start.6 = (bf16[12,1728]{1,0:T(8,128)(2,1)S(1)}, bf16[12,1728]{1,0:T(8,128)(2,1)S(1)}, u32[]{:S(2)}, u32[]{:S(2)}) collective-permute-start(bf16[12,1728]{1,0:T(8,128)(2,1)S(1)} %select_n.105), channel_id=1, source_target_pairs={{0,0},{1,1},{2,4},{3,5},{4,8},{5,9},{6,12},{7,13},{8,64},{9,65},{1... | collective-permute-start | bytes 124424 | tf_op jit(solution)/shard_map/ppermute | solution.py:348
  14.7 3.7 %collective-permute-done.6 = bf16[12,1728]{1,0:T(8,128)(2,1)S(1)} collective-permute-done((bf16[12,1728]{1,0:T(8,128)(2,1)S(1)}, bf16[12,1728]{1,0:T(8,128)(2,1)S(1)}, u32[]{:S(2)}, u32[]{:S(2)}) %collective-permute-start.6) | collective-permute-done | bytes 41504 | tf_op jit(solution)/shard_map/ppermute | solution.py:348
  18.4 1.2 broadcast_in_dim.3
  19.7 3.8 %all-to-all-start = ((bf16[16,24,1728]{2,1,0:T(8,128)(2,1)}), bf16[16,24,1728]{2,1,0:T(8,128)(2,1)S(1)}, u32[]{:S(2)}, u32[]{:S(2)}) async-start(bf16[16,24,1728]{2,1,0:T(8,128)(2,1)} %broadcast_in_dim.3), calls=%async_computation | async-start | bytes 2752512 | tf_op jit(solution)/shard_map/all_to_all | solution.py:354
  23.5 3.8 %collective-permute-start = (bf16[256,384]{1,0:T(8,128)(2,1)S(1)}, bf16[256,384]{1,0:T(8,128)(2,1)S(1)}, u32[]{:S(2)}, u32[]{:S(2)}) collective-permute-start(bf16[256,384]{1,0:T(8,128)(2,1)S(1)} %copy-done.1), channel_id=1, source_target_pairs={{0,1},{1,2},{2,3},{3,4},{4,5},{5,6},{6,7},{7,8},{8,9},{9,10},{10,1... | collective-permute-start | bytes 589832 | tf_op jit(solution)/shard_map/ppermute | solution.py:74
  27.4 4.0 %collective-permute-done.x_ref = bf16[256,384]{1,0:T(8,128)(2,1)S(1)} collective-permute-done((bf16[256,384]{1,0:T(8,128)(2,1)S(1)}, bf16[256,384]{1,0:T(8,128)(2,1)S(1)}, u32[]{:S(2)}, u32[]{:S(2)}) %collective-permute-start) | collective-permute-done | bytes 196640 | tf_op jit(solution)/shard_map/ppermute | solution.py:74
  32.2 5.6 %collective-permute-start.1 = (bf16[96,256]{1,0:T(8,128)(2,1)S(1)}, bf16[96,256]{1,0:T(8,128)(2,1)S(1)}, u32[]{:S(2)}, u32[]{:S(2)}) collective-permute-start(bf16[96,256]{1,0:T(8,128)(2,1)S(1)} %get-tuple-element.21), channel_id=1, source_target_pairs={{0,0},{1,64},{2,1},{3,65},{4,4},{5,68},{6,5},{7,69},{8,8},{9,72},{... | collective-permute-start | bytes 147464 | tf_op jit(solution)/shard_map/ppermute | solution.py:360
  37.7 1.9 %collective-permute-start.2 = (bf16[96,256]{1,0:T(8,128)(2,1)S(1)}, bf16[96,256]{1,0:T(8,128)(2,1)S(1)}, u32[]{:S(2)}, u32[]{:S(2)}) collective-permute-start(bf16[96,256]{1,0:T(8,128)(2,1)S(1)} %get-tuple-element.22), channel_id=1, source_target_pairs={{0,64},{1,1},{2,65},{3,0},{4,68},{5,5},{6,69},{7,4},{8,72},{9,9},{... | collective-permute-start | bytes 147464 | tf_op jit(solution)/shard_map/ppermute | solution.py:360
  39.7 31.0 %collective-permute-start.3 = (bf16[96,256]{1,0:T(8,128)(2,1)S(1)}, bf16[96,256]{1,0:T(8,128)(2,1)S(1)}, u32[]{:S(2)}, u32[]{:S(2)}) collective-permute-start(bf16[96,256]{1,0:T(8,128)(2,1)S(1)} %get-tuple-element.23), channel_id=1, source_target_pairs={{0,1},{1,65},{2,0},{3,64},{4,5},{5,69},{6,4},{7,68},{8,9},{9,73},{... | collective-permute-start | bytes 147464 | tf_op jit(solution)/shard_map/ppermute | solution.py:360
  70.7 4.5 %collective-permute-start.4 = (bf16[96,256]{1,0:T(8,128)(2,1)S(1)}, bf16[96,256]{1,0:T(8,128)(2,1)S(1)}, u32[]{:S(2)}, u32[]{:S(2)}) collective-permute-start(bf16[96,256]{1,0:T(8,128)(2,1)S(1)} %get-tuple-element.24), channel_id=1, source_target_pairs={{0,65},{1,0},{2,64},{3,1},{4,69},{5,4},{6,68},{7,5},{8,73},{9,8},{... | collective-permute-start | bytes 147464 | tf_op jit(solution)/shard_map/ppermute | solution.py:360
  75.3 1.7 collective-permute-done.4.refs_3_
  77.0 0.8 shard_map.51
  77.9 1.6 collective-permute-start.8
  79.5 1.1 collective-permute-start.9
  80.6 3.0 %collective-permute-done.7.a1 = bf16[96,1024]{1,0:T(8,128)(2,1)S(1)} collective-permute-done((bf16[96,1024]{1,0:T(8,128)(2,1)S(1)}, bf16[96,1024]{1,0:T(8,128)(2,1)S(1)}, u32[]{:S(2)}, u32[]{:S(2)}) %collective-permute-start.7) | collective-permute-done | bytes 196640 | tf_op jit(solution)/shard_map/ppermute | solution.py:70
  83.6 4.5 %collective-permute-done.8.a2 = bf16[96,1024]{1,0:T(8,128)(2,1)S(1)} collective-permute-done((bf16[96,1024]{1,0:T(8,128)(2,1)S(1)}, bf16[96,1024]{1,0:T(8,128)(2,1)S(1)}, u32[]{:S(2)}, u32[]{:S(2)}) %collective-permute-start.8) | collective-permute-done | bytes 196640 | tf_op jit(solution)/shard_map/ppermute | solution.py:70
  88.1 3.7 %collective-permute-done.9.a3 = bf16[96,1024]{1,0:T(8,128)(2,1)S(1)} collective-permute-done((bf16[96,1024]{1,0:T(8,128)(2,1)S(1)}, bf16[96,1024]{1,0:T(8,128)(2,1)S(1)}, u32[]{:S(2)}, u32[]{:S(2)}) %collective-permute-start.9) | collective-permute-done | bytes 196640 | tf_op jit(solution)/shard_map/ppermute | solution.py:70
  91.8 2.8 %shard_map.52 = (bf16[384,1024]{1,0:T(8,128)(2,1)S(1)}, f32[96,1024]{1,0:T(8,128)S(1)}, f32[96,1024]{1,0:T(8,128)S(1)}) custom-call(s32[5]{0:T(128)S(1)} %pad_add_fusion.prm, bf16[384,1728]{1,0:T(8,128)(2,1)S(1)} %bitcast.13, bf16[96,1024]{1,0:T(8,128)(2,1)S(1)} %get-tuple-element.26.a0, bf16[96,1024]{1,0:T(8,128)(2,1)S(1)} %collective-permute-done.7.a1, ...), custom_call_target="tpu_custom_call" | custom-call | tf_op jit(solution)/shard_map/pallas_call | solution.py:324
  94.8 1.6 collective-permute-done.10.got
  97.0 2.0 %collective-permute-start.11 = (bf16[96,1024]{1,0:T(8,128)(2,1)S(1)}, bf16[96,1024]{1,0:T(8,128)(2,1)S(1)}, u32[]{:S(2)}, u32[]{:S(2)}) collective-permute-start(bf16[96,1024]{1,0:T(8,128)(2,1)S(1)} %shard_map.53.mine), channel_id=1, source_target_pairs={{0,128},{128,0},{1,129},{129,1},{2,130},{130,2},{3,131},{131,3},{4... | collective-permute-start | bytes 589832 | tf_op jit(solution)/shard_map/ppermute | solution.py:66
  99.0 5.0 %collective-permute-done.12.g = bf16[96,1024]{1,0:T(8,128)(2,1)S(1)} collective-permute-done((bf16[96,1024]{1,0:T(8,128)(2,1)S(1)}, bf16[96,1024]{1,0:T(8,128)(2,1)S(1)}, u32[]{:S(2)}, u32[]{:S(2)}) %collective-permute-start.12) | collective-permute-done | bytes 196640 | tf_op jit(solution)/shard_map/ppermute | solution.py:66
  104.1 3.7 %collective-permute-done.11.theirs = bf16[96,1024]{1,0:T(8,128)(2,1)S(1)} collective-permute-done((bf16[96,1024]{1,0:T(8,128)(2,1)S(1)}, bf16[96,1024]{1,0:T(8,128)(2,1)S(1)}, u32[]{:S(2)}, u32[]{:S(2)}) %collective-permute-start.11) | collective-permute-done | bytes 196640 | tf_op jit(solution)/shard_map/ppermute | solution.py:66
  107.7 1.0 shard_map.54
  108.8 1.4 collective-permute-done.13.b_other
  110.3 4.3 %shard_map.58 = bf16[384,1728]{1,0:T(8,128)(2,1)} custom-call(s32[5]{0:T(128)S(1)} %pad_add_fusion.prm, bf16[384,1024]{1,0:T(8,128)(2,1)S(1)} %get-tuple-element.39.full, bf16[96,1024]{1,0:T(8,128)(2,1)S(1)} %get-tuple-element.30.b_own, bf16[96,1024]{1,0:T(8,128)(2,1)S(1)} %collective-permute-done.13.b_other), custom_call_target="tpu_custom_call" | custom-call | tf_op jit(solution)/shard_map/pallas_call | solution.py:324
  114.5 4.6 %all-to-all-start.1 = ((bf16[16,24,1728]{2,1,0:T(8,128)(2,1)}), bf16[16,24,1728]{2,1,0:T(8,128)(2,1)}, u32[]{:S(2)}, u32[]{:S(2)}) async-start(bf16[16,24,1728]{2,1,0:T(8,128)(2,1)} %bitcast.5), calls=%async_computation.1 | async-start | bytes 2752512 | tf_op jit(solution)/shard_map/all_to_all | solution.py:412
  119.1 4.8 %shard_map.55 = (f32[96,1024]{1,0:T(8,128)S(1)}, bf16[96,1024]{1,0:T(8,128)(2,1)S(1)}, bf16[96,1024]{1,0:T(8,128)(2,1)S(1)}, bf16[96,1024]{1,0:T(8,128)(2,1)S(1)}) custom-call(s32[5]{0:T(128)S(1)} %pad_add_fusion.prm, bf16[384,1728]{1,0:T(8,128)(2,1)S(1)} %bitcast.14, bf16[96,1024]{1,0:T(8,128)(2,1)S(1)} %get-tuple-element.30.b_own, ...), custom_call_target="tpu_custom_call" | custom-call | tf_op jit(solution)/shard_map/pallas_call | solution.py:324
  123.9 1.6 collective-permute-start.14
  125.4 1.3 collective-permute-start.15
  127.0 4.2 %collective-permute-done.14.r1 = bf16[96,1024]{1,0:T(8,128)(2,1)S(1)} collective-permute-done((bf16[96,1024]{1,0:T(8,128)(2,1)S(1)}, bf16[96,1024]{1,0:T(8,128)(2,1)S(1)}, u32[]{:S(2)}, u32[]{:S(2)}) %collective-permute-start.14) | collective-permute-done | bytes 196640 | tf_op jit(solution)/shard_map/ppermute | solution.py:70
  131.2 4.4 %collective-permute-done.15.r2 = bf16[96,1024]{1,0:T(8,128)(2,1)S(1)} collective-permute-done((bf16[96,1024]{1,0:T(8,128)(2,1)S(1)}, bf16[96,1024]{1,0:T(8,128)(2,1)S(1)}, u32[]{:S(2)}, u32[]{:S(2)}) %collective-permute-start.15) | collective-permute-done | bytes 196640 | tf_op jit(solution)/shard_map/ppermute | solution.py:70
  135.6 1.2 collective-permute-done.16.r3
  136.8 0.8 shard_map.56
  137.5 1.9 %collective-permute-start.17 = (bf16[96,256]{1,0:T(8,128)(2,1)S(1)}, bf16[96,256]{1,0:T(8,128)(2,1)S(1)}, u32[]{:S(2)}, u32[]{:S(2)}) collective-permute-start(bf16[96,256]{1,0:T(8,128)(2,1)S(1)} %get-tuple-element.35), channel_id=1, source_target_pairs={{0,0},{64,1},{1,2},{65,3},{4,4},{68,5},{5,6},{69,7},{8,8},{72,9},{... | collective-permute-start | bytes 147464 | tf_op jit(solution)/shard_map/ppermute | solution.py:406
  139.5 1.9 %collective-permute-start.18 = (bf16[96,256]{1,0:T(8,128)(2,1)S(1)}, bf16[96,256]{1,0:T(8,128)(2,1)S(1)}, u32[]{:S(2)}, u32[]{:S(2)}) collective-permute-start(bf16[96,256]{1,0:T(8,128)(2,1)S(1)} %get-tuple-element.36), channel_id=1, source_target_pairs={{64,0},{1,1},{65,2},{0,3},{68,4},{5,5},{69,6},{4,7},{72,8},{9,9},{... | collective-permute-start | bytes 147464 | tf_op jit(solution)/shard_map/ppermute | solution.py:406
  141.4 2.2 %collective-permute-start.19 = (bf16[96,256]{1,0:T(8,128)(2,1)S(1)}, bf16[96,256]{1,0:T(8,128)(2,1)S(1)}, u32[]{:S(2)}, u32[]{:S(2)}) collective-permute-start(bf16[96,256]{1,0:T(8,128)(2,1)S(1)} %get-tuple-element.37), channel_id=1, source_target_pairs={{1,0},{65,1},{0,2},{64,3},{5,4},{69,5},{4,6},{68,7},{9,8},{73,9},{... | collective-permute-start | bytes 147464 | tf_op jit(solution)/shard_map/ppermute | solution.py:406
  143.6 2.1 %collective-permute-start.20 = (bf16[96,256]{1,0:T(8,128)(2,1)S(1)}, bf16[96,256]{1,0:T(8,128)(2,1)S(1)}, u32[]{:S(2)}, u32[]{:S(2)}) collective-permute-start(bf16[96,256]{1,0:T(8,128)(2,1)S(1)} %get-tuple-element.38), channel_id=1, source_target_pairs={{65,0},{0,1},{64,2},{1,3},{69,4},{4,5},{68,6},{5,7},{73,8},{8,9},{... | collective-permute-start | bytes 147464 | tf_op jit(solution)/shard_map/ppermute | solution.py:406
  145.7 1.3 collective-permute-done.19.refs_2_
  147.1 4.2 %collective-permute-done.20.refs_3_ = bf16[96,256]{1,0:T(8,128)(2,1)S(1)} collective-permute-done((bf16[96,256]{1,0:T(8,128)(2,1)S(1)}, bf16[96,256]{1,0:T(8,128)(2,1)S(1)}, u32[]{:S(2)}, u32[]{:S(2)}) %collective-permute-start.20) | collective-permute-done | bytes 49184 | tf_op jit(solution)/shard_map/ppermute | solution.py:406
  152.1 3.1 %all-to-all-done.1 = bf16[16,24,1728]{2,1,0:T(8,128)(2,1)} async-done(((bf16[16,24,1728]{2,1,0:T(8,128)(2,1)}), bf16[16,24,1728]{2,1,0:T(8,128)(2,1)}, u32[]{:S(2)}, u32[]{:S(2)}) %all-to-all-start.1) | async-done | bytes 1327136 | tf_op jit(solution)/shard_map/all_to_all | solution.py:412
  155.1 1.5 reduce_sum.12
  156.7 3.2 %collective-permute-start.22 = (bf16[12,1728]{1,0:T(8,128)(2,1)S(1)}, bf16[12,1728]{1,0:T(8,128)(2,1)S(1)}, u32[]{:S(2)}, u32[]{:S(2)}) collective-permute-start(bf16[12,1728]{1,0:T(8,128)(2,1)S(1)} %get-tuple-element.48), channel_id=1, source_target_pairs={{1,0},{0,1},{5,2},{4,3},{9,4},{8,5},{13,6},{12,7},{65,8},{64,9},{6... | collective-permute-start | bytes 124424 | tf_op jit(solution)/shard_map/ppermute | solution.py:417
  159.9 7.8 %collective-permute-start.23 = (bf16[12,1728]{1,0:T(8,128)(2,1)S(1)}, bf16[12,1728]{1,0:T(8,128)(2,1)S(1)}, u32[]{:S(2)}, u32[]{:S(2)}) collective-permute-start(bf16[12,1728]{1,0:T(8,128)(2,1)S(1)} %get-tuple-element.49), channel_id=1, source_target_pairs={{0,0},{1,1},{4,2},{5,3},{8,4},{9,5},{12,6},{13,7},{64,8},{65,9},{6... | collective-permute-start | bytes 124424 | tf_op jit(solution)/shard_map/ppermute | solution.py:416
  167.7 3.1 %collective-permute-done.22 = bf16[12,1728]{1,0:T(8,128)(2,1)S(1)} collective-permute-done((bf16[12,1728]{1,0:T(8,128)(2,1)S(1)}, bf16[12,1728]{1,0:T(8,128)(2,1)S(1)}, u32[]{:S(2)}, u32[]{:S(2)}) %collective-permute-start.22) | collective-permute-done | bytes 41504 | tf_op jit(solution)/shard_map/ppermute | solution.py:417
  170.8 1.3 collective-permute-done.23
  173.4 0.7 select_convert_fusion
  (44 shorter events, 5.9 us)
Async XLA Ops:
  2.7 12.0 %collective-permute-start.5 = (bf16[12,1728]{1,0:T(8,128)(2,1)S(1)}, bf16[12,1728]{1,0:T(8,128)(2,1)S(1)}, u32[]{:S(2)}, u32[]{:S(2)}) collective-permute-start(bf16[12,1728]{1,0:T(8,128)(2,1)S(1)} %select_n.103), channel_id=1, source_target_pairs={{0,1},{1,0},{2,5},{3,4},{4,9},{5,8},{6,13},{7,12},{8,65},{9,64},{1... | collective-permute-start | bytes 124424 | tf_op jit(solution)/shard_map/ppermute | solution.py:349
  9.8 8.6 %collective-permute-start.6 = (bf16[12,1728]{1,0:T(8,128)(2,1)S(1)}, bf16[12,1728]{1,0:T(8,128)(2,1)S(1)}, u32[]{:S(2)}, u32[]{:S(2)}) collective-permute-start(bf16[12,1728]{1,0:T(8,128)(2,1)S(1)} %select_n.105), channel_id=1, source_target_pairs={{0,0},{1,1},{2,4},{3,5},{4,8},{5,9},{6,12},{7,13},{8,64},{9,65},{1... | collective-permute-start | bytes 124424 | tf_op jit(solution)/shard_map/ppermute | solution.py:348
  19.7 3.8 %copy-start.1 = (bf16[256,384]{1,0:T(8,128)(2,1)S(1)}, bf16[256,384]{1,0:T(8,128)(2,1)}, u32[]{:S(2)}) copy-start(bf16[256,384]{1,0:T(8,128)(2,1)} %param.3) | copy-start | bytes 589828
  19.7 7.7 %copy-start = (s32[2,2]{1,0:T(2,128)S(1)}, s32[2,2]{1,0:T(2,128)}, u32[]{:S(2)}) copy-start(s32[2,2]{1,0:T(2,128)} %param.5) | copy-start | bytes 52
  19.7 72.1 %all-to-all-start = ((bf16[16,24,1728]{2,1,0:T(8,128)(2,1)}), bf16[16,24,1728]{2,1,0:T(8,128)(2,1)S(1)}, u32[]{:S(2)}, u32[]{:S(2)}) async-start(bf16[16,24,1728]{2,1,0:T(8,128)(2,1)} %broadcast_in_dim.3), calls=%async_computation | async-start | bytes 2752512 | tf_op jit(solution)/shard_map/all_to_all | solution.py:354
  23.5 7.9 %collective-permute-start = (bf16[256,384]{1,0:T(8,128)(2,1)S(1)}, bf16[256,384]{1,0:T(8,128)(2,1)S(1)}, u32[]{:S(2)}, u32[]{:S(2)}) collective-permute-start(bf16[256,384]{1,0:T(8,128)(2,1)S(1)} %copy-done.1), channel_id=1, source_target_pairs={{0,1},{1,2},{2,3},{3,4},{4,5},{5,6},{6,7},{7,8},{8,9},{9,10},{10,1... | collective-permute-start | bytes 589832 | tf_op jit(solution)/shard_map/ppermute | solution.py:74
  32.2 43.1 %collective-permute-start.1 = (bf16[96,256]{1,0:T(8,128)(2,1)S(1)}, bf16[96,256]{1,0:T(8,128)(2,1)S(1)}, u32[]{:S(2)}, u32[]{:S(2)}) collective-permute-start(bf16[96,256]{1,0:T(8,128)(2,1)S(1)} %get-tuple-element.21), channel_id=1, source_target_pairs={{0,0},{1,64},{2,1},{3,65},{4,4},{5,68},{6,5},{7,69},{8,8},{9,72},{... | collective-permute-start | bytes 147464 | tf_op jit(solution)/shard_map/ppermute | solution.py:360
  37.7 37.5 %collective-permute-start.2 = (bf16[96,256]{1,0:T(8,128)(2,1)S(1)}, bf16[96,256]{1,0:T(8,128)(2,1)S(1)}, u32[]{:S(2)}, u32[]{:S(2)}) collective-permute-start(bf16[96,256]{1,0:T(8,128)(2,1)S(1)} %get-tuple-element.22), channel_id=1, source_target_pairs={{0,64},{1,1},{2,65},{3,0},{4,68},{5,5},{6,69},{7,4},{8,72},{9,9},{... | collective-permute-start | bytes 147464 | tf_op jit(solution)/shard_map/ppermute | solution.py:360
  39.7 35.6 %collective-permute-start.3 = (bf16[96,256]{1,0:T(8,128)(2,1)S(1)}, bf16[96,256]{1,0:T(8,128)(2,1)S(1)}, u32[]{:S(2)}, u32[]{:S(2)}) collective-permute-start(bf16[96,256]{1,0:T(8,128)(2,1)S(1)} %get-tuple-element.23), channel_id=1, source_target_pairs={{0,1},{1,65},{2,0},{3,64},{4,5},{5,69},{6,4},{7,68},{8,9},{9,73},{... | collective-permute-start | bytes 147464 | tf_op jit(solution)/shard_map/ppermute | solution.py:360
  70.7 6.3 %collective-permute-start.4 = (bf16[96,256]{1,0:T(8,128)(2,1)S(1)}, bf16[96,256]{1,0:T(8,128)(2,1)S(1)}, u32[]{:S(2)}, u32[]{:S(2)}) collective-permute-start(bf16[96,256]{1,0:T(8,128)(2,1)S(1)} %get-tuple-element.24), channel_id=1, source_target_pairs={{0,65},{1,0},{2,64},{3,1},{4,69},{5,4},{6,68},{7,5},{8,73},{9,8},{... | collective-permute-start | bytes 147464 | tf_op jit(solution)/shard_map/ppermute | solution.py:360
  77.8 5.7 %collective-permute-start.7 = (bf16[96,1024]{1,0:T(8,128)(2,1)S(1)}, bf16[96,1024]{1,0:T(8,128)(2,1)S(1)}, u32[]{:S(2)}, u32[]{:S(2)}) collective-permute-start(bf16[96,1024]{1,0:T(8,128)(2,1)S(1)} %get-tuple-element.26.a0), channel_id=1, source_target_pairs={{0,1},{1,2},{2,3},{3,0},{4,5},{5,6},{6,7},{7,4},{8,9},{9,10},{10,1... | collective-permute-start | bytes 589832 | tf_op jit(solution)/shard_map/ppermute | solution.py:70
  77.9 10.2 %collective-permute-start.8 = (bf16[96,1024]{1,0:T(8,128)(2,1)S(1)}, bf16[96,1024]{1,0:T(8,128)(2,1)S(1)}, u32[]{:S(2)}, u32[]{:S(2)}) collective-permute-start(bf16[96,1024]{1,0:T(8,128)(2,1)S(1)} %get-tuple-element.26.a0), channel_id=1, source_target_pairs={{0,2},{1,3},{2,0},{3,1},{4,6},{5,7},{6,4},{7,5},{8,10},{9,11},{10,... | collective-permute-start | bytes 589832 | tf_op jit(solution)/shard_map/ppermute | solution.py:70
  79.5 12.3 %collective-permute-start.9 = (bf16[96,1024]{1,0:T(8,128)(2,1)S(1)}, bf16[96,1024]{1,0:T(8,128)(2,1)S(1)}, u32[]{:S(2)}, u32[]{:S(2)}) collective-permute-start(bf16[96,1024]{1,0:T(8,128)(2,1)S(1)} %get-tuple-element.26.a0), channel_id=1, source_target_pairs={{0,3},{1,0},{2,1},{3,2},{4,7},{5,4},{6,5},{7,6},{8,11},{9,8},{10,9... | collective-permute-start | bytes 589832 | tf_op jit(solution)/shard_map/ppermute | solution.py:70
  94.6 1.8 %collective-permute-start.10 = (f32[96,1024]{1,0:T(8,128)S(1)}, f32[96,1024]{1,0:T(8,128)S(1)}, u32[]{:S(2)}, u32[]{:S(2)}) collective-permute-start(f32[96,1024]{1,0:T(8,128)S(1)} %get-tuple-element.28), channel_id=1, source_target_pairs={{0,64},{64,0},{1,65},{65,1},{2,66},{66,2},{3,67},{67,3},{4,68},{68... | collective-permute-start | bytes 1179656 | tf_op jit(solution)/shard_map/ppermute | solution.py:66
  94.7 9.4 %collective-permute-start.12 = (bf16[96,1024]{1,0:T(8,128)(2,1)S(1)}, bf16[96,1024]{1,0:T(8,128)(2,1)S(1)}, u32[]{:S(2)}, u32[]{:S(2)}) collective-permute-start(bf16[96,1024]{1,0:T(8,128)(2,1)S(1)} %get-tuple-element.25.x), channel_id=1, source_target_pairs={{0,128},{128,0},{1,129},{129,1},{2,130},{130,2},{3,131},{131,3},{4... | collective-permute-start | bytes 589832 | tf_op jit(solution)/shard_map/ppermute | solution.py:66
  97.0 10.7 %collective-permute-start.11 = (bf16[96,1024]{1,0:T(8,128)(2,1)S(1)}, bf16[96,1024]{1,0:T(8,128)(2,1)S(1)}, u32[]{:S(2)}, u32[]{:S(2)}) collective-permute-start(bf16[96,1024]{1,0:T(8,128)(2,1)S(1)} %shard_map.53.mine), channel_id=1, source_target_pairs={{0,128},{128,0},{1,129},{129,1},{2,130},{130,2},{3,131},{131,3},{4... | collective-permute-start | bytes 589832 | tf_op jit(solution)/shard_map/ppermute | solution.py:66
  108.7 1.5 collective-permute-start.13
  114.5 40.6 %all-to-all-start.1 = ((bf16[16,24,1728]{2,1,0:T(8,128)(2,1)}), bf16[16,24,1728]{2,1,0:T(8,128)(2,1)}, u32[]{:S(2)}, u32[]{:S(2)}) async-start(bf16[16,24,1728]{2,1,0:T(8,128)(2,1)} %bitcast.5), calls=%async_computation.1 | async-start | bytes 2752512 | tf_op jit(solution)/shard_map/all_to_all | solution.py:412
  123.9 7.3 %collective-permute-start.14 = (bf16[96,1024]{1,0:T(8,128)(2,1)S(1)}, bf16[96,1024]{1,0:T(8,128)(2,1)S(1)}, u32[]{:S(2)}, u32[]{:S(2)}) collective-permute-start(bf16[96,1024]{1,0:T(8,128)(2,1)S(1)} %get-tuple-element.32), channel_id=1, source_target_pairs={{0,1},{1,2},{2,3},{3,0},{4,5},{5,6},{6,7},{7,4},{8,9},{9,10},{10,1... | collective-permute-start | bytes 589832 | tf_op jit(solution)/shard_map/ppermute | solution.py:70
  125.4 10.2 %collective-permute-start.15 = (bf16[96,1024]{1,0:T(8,128)(2,1)S(1)}, bf16[96,1024]{1,0:T(8,128)(2,1)S(1)}, u32[]{:S(2)}, u32[]{:S(2)}) collective-permute-start(bf16[96,1024]{1,0:T(8,128)(2,1)S(1)} %get-tuple-element.33), channel_id=1, source_target_pairs={{0,2},{1,3},{2,0},{3,1},{4,6},{5,7},{6,4},{7,5},{8,10},{9,11},{10,... | collective-permute-start | bytes 589832 | tf_op jit(solution)/shard_map/ppermute | solution.py:70
  126.7 10.0 %collective-permute-start.16 = (bf16[96,1024]{1,0:T(8,128)(2,1)S(1)}, bf16[96,1024]{1,0:T(8,128)(2,1)S(1)}, u32[]{:S(2)}, u32[]{:S(2)}) collective-permute-start(bf16[96,1024]{1,0:T(8,128)(2,1)S(1)} %get-tuple-element.34), channel_id=1, source_target_pairs={{0,3},{1,0},{2,1},{3,2},{4,7},{5,4},{6,5},{7,6},{8,11},{9,8},{10,9... | collective-permute-start | bytes 589832 | tf_op jit(solution)/shard_map/ppermute | solution.py:70
  137.5 8.2 %collective-permute-start.17 = (bf16[96,256]{1,0:T(8,128)(2,1)S(1)}, bf16[96,256]{1,0:T(8,128)(2,1)S(1)}, u32[]{:S(2)}, u32[]{:S(2)}) collective-permute-start(bf16[96,256]{1,0:T(8,128)(2,1)S(1)} %get-tuple-element.35), channel_id=1, source_target_pairs={{0,0},{64,1},{1,2},{65,3},{4,4},{68,5},{5,6},{69,7},{8,8},{72,9},{... | collective-permute-start | bytes 147464 | tf_op jit(solution)/shard_map/ppermute | solution.py:406
  139.5 6.2 %collective-permute-start.18 = (bf16[96,256]{1,0:T(8,128)(2,1)S(1)}, bf16[96,256]{1,0:T(8,128)(2,1)S(1)}, u32[]{:S(2)}, u32[]{:S(2)}) collective-permute-start(bf16[96,256]{1,0:T(8,128)(2,1)S(1)} %get-tuple-element.36), channel_id=1, source_target_pairs={{64,0},{1,1},{65,2},{0,3},{68,4},{5,5},{69,6},{4,7},{72,8},{9,9},{... | collective-permute-start | bytes 147464 | tf_op jit(solution)/shard_map/ppermute | solution.py:406
  141.4 5.7 %collective-permute-start.19 = (bf16[96,256]{1,0:T(8,128)(2,1)S(1)}, bf16[96,256]{1,0:T(8,128)(2,1)S(1)}, u32[]{:S(2)}, u32[]{:S(2)}) collective-permute-start(bf16[96,256]{1,0:T(8,128)(2,1)S(1)} %get-tuple-element.37), channel_id=1, source_target_pairs={{1,0},{65,1},{0,2},{64,3},{5,4},{69,5},{4,6},{68,7},{9,8},{73,9},{... | collective-permute-start | bytes 147464 | tf_op jit(solution)/shard_map/ppermute | solution.py:406
  143.6 7.7 %collective-permute-start.20 = (bf16[96,256]{1,0:T(8,128)(2,1)S(1)}, bf16[96,256]{1,0:T(8,128)(2,1)S(1)}, u32[]{:S(2)}, u32[]{:S(2)}) collective-permute-start(bf16[96,256]{1,0:T(8,128)(2,1)S(1)} %get-tuple-element.38), channel_id=1, source_target_pairs={{65,0},{0,1},{64,2},{1,3},{69,4},{4,5},{68,6},{5,7},{73,8},{8,9},{... | collective-permute-start | bytes 147464 | tf_op jit(solution)/shard_map/ppermute | solution.py:406
  152.0 15.7 %collective-permute-start.21 = (bf16[256,384]{1,0:T(8,128)(2,1)S(1)}, bf16[256,384]{1,0:T(8,128)(2,1)S(1)}, u32[]{:S(2)}, u32[]{:S(2)}) collective-permute-start(bf16[256,384]{1,0:T(8,128)(2,1)S(1)} %shard_map.57), channel_id=1, source_target_pairs={{0,63},{1,0},{2,1},{3,2},{4,3},{5,4},{6,5},{7,6},{8,7},{9,8},{10,9... | collective-permute-start | bytes 589832 | tf_op jit(solution)/shard_map/ppermute | solution.py:74
  156.7 14.1 %collective-permute-start.22 = (bf16[12,1728]{1,0:T(8,128)(2,1)S(1)}, bf16[12,1728]{1,0:T(8,128)(2,1)S(1)}, u32[]{:S(2)}, u32[]{:S(2)}) collective-permute-start(bf16[12,1728]{1,0:T(8,128)(2,1)S(1)} %get-tuple-element.48), channel_id=1, source_target_pairs={{1,0},{0,1},{5,2},{4,3},{9,4},{8,5},{13,6},{12,7},{65,8},{64,9},{6... | collective-permute-start | bytes 124424 | tf_op jit(solution)/shard_map/ppermute | solution.py:417
  159.9 12.2 %collective-permute-start.23 = (bf16[12,1728]{1,0:T(8,128)(2,1)S(1)}, bf16[12,1728]{1,0:T(8,128)(2,1)S(1)}, u32[]{:S(2)}, u32[]{:S(2)}) collective-permute-start(bf16[12,1728]{1,0:T(8,128)(2,1)S(1)} %get-tuple-element.49), channel_id=1, source_target_pairs={{0,0},{1,1},{4,2},{5,3},{8,4},{9,5},{12,6},{13,7},{64,8},{65,9},{6... | collective-permute-start | bytes 124424 | tf_op jit(solution)/shard_map/ppermute | solution.py:416

commit v5 on v3

--- a/solution.py
+++ b/solution.py
@@ -342,8 +342,12 @@
     own32 = ((OWN, PIX), F32)
 
     cut = conv_weight.reshape(12, TAPS, 4, OWN)
-    low = jnp.where(xh == 0, cut[:, :, 0:2], cut[:, :, 0::2]).reshape(12, LANES)
-    high = jnp.where(xh == 0, cut[:, :, 2:4], cut[:, :, 1::2]).reshape(12, LANES)
+    inner = [
+        jnp.where(xh == 0, cut[:, :, 1:2], cut[:, :, 2:3]),
+        jnp.where(xh == 0, cut[:, :, 2:3], cut[:, :, 1:2]),
+    ]
+    low = jnp.concatenate([cut[:, :, 0:1], inner[0]], axis=2).reshape(12, LANES)
+    high = jnp.concatenate([inner[1], cut[:, :, 3:4]], axis=2).reshape(12, LANES)
     odd = y % 2 == 1
     got = [
         lax.ppermute(jnp.where(odd, high, low), AX, weight_pairs(0)),
@@ -410,7 +414,10 @@
     )
 
     shares = lax.all_to_all(dw.reshape(16, 24, LANES), WEIGHT_GROUP, 0, 0, tiled=True)
-    total = jnp.sum(shares.astype(F32), axis=0).astype(BF16)
+    total = shares[0].astype(F32)
+    for k in range(1, 16):
+        total = total + shares[k].astype(F32)
+    total = total.astype(BF16)
     first, second = total[:12], total[12:]
     low_high = [
         lax.ppermute(jnp.where(flip, second, first), AX, back(weight_pairs(0))),
@@ -418,9 +425,12 @@
     ]
     low = jnp.where(odd, low_high[1], low_high[0]).reshape(12, TAPS, 2, OWN)
     high = jnp.where(odd, low_high[0], low_high[1]).reshape(12, TAPS, 2, OWN)
-    apart = jnp.concatenate([low, high], axis=2)
-    woven = jnp.stack([low, high], axis=3).reshape(12, TAPS, 4, OWN)
-    grad_weight = jnp.where(xh == 0, apart, woven).reshape(12, TAPS, QUAD).astype(F32)
+    inner = [
+        jnp.where(xh == 0, low[:, :, 1:2], high[:, :, 0:1]),
+        jnp.where(xh == 0, high[:, :, 0:1], low[:, :, 1:2]),
+    ]
+    chunks = [low[:, :, 0:1], inner[0], inner[1], high[:, :, 1:2]]
+    grad_weight = jnp.concatenate(chunks, axis=2).reshape(12, TAPS, QUAD).astype(F32)
     return results, grad_weight
 
 

time: 173 us -> 172 us (level)
  no operation moved by 1% of the time
where the time goes in v5:
time: 172 us; the launch traced here: 171 us
  starting transfers between devices  73.7 us (43%)
  waiting for transfers between devices  73.2 us (43%)
  Pallas kernels  17 us (10%)
  local copies, waits for them, and re-layouts  3.91 us (2%)
  other arithmetic  2.65 us (2%)
    ppermute x4, waiting for transfers between devices, step(): lax.ppermute(b, AX, pixel_pairs(v, 0))  30.6 us
    ppermute x6, waiting for transfers between devices, turn_y(): return lax.ppermute(value, 'y', [(i, (i + d) % 4) for i in range(4)])  17.6 us
    pallas_call x9, Pallas kernels, call(): pl.pallas_call(kernel, out_shape=[jax.ShapeDtypeStruct(s, d) for s, d in...  17 us
    ppermute x4, starting transfers between devices, step(): lax.ppermute(b, AX, back(pixel_pairs(v, 1)))  14.8 us
    ppermute x6, starting transfers between devices, turn_y(): return lax.ppermute(value, 'y', [(i, (i + d) % 4) for i in range(4)])  13.4 us
    ppermute x4, waiting for transfers between devices, swap(): return lax.ppermute(value, axis, [(0, 1), (1, 0)])  10.6 us
    ppermute x1, starting transfers between devices, step(): lax.ppermute(jnp.where(odd, low, high), AX, weight_pairs(1))  8.15 us
    ppermute x4, starting transfers between devices, step(): lax.ppermute(b, AX, pixel_pairs(v, 0))  7.89 us
  transfers between devices with their start and end apart: 25, of which 13 were waited for; matrix products, arithmetic and copies ran while one was open for 1% of the time, Pallas kernels for 5%

profile of v5, /device:TPU:21, one launch (start us, length us, event | category | flops | bytes accessed | tf_op | source)
XLA Modules:
  0.0 171.5 jit_solution(10128314947416385799)
XLA Ops:
  0.6 1.0 reshape.65
  2.4 8.1 %collective-permute-start.5 = (bf16[12,1728]{1,0:T(8,128)(2,1)S(1)}, bf16[12,1728]{1,0:T(8,128)(2,1)S(1)}, u32[]{:S(2)}, u32[]{:S(2)}) collective-permute-start(bf16[12,1728]{1,0:T(8,128)(2,1)S(1)} %select_n.107), channel_id=1, source_target_pairs={{0,1},{1,0},{2,5},{3,4},{4,9},{5,8},{6,13},{7,12},{8,65},{9,64},{1... | collective-permute-start | bytes 124424 | tf_op jit(solution)/shard_map/ppermute | solution.py:354
  10.7 5.1 %collective-permute-start.6 = (bf16[12,1728]{1,0:T(8,128)(2,1)S(1)}, bf16[12,1728]{1,0:T(8,128)(2,1)S(1)}, u32[]{:S(2)}, u32[]{:S(2)}) collective-permute-start(bf16[12,1728]{1,0:T(8,128)(2,1)S(1)} %select_n.109), channel_id=1, source_target_pairs={{0,0},{1,1},{2,4},{3,5},{4,8},{5,9},{6,12},{7,13},{8,64},{9,65},{1... | collective-permute-start | bytes 124424 | tf_op jit(solution)/shard_map/ppermute | solution.py:353
  15.9 3.7 %collective-permute-done.6 = bf16[12,1728]{1,0:T(8,128)(2,1)S(1)} collective-permute-done((bf16[12,1728]{1,0:T(8,128)(2,1)S(1)}, bf16[12,1728]{1,0:T(8,128)(2,1)S(1)}, u32[]{:S(2)}, u32[]{:S(2)}) %collective-permute-start.6) | collective-permute-done | bytes 41504 | tf_op jit(solution)/shard_map/ppermute | solution.py:353
  19.7 1.2 broadcast_in_dim.3
  20.9 3.8 %all-to-all-start = ((bf16[16,24,1728]{2,1,0:T(8,128)(2,1)}), bf16[16,24,1728]{2,1,0:T(8,128)(2,1)S(1)}, u32[]{:S(2)}, u32[]{:S(2)}) async-start(bf16[16,24,1728]{2,1,0:T(8,128)(2,1)} %broadcast_in_dim.3), calls=%async_computation | async-start | bytes 2752512 | tf_op jit(solution)/shard_map/all_to_all | solution.py:359
  24.7 1.9 %collective-permute-start = (bf16[256,384]{1,0:T(8,128)(2,1)S(1)}, bf16[256,384]{1,0:T(8,128)(2,1)S(1)}, u32[]{:S(2)}, u32[]{:S(2)}) collective-permute-start(bf16[256,384]{1,0:T(8,128)(2,1)S(1)} %copy-done.1), channel_id=1, source_target_pairs={{0,1},{1,2},{2,3},{3,4},{4,5},{5,6},{6,7},{7,8},{8,9},{9,10},{10,1... | collective-permute-start | bytes 589832 | tf_op jit(solution)/shard_map/ppermute | solution.py:361
  26.7 5.8 %collective-permute-done.x_ref = bf16[256,384]{1,0:T(8,128)(2,1)S(1)} collective-permute-done((bf16[256,384]{1,0:T(8,128)(2,1)S(1)}, bf16[256,384]{1,0:T(8,128)(2,1)S(1)}, u32[]{:S(2)}, u32[]{:S(2)}) %collective-permute-start) | collective-permute-done | bytes 196640 | tf_op jit(solution)/shard_map/ppermute | solution.py:361
  32.5 0.7 shard_map.50
  33.2 5.2 %collective-permute-start.1 = (bf16[96,256]{1,0:T(8,128)(2,1)S(1)}, bf16[96,256]{1,0:T(8,128)(2,1)S(1)}, u32[]{:S(2)}, u32[]{:S(2)}) collective-permute-start(bf16[96,256]{1,0:T(8,128)(2,1)S(1)} %get-tuple-element.21), channel_id=1, source_target_pairs={{0,0},{1,64},{2,1},{3,65},{4,4},{5,68},{6,5},{7,69},{8,8},{9,72},{... | collective-permute-start | bytes 147464 | tf_op jit(solution)/shard_map/ppermute | solution.py:365
  38.4 1.9 %collective-permute-start.2 = (bf16[96,256]{1,0:T(8,128)(2,1)S(1)}, bf16[96,256]{1,0:T(8,128)(2,1)S(1)}, u32[]{:S(2)}, u32[]{:S(2)}) collective-permute-start(bf16[96,256]{1,0:T(8,128)(2,1)S(1)} %get-tuple-element.22), channel_id=1, source_target_pairs={{0,64},{1,1},{2,65},{3,0},{4,68},{5,5},{6,69},{7,4},{8,72},{9,9},{... | collective-permute-start | bytes 147464 | tf_op jit(solution)/shard_map/ppermute | solution.py:365
  40.5 0.7 collective-permute-start.4
  41.1 30.6 %collective-permute-done.2.refs_1_ = bf16[96,256]{1,0:T(8,128)(2,1)S(1)} collective-permute-done((bf16[96,256]{1,0:T(8,128)(2,1)S(1)}, bf16[96,256]{1,0:T(8,128)(2,1)S(1)}, u32[]{:S(2)}, u32[]{:S(2)}) %collective-permute-start.2) | collective-permute-done | bytes 49184 | tf_op jit(solution)/shard_map/ppermute | solution.py:365
  71.8 0.8 shard_map.51
  72.6 6.0 %collective-permute-start.7 = (bf16[96,1024]{1,0:T(8,128)(2,1)S(1)}, bf16[96,1024]{1,0:T(8,128)(2,1)S(1)}, u32[]{:S(2)}, u32[]{:S(2)}) collective-permute-start(bf16[96,1024]{1,0:T(8,128)(2,1)S(1)} %get-tuple-element.26.a0), channel_id=1, source_target_pairs={{0,1},{1,2},{2,3},{3,0},{4,5},{5,6},{6,7},{7,4},{8,9},{9,10},{10,1... | collective-permute-start | bytes 589832 | tf_op jit(solution)/shard_map/ppermute | solution.py:74
  78.6 2.7 %collective-permute-start.8 = (bf16[96,1024]{1,0:T(8,128)(2,1)S(1)}, bf16[96,1024]{1,0:T(8,128)(2,1)S(1)}, u32[]{:S(2)}, u32[]{:S(2)}) collective-permute-start(bf16[96,1024]{1,0:T(8,128)(2,1)S(1)} %get-tuple-element.26.a0), channel_id=1, source_target_pairs={{0,2},{1,3},{2,0},{3,1},{4,6},{5,7},{6,4},{7,5},{8,10},{9,11},{10,... | collective-permute-start | bytes 589832 | tf_op jit(solution)/shard_map/ppermute | solution.py:74
  81.3 2.0 %collective-permute-start.9 = (bf16[96,1024]{1,0:T(8,128)(2,1)S(1)}, bf16[96,1024]{1,0:T(8,128)(2,1)S(1)}, u32[]{:S(2)}, u32[]{:S(2)}) collective-permute-start(bf16[96,1024]{1,0:T(8,128)(2,1)S(1)} %get-tuple-element.26.a0), channel_id=1, source_target_pairs={{0,3},{1,0},{2,1},{3,2},{4,7},{5,4},{6,5},{7,6},{8,11},{9,8},{10,9... | collective-permute-start | bytes 589832 | tf_op jit(solution)/shard_map/ppermute | solution.py:74
  83.3 5.9 %collective-permute-done.8.a2 = bf16[96,1024]{1,0:T(8,128)(2,1)S(1)} collective-permute-done((bf16[96,1024]{1,0:T(8,128)(2,1)S(1)}, bf16[96,1024]{1,0:T(8,128)(2,1)S(1)}, u32[]{:S(2)}, u32[]{:S(2)}) %collective-permute-start.8) | collective-permute-done | bytes 196640 | tf_op jit(solution)/shard_map/ppermute | solution.py:74
  89.2 2.4 %collective-permute-done.9.a3 = bf16[96,1024]{1,0:T(8,128)(2,1)S(1)} collective-permute-done((bf16[96,1024]{1,0:T(8,128)(2,1)S(1)}, bf16[96,1024]{1,0:T(8,128)(2,1)S(1)}, u32[]{:S(2)}, u32[]{:S(2)}) %collective-permute-start.9) | collective-permute-done | bytes 196640 | tf_op jit(solution)/shard_map/ppermute | solution.py:74
  91.6 2.8 %shard_map.52 = (bf16[384,1024]{1,0:T(8,128)(2,1)S(1)}, f32[96,1024]{1,0:T(8,128)S(1)}, f32[96,1024]{1,0:T(8,128)S(1)}) custom-call(s32[6]{0:T(128)S(1)} %stack.19.prm, bf16[384,1728]{1,0:T(8,128)(2,1)S(1)} %bitcast.19, bf16[96,1024]{1,0:T(8,128)(2,1)S(1)} %get-tuple-element.26.a0, bf16[96,1024]{1,0:T(8,128)(2,1)S(1)} %collective-permute-done.7.a1, ...), custom_call_target="tpu_custom_call" | custom-call | tf_op jit(solution)/shard_map/pallas_call | solution.py:324
  94.5 0.7 collective-permute-start.10
  95.2 1.3 collective-permute-done.10.got
  96.5 0.6 shard_map.53.mine
  97.2 1.9 %collective-permute-start.11 = (bf16[96,1024]{1,0:T(8,128)(2,1)S(1)}, bf16[96,1024]{1,0:T(8,128)(2,1)S(1)}, u32[]{:S(2)}, u32[]{:S(2)}) collective-permute-start(bf16[96,1024]{1,0:T(8,128)(2,1)S(1)} %shard_map.53.mine), channel_id=1, source_target_pairs={{0,128},{128,0},{1,129},{129,1},{2,130},{130,2},{3,131},{131,3},{4... | collective-permute-start | bytes 589832 | tf_op jit(solution)/shard_map/ppermute | solution.py:70
  99.1 4.0 %collective-permute-done.12.g = bf16[96,1024]{1,0:T(8,128)(2,1)S(1)} collective-permute-done((bf16[96,1024]{1,0:T(8,128)(2,1)S(1)}, bf16[96,1024]{1,0:T(8,128)(2,1)S(1)}, u32[]{:S(2)}, u32[]{:S(2)}) %collective-permute-start.12) | collective-permute-done | bytes 196640 | tf_op jit(solution)/shard_map/ppermute | solution.py:70
  103.0 4.2 %collective-permute-done.11.theirs = bf16[96,1024]{1,0:T(8,128)(2,1)S(1)} collective-permute-done((bf16[96,1024]{1,0:T(8,128)(2,1)S(1)}, bf16[96,1024]{1,0:T(8,128)(2,1)S(1)}, u32[]{:S(2)}, u32[]{:S(2)}) %collective-permute-start.11) | collective-permute-done | bytes 196640 | tf_op jit(solution)/shard_map/ppermute | solution.py:70
  107.3 0.9 shard_map.54
  108.1 1.0 collective-permute-start.13
  109.2 1.1 collective-permute-done.13.b_other
  110.2 4.2 %shard_map.58 = bf16[384,1728]{1,0:T(8,128)(2,1)} custom-call(s32[6]{0:T(128)S(1)} %stack.19.prm, bf16[384,1024]{1,0:T(8,128)(2,1)S(1)} %get-tuple-element.39.full, bf16[96,1024]{1,0:T(8,128)(2,1)S(1)} %get-tuple-element.30.b_own, bf16[96,1024]{1,0:T(8,128)(2,1)S(1)} %collective-permute-done.13.b_other), custom_call_target="tpu_custom_call" | custom-call | tf_op jit(solution)/shard_map/pallas_call | solution.py:324
  114.5 4.4 %all-to-all-start.1 = ((bf16[16,24,1728]{2,1,0:T(8,128)(2,1)}), bf16[16,24,1728]{2,1,0:T(8,128)(2,1)}, u32[]{:S(2)}, u32[]{:S(2)}) async-start(bf16[16,24,1728]{2,1,0:T(8,128)(2,1)} %bitcast.6), calls=%async_computation.1 | async-start | bytes 2752512 | tf_op jit(solution)/shard_map/all_to_all | solution.py:416
  118.9 4.8 %shard_map.55 = (f32[96,1024]{1,0:T(8,128)S(1)}, bf16[96,1024]{1,0:T(8,128)(2,1)S(1)}, bf16[96,1024]{1,0:T(8,128)(2,1)S(1)}, bf16[96,1024]{1,0:T(8,128)(2,1)S(1)}) custom-call(s32[6]{0:T(128)S(1)} %stack.19.prm, bf16[384,1728]{1,0:T(8,128)(2,1)S(1)} %bitcast.20, bf16[96,1024]{1,0:T(8,128)(2,1)S(1)} %get-tuple-element.30.b_own, ...), custom_call_target="tpu_custom_call" | custom-call | tf_op jit(solution)/shard_map/pallas_call | solution.py:324
  123.6 1.2 collective-permute-start.14
  124.8 1.0 collective-permute-start.15
  126.3 3.5 %collective-permute-done.14.r1 = bf16[96,1024]{1,0:T(8,128)(2,1)S(1)} collective-permute-done((bf16[96,1024]{1,0:T(8,128)(2,1)S(1)}, bf16[96,1024]{1,0:T(8,128)(2,1)S(1)}, u32[]{:S(2)}, u32[]{:S(2)}) %collective-permute-start.14) | collective-permute-done | bytes 196640 | tf_op jit(solution)/shard_map/ppermute | solution.py:74
  129.8 4.7 %collective-permute-done.15.r2 = bf16[96,1024]{1,0:T(8,128)(2,1)S(1)} collective-permute-done((bf16[96,1024]{1,0:T(8,128)(2,1)S(1)}, bf16[96,1024]{1,0:T(8,128)(2,1)S(1)}, u32[]{:S(2)}, u32[]{:S(2)}) %collective-permute-start.15) | collective-permute-done | bytes 196640 | tf_op jit(solution)/shard_map/ppermute | solution.py:74
  134.5 1.1 collective-permute-done.16.r3
  135.6 0.8 shard_map.56
  136.3 2.8 %collective-permute-start.17 = (bf16[96,256]{1,0:T(8,128)(2,1)S(1)}, bf16[96,256]{1,0:T(8,128)(2,1)S(1)}, u32[]{:S(2)}, u32[]{:S(2)}) collective-permute-start(bf16[96,256]{1,0:T(8,128)(2,1)S(1)} %get-tuple-element.35), channel_id=1, source_target_pairs={{64,0},{1,1},{65,2},{4,3},{68,4},{5,5},{69,6},{8,7},{72,8},{9,9},{... | collective-permute-start | bytes 147464 | tf_op jit(solution)/shard_map/ppermute | solution.py:411
  139.1 4.4 %collective-permute-start.18 = (bf16[96,256]{1,0:T(8,128)(2,1)S(1)}, bf16[96,256]{1,0:T(8,128)(2,1)S(1)}, u32[]{:S(2)}, u32[]{:S(2)}) collective-permute-start(bf16[96,256]{1,0:T(8,128)(2,1)S(1)} %get-tuple-element.36), channel_id=1, source_target_pairs={{1,0},{65,1},{0,2},{68,3},{5,4},{69,5},{4,6},{72,7},{9,8},{73,9},{... | collective-permute-start | bytes 147464 | tf_op jit(solution)/shard_map/ppermute | solution.py:411
  143.5 0.7 collective-permute-start.19
  144.2 7.0 %collective-permute-start.20 = (bf16[96,256]{1,0:T(8,128)(2,1)S(1)}, bf16[96,256]{1,0:T(8,128)(2,1)S(1)}, u32[]{:S(2)}, u32[]{:S(2)}) collective-permute-start(bf16[96,256]{1,0:T(8,128)(2,1)S(1)} %get-tuple-element.38), channel_id=1, source_target_pairs={{0,0},{64,1},{1,2},{69,3},{4,4},{68,5},{5,6},{73,7},{8,8},{72,9},{... | collective-permute-start | bytes 147464 | tf_op jit(solution)/shard_map/ppermute | solution.py:411
  151.2 1.6 fusion
  152.8 6.0 %collective-permute-start.21 = (bf16[12,1728]{1,0:T(8,128)(2,1)S(1)}, bf16[12,1728]{1,0:T(8,128)(2,1)S(1)}, u32[]{:S(2)}, u32[]{:S(2)}) collective-permute-start(bf16[12,1728]{1,0:T(8,128)(2,1)S(1)} %get-tuple-element.52), channel_id=1, source_target_pairs={{1,0},{0,1},{5,2},{4,3},{9,4},{8,5},{13,6},{12,7},{65,8},{64,9},{6... | collective-permute-start | bytes 124424 | tf_op jit(solution)/shard_map/ppermute | solution.py:424
  158.8 4.7 %collective-permute-start.22 = (bf16[12,1728]{1,0:T(8,128)(2,1)S(1)}, bf16[12,1728]{1,0:T(8,128)(2,1)S(1)}, u32[]{:S(2)}, u32[]{:S(2)}) collective-permute-start(bf16[12,1728]{1,0:T(8,128)(2,1)S(1)} %get-tuple-element.53), channel_id=1, source_target_pairs={{0,0},{1,1},{4,2},{5,3},{8,4},{9,5},{12,6},{13,7},{64,8},{65,9},{6... | collective-permute-start | bytes 124424 | tf_op jit(solution)/shard_map/ppermute | solution.py:423
  163.5 1.4 shard_map.57
  164.9 4.8 %collective-permute-done.22 = bf16[12,1728]{1,0:T(8,128)(2,1)S(1)} collective-permute-done((bf16[12,1728]{1,0:T(8,128)(2,1)S(1)}, bf16[12,1728]{1,0:T(8,128)(2,1)S(1)}, u32[]{:S(2)}, u32[]{:S(2)}) %collective-permute-start.22) | collective-permute-done | bytes 41504 | tf_op jit(solution)/shard_map/ppermute | solution.py:423
  170.6 0.8 reshape.82
  (36 shorter events, 2.5 us)
Async XLA Ops:
  2.4 13.4 %collective-permute-start.5 = (bf16[12,1728]{1,0:T(8,128)(2,1)S(1)}, bf16[12,1728]{1,0:T(8,128)(2,1)S(1)}, u32[]{:S(2)}, u32[]{:S(2)}) collective-permute-start(bf16[12,1728]{1,0:T(8,128)(2,1)S(1)} %select_n.107), channel_id=1, source_target_pairs={{0,1},{1,0},{2,5},{3,4},{4,9},{5,8},{6,13},{7,12},{8,65},{9,64},{1... | collective-permute-start | bytes 124424 | tf_op jit(solution)/shard_map/ppermute | solution.py:354
  10.7 8.9 %collective-permute-start.6 = (bf16[12,1728]{1,0:T(8,128)(2,1)S(1)}, bf16[12,1728]{1,0:T(8,128)(2,1)S(1)}, u32[]{:S(2)}, u32[]{:S(2)}) collective-permute-start(bf16[12,1728]{1,0:T(8,128)(2,1)S(1)} %select_n.109), channel_id=1, source_target_pairs={{0,0},{1,1},{2,4},{3,5},{4,8},{5,9},{6,12},{7,13},{8,64},{9,65},{1... | collective-permute-start | bytes 124424 | tf_op jit(solution)/shard_map/ppermute | solution.py:353
  20.9 3.8 %copy-start.1 = (bf16[256,384]{1,0:T(8,128)(2,1)S(1)}, bf16[256,384]{1,0:T(8,128)(2,1)}, u32[]{:S(2)}) copy-start(bf16[256,384]{1,0:T(8,128)(2,1)} %param.3) | copy-start | bytes 589828
  20.9 5.7 %copy-start = (s32[2,2]{1,0:T(2,128)S(1)}, s32[2,2]{1,0:T(2,128)}, u32[]{:S(2)}) copy-start(s32[2,2]{1,0:T(2,128)} %param.5) | copy-start | bytes 52
  20.9 70.7 %all-to-all-start = ((bf16[16,24,1728]{2,1,0:T(8,128)(2,1)}), bf16[16,24,1728]{2,1,0:T(8,128)(2,1)S(1)}, u32[]{:S(2)}, u32[]{:S(2)}) async-start(bf16[16,24,1728]{2,1,0:T(8,128)(2,1)} %broadcast_in_dim.3), calls=%async_computation | async-start | bytes 2752512 | tf_op jit(solution)/shard_map/all_to_all | solution.py:359
  24.7 7.8 %collective-permute-start = (bf16[256,384]{1,0:T(8,128)(2,1)S(1)}, bf16[256,384]{1,0:T(8,128)(2,1)S(1)}, u32[]{:S(2)}, u32[]{:S(2)}) collective-permute-start(bf16[256,384]{1,0:T(8,128)(2,1)S(1)} %copy-done.1), channel_id=1, source_target_pairs={{0,1},{1,2},{2,3},{3,4},{4,5},{5,6},{6,7},{7,8},{8,9},{9,10},{10,1... | collective-permute-start | bytes 589832 | tf_op jit(solution)/shard_map/ppermute | solution.py:361
  33.2 7.9 %collective-permute-start.1 = (bf16[96,256]{1,0:T(8,128)(2,1)S(1)}, bf16[96,256]{1,0:T(8,128)(2,1)S(1)}, u32[]{:S(2)}, u32[]{:S(2)}) collective-permute-start(bf16[96,256]{1,0:T(8,128)(2,1)S(1)} %get-tuple-element.21), channel_id=1, source_target_pairs={{0,0},{1,64},{2,1},{3,65},{4,4},{5,68},{6,5},{7,69},{8,8},{9,72},{... | collective-permute-start | bytes 147464 | tf_op jit(solution)/shard_map/ppermute | solution.py:365
  38.4 33.3 %collective-permute-start.2 = (bf16[96,256]{1,0:T(8,128)(2,1)S(1)}, bf16[96,256]{1,0:T(8,128)(2,1)S(1)}, u32[]{:S(2)}, u32[]{:S(2)}) collective-permute-start(bf16[96,256]{1,0:T(8,128)(2,1)S(1)} %get-tuple-element.22), channel_id=1, source_target_pairs={{0,64},{1,1},{2,65},{3,0},{4,68},{5,5},{6,69},{7,4},{8,72},{9,9},{... | collective-permute-start | bytes 147464 | tf_op jit(solution)/shard_map/ppermute | solution.py:365
  40.4 31.4 %collective-permute-start.3 = (bf16[96,256]{1,0:T(8,128)(2,1)S(1)}, bf16[96,256]{1,0:T(8,128)(2,1)S(1)}, u32[]{:S(2)}, u32[]{:S(2)}) collective-permute-start(bf16[96,256]{1,0:T(8,128)(2,1)S(1)} %get-tuple-element.23), channel_id=1, source_target_pairs={{0,1},{1,65},{2,0},{3,64},{4,5},{5,69},{6,4},{7,68},{8,9},{9,73},{... | collective-permute-start | bytes 147464 | tf_op jit(solution)/shard_map/ppermute | solution.py:365
  40.5 31.3 %collective-permute-start.4 = (bf16[96,256]{1,0:T(8,128)(2,1)S(1)}, bf16[96,256]{1,0:T(8,128)(2,1)S(1)}, u32[]{:S(2)}, u32[]{:S(2)}) collective-permute-start(bf16[96,256]{1,0:T(8,128)(2,1)S(1)} %get-tuple-element.24), channel_id=1, source_target_pairs={{0,65},{1,0},{2,64},{3,1},{4,69},{5,4},{6,68},{7,5},{8,73},{9,8},{... | collective-permute-start | bytes 147464 | tf_op jit(solution)/shard_map/ppermute | solution.py:365
  72.6 10.7 %collective-permute-start.7 = (bf16[96,1024]{1,0:T(8,128)(2,1)S(1)}, bf16[96,1024]{1,0:T(8,128)(2,1)S(1)}, u32[]{:S(2)}, u32[]{:S(2)}) collective-permute-start(bf16[96,1024]{1,0:T(8,128)(2,1)S(1)} %get-tuple-element.26.a0), channel_id=1, source_target_pairs={{0,1},{1,2},{2,3},{3,0},{4,5},{5,6},{6,7},{7,4},{8,9},{9,10},{10,1... | collective-permute-start | bytes 589832 | tf_op jit(solution)/shard_map/ppermute | solution.py:74
  78.6 10.6 %collective-permute-start.8 = (bf16[96,1024]{1,0:T(8,128)(2,1)S(1)}, bf16[96,1024]{1,0:T(8,128)(2,1)S(1)}, u32[]{:S(2)}, u32[]{:S(2)}) collective-permute-start(bf16[96,1024]{1,0:T(8,128)(2,1)S(1)} %get-tuple-element.26.a0), channel_id=1, source_target_pairs={{0,2},{1,3},{2,0},{3,1},{4,6},{5,7},{6,4},{7,5},{8,10},{9,11},{10,... | collective-permute-start | bytes 589832 | tf_op jit(solution)/shard_map/ppermute | solution.py:74
  81.3 10.3 %collective-permute-start.9 = (bf16[96,1024]{1,0:T(8,128)(2,1)S(1)}, bf16[96,1024]{1,0:T(8,128)(2,1)S(1)}, u32[]{:S(2)}, u32[]{:S(2)}) collective-permute-start(bf16[96,1024]{1,0:T(8,128)(2,1)S(1)} %get-tuple-element.26.a0), channel_id=1, source_target_pairs={{0,3},{1,0},{2,1},{3,2},{4,7},{5,4},{6,5},{7,6},{8,11},{9,8},{10,9... | collective-permute-start | bytes 589832 | tf_op jit(solution)/shard_map/ppermute | solution.py:74
  94.5 2.1 %collective-permute-start.10 = (f32[96,1024]{1,0:T(8,128)S(1)}, f32[96,1024]{1,0:T(8,128)S(1)}, u32[]{:S(2)}, u32[]{:S(2)}) collective-permute-start(f32[96,1024]{1,0:T(8,128)S(1)} %get-tuple-element.28), channel_id=1, source_target_pairs={{0,64},{64,0},{1,65},{65,1},{2,66},{66,2},{3,67},{67,3},{4,68},{68... | collective-permute-start | bytes 1179656 | tf_op jit(solution)/shard_map/ppermute | solution.py:70
  95.2 7.9 %collective-permute-start.12 = (bf16[96,1024]{1,0:T(8,128)(2,1)S(1)}, bf16[96,1024]{1,0:T(8,128)(2,1)S(1)}, u32[]{:S(2)}, u32[]{:S(2)}) collective-permute-start(bf16[96,1024]{1,0:T(8,128)(2,1)S(1)} %get-tuple-element.25.x), channel_id=1, source_target_pairs={{0,128},{128,0},{1,129},{129,1},{2,130},{130,2},{3,131},{131,3},{4... | collective-permute-start | bytes 589832 | tf_op jit(solution)/shard_map/ppermute | solution.py:70
  97.2 10.1 %collective-permute-start.11 = (bf16[96,1024]{1,0:T(8,128)(2,1)S(1)}, bf16[96,1024]{1,0:T(8,128)(2,1)S(1)}, u32[]{:S(2)}, u32[]{:S(2)}) collective-permute-start(bf16[96,1024]{1,0:T(8,128)(2,1)S(1)} %shard_map.53.mine), channel_id=1, source_target_pairs={{0,128},{128,0},{1,129},{129,1},{2,130},{130,2},{3,131},{131,3},{4... | collective-permute-start | bytes 589832 | tf_op jit(solution)/shard_map/ppermute | solution.py:70
  108.1 2.1 %collective-permute-start.13 = (bf16[96,1024]{1,0:T(8,128)(2,1)S(1)}, bf16[96,1024]{1,0:T(8,128)(2,1)S(1)}, u32[]{:S(2)}, u32[]{:S(2)}) collective-permute-start(bf16[96,1024]{1,0:T(8,128)(2,1)S(1)} %get-tuple-element.30.b_own), channel_id=1, source_target_pairs={{0,64},{64,0},{1,65},{65,1},{2,66},{66,2},{3,67},{67,3},{4,68},{68... | collective-permute-start | bytes 589832 | tf_op jit(solution)/shard_map/ppermute | solution.py:70
  114.5 36.7 %all-to-all-start.1 = ((bf16[16,24,1728]{2,1,0:T(8,128)(2,1)}), bf16[16,24,1728]{2,1,0:T(8,128)(2,1)}, u32[]{:S(2)}, u32[]{:S(2)}) async-start(bf16[16,24,1728]{2,1,0:T(8,128)(2,1)} %bitcast.6), calls=%async_computation.1 | async-start | bytes 2752512 | tf_op jit(solution)/shard_map/all_to_all | solution.py:416
  123.6 6.1 %collective-permute-start.14 = (bf16[96,1024]{1,0:T(8,128)(2,1)S(1)}, bf16[96,1024]{1,0:T(8,128)(2,1)S(1)}, u32[]{:S(2)}, u32[]{:S(2)}) collective-permute-start(bf16[96,1024]{1,0:T(8,128)(2,1)S(1)} %get-tuple-element.32), channel_id=1, source_target_pairs={{0,1},{1,2},{2,3},{3,0},{4,5},{5,6},{6,7},{7,4},{8,9},{9,10},{10,1... | collective-permute-start | bytes 589832 | tf_op jit(solution)/shard_map/ppermute | solution.py:74
  124.8 9.7 %collective-permute-start.15 = (bf16[96,1024]{1,0:T(8,128)(2,1)S(1)}, bf16[96,1024]{1,0:T(8,128)(2,1)S(1)}, u32[]{:S(2)}, u32[]{:S(2)}) collective-permute-start(bf16[96,1024]{1,0:T(8,128)(2,1)S(1)} %get-tuple-element.33), channel_id=1, source_target_pairs={{0,2},{1,3},{2,0},{3,1},{4,6},{5,7},{6,4},{7,5},{8,10},{9,11},{10,... | collective-permute-start | bytes 589832 | tf_op jit(solution)/shard_map/ppermute | solution.py:74
  125.8 9.8 %collective-permute-start.16 = (bf16[96,1024]{1,0:T(8,128)(2,1)S(1)}, bf16[96,1024]{1,0:T(8,128)(2,1)S(1)}, u32[]{:S(2)}, u32[]{:S(2)}) collective-permute-start(bf16[96,1024]{1,0:T(8,128)(2,1)S(1)} %get-tuple-element.34), channel_id=1, source_target_pairs={{0,3},{1,0},{2,1},{3,2},{4,7},{5,4},{6,5},{7,6},{8,11},{9,8},{10,9... | collective-permute-start | bytes 589832 | tf_op jit(solution)/shard_map/ppermute | solution.py:74
  136.3 22.4 %collective-permute-start.17 = (bf16[96,256]{1,0:T(8,128)(2,1)S(1)}, bf16[96,256]{1,0:T(8,128)(2,1)S(1)}, u32[]{:S(2)}, u32[]{:S(2)}) collective-permute-start(bf16[96,256]{1,0:T(8,128)(2,1)S(1)} %get-tuple-element.35), channel_id=1, source_target_pairs={{64,0},{1,1},{65,2},{4,3},{68,4},{5,5},{69,6},{8,7},{72,8},{9,9},{... | collective-permute-start | bytes 147464 | tf_op jit(solution)/shard_map/ppermute | solution.py:411
  139.1 24.3 %collective-permute-start.18 = (bf16[96,256]{1,0:T(8,128)(2,1)S(1)}, bf16[96,256]{1,0:T(8,128)(2,1)S(1)}, u32[]{:S(2)}, u32[]{:S(2)}) collective-permute-start(bf16[96,256]{1,0:T(8,128)(2,1)S(1)} %get-tuple-element.36), channel_id=1, source_target_pairs={{1,0},{65,1},{0,2},{68,3},{5,4},{69,5},{4,6},{72,7},{9,8},{73,9},{... | collective-permute-start | bytes 147464 | tf_op jit(solution)/shard_map/ppermute | solution.py:411
  143.5 20.0 %collective-permute-start.19 = (bf16[96,256]{1,0:T(8,128)(2,1)S(1)}, bf16[96,256]{1,0:T(8,128)(2,1)S(1)}, u32[]{:S(2)}, u32[]{:S(2)}) collective-permute-start(bf16[96,256]{1,0:T(8,128)(2,1)S(1)} %get-tuple-element.37), channel_id=1, source_target_pairs={{65,0},{0,1},{64,2},{5,3},{69,4},{4,5},{68,6},{9,7},{73,8},{8,9},{... | collective-permute-start | bytes 147464 | tf_op jit(solution)/shard_map/ppermute | solution.py:411
  144.2 19.3 %collective-permute-start.20 = (bf16[96,256]{1,0:T(8,128)(2,1)S(1)}, bf16[96,256]{1,0:T(8,128)(2,1)S(1)}, u32[]{:S(2)}, u32[]{:S(2)}) collective-permute-start(bf16[96,256]{1,0:T(8,128)(2,1)S(1)} %get-tuple-element.38), channel_id=1, source_target_pairs={{0,0},{64,1},{1,2},{69,3},{4,4},{68,5},{5,6},{73,7},{8,8},{72,9},{... | collective-permute-start | bytes 147464 | tf_op jit(solution)/shard_map/ppermute | solution.py:411
  152.8 12.1 %collective-permute-start.21 = (bf16[12,1728]{1,0:T(8,128)(2,1)S(1)}, bf16[12,1728]{1,0:T(8,128)(2,1)S(1)}, u32[]{:S(2)}, u32[]{:S(2)}) collective-permute-start(bf16[12,1728]{1,0:T(8,128)(2,1)S(1)} %get-tuple-element.52), channel_id=1, source_target_pairs={{1,0},{0,1},{5,2},{4,3},{9,4},{8,5},{13,6},{12,7},{65,8},{64,9},{6... | collective-permute-start | bytes 124424 | tf_op jit(solution)/shard_map/ppermute | solution.py:424
  158.8 10.9 %collective-permute-start.22 = (bf16[12,1728]{1,0:T(8,128)(2,1)S(1)}, bf16[12,1728]{1,0:T(8,128)(2,1)S(1)}, u32[]{:S(2)}, u32[]{:S(2)}) collective-permute-start(bf16[12,1728]{1,0:T(8,128)(2,1)S(1)} %get-tuple-element.53), channel_id=1, source_target_pairs={{0,0},{1,1},{4,2},{5,3},{8,4},{9,5},{12,6},{13,7},{64,8},{65,9},{6... | collective-permute-start | bytes 124424 | tf_op jit(solution)/shard_map/ppermute | solution.py:423

commit v6 on v5

--- a/solution.py
+++ b/solution.py
@@ -341,13 +341,10 @@
     own = ((OWN, PIX), BF16)
     own32 = ((OWN, PIX), F32)
 
-    cut = conv_weight.reshape(12, TAPS, 4, OWN)
-    inner = [
-        jnp.where(xh == 0, cut[:, :, 1:2], cut[:, :, 2:3]),
-        jnp.where(xh == 0, cut[:, :, 2:3], cut[:, :, 1:2]),
-    ]
-    low = jnp.concatenate([cut[:, :, 0:1], inner[0]], axis=2).reshape(12, LANES)
-    high = jnp.concatenate([inner[1], cut[:, :, 3:4]], axis=2).reshape(12, LANES)
+    cut = [conv_weight[:, :, k * OWN : (k + 1) * OWN] for k in range(4)]
+    inner = [jnp.where(xh == 0, cut[1], cut[2]), jnp.where(xh == 0, cut[2], cut[1])]
+    low = jnp.concatenate([cut[0], inner[0]], axis=2).reshape(12, LANES)
+    high = jnp.concatenate([inner[1], cut[3]], axis=2).reshape(12, LANES)
     odd = y % 2 == 1
     got = [
         lax.ppermute(jnp.where(odd, high, low), AX, weight_pairs(0)),
@@ -423,14 +420,16 @@
         lax.ppermute(jnp.where(flip, second, first), AX, back(weight_pairs(0))),
         lax.ppermute(jnp.where(flip, first, second), AX, back(weight_pairs(1))),
     ]
-    low = jnp.where(odd, low_high[1], low_high[0]).reshape(12, TAPS, 2, OWN)
-    high = jnp.where(odd, low_high[0], low_high[1]).reshape(12, TAPS, 2, OWN)
-    inner = [
-        jnp.where(xh == 0, low[:, :, 1:2], high[:, :, 0:1]),
-        jnp.where(xh == 0, high[:, :, 0:1], low[:, :, 1:2]),
+    low = jnp.where(odd, low_high[1], low_high[0]).reshape(12, TAPS, PAIR)
+    high = jnp.where(odd, low_high[0], low_high[1]).reshape(12, TAPS, PAIR)
+    inner = [low[:, :, OWN:], high[:, :, :OWN]]
+    chunks = [
+        low[:, :, :OWN],
+        jnp.where(xh == 0, inner[0], inner[1]),
+        jnp.where(xh == 0, inner[1], inner[0]),
+        high[:, :, OWN:],
     ]
-    chunks = [low[:, :, 0:1], inner[0], inner[1], high[:, :, 1:2]]
-    grad_weight = jnp.concatenate(chunks, axis=2).reshape(12, TAPS, QUAD).astype(F32)
+    grad_weight = jnp.concatenate(chunks, axis=2).astype(F32)
     return results, grad_weight
 
 

time: 172 us -> 171 us (level)
  no operation moved by 1% of the time
where the time goes in v6:
time: 171 us
  waiting for transfers between devices  73.6 us (43%)
  starting transfers between devices  73.3 us (43%)
  Pallas kernels  17.2 us (10%)
  local copies, waits for them, and re-layouts  3.61 us (2%)
  other arithmetic  2.05 us (1%)
    ppermute x4, waiting for transfers between devices, step(): lax.ppermute(b, AX, pixel_pairs(v, 0))  30.6 us
    ppermute x6, waiting for transfers between devices, turn_y(): return lax.ppermute(value, 'y', [(i, (i + d) % 4) for i in range(4)])  17.7 us
    pallas_call x9, Pallas kernels, call(): pl.pallas_call(kernel, out_shape=[jax.ShapeDtypeStruct(s, d) for s, d in...  17.2 us
    ppermute x4, starting transfers between devices, step(): lax.ppermute(b, AX, back(pixel_pairs(v, 1)))  14.5 us
    ppermute x6, starting transfers between devices, turn_y(): return lax.ppermute(value, 'y', [(i, (i + d) % 4) for i in range(4)])  13.2 us
    ppermute x4, waiting for transfers between devices, swap(): return lax.ppermute(value, axis, [(0, 1), (1, 0)])  10.8 us
    ppermute x1, starting transfers between devices, step(): lax.ppermute(jnp.where(odd, low, high), AX, weight_pairs(1))  8.15 us
    ppermute x4, starting transfers between devices, step(): lax.ppermute(b, AX, pixel_pairs(v, 0))  7.89 us
  transfers between devices with their start and end apart: 25, of which 13 were waited for; matrix products, arithmetic and copies ran while one was open for 1% of the time, Pallas kernels for 5%

profile of v6, /device:TPU:21, one launch (start us, length us, event | category | flops | bytes accessed | tf_op | source)
XLA Modules:
  0.0 170.7 jit_solution(9974297761993627438)
XLA Ops:
  0.6 1.1 fusion.4
  2.0 8.1 %collective-permute-start.5 = (bf16[12,1728]{1,0:T(8,128)(2,1)S(1)}, bf16[12,1728]{1,0:T(8,128)(2,1)S(1)}, u32[]{:S(2)}, u32[]{:S(2)}) collective-permute-start(bf16[12,1728]{1,0:T(8,128)(2,1)S(1)} %select_n.107), channel_id=1, source_target_pairs={{0,1},{1,0},{2,5},{3,4},{4,9},{5,8},{6,13},{7,12},{8,65},{9,64},{1... | collective-permute-start | bytes 124424 | tf_op jit(solution)/shard_map/ppermute | solution.py:351
  10.3 5.1 %collective-permute-start.6 = (bf16[12,1728]{1,0:T(8,128)(2,1)S(1)}, bf16[12,1728]{1,0:T(8,128)(2,1)S(1)}, u32[]{:S(2)}, u32[]{:S(2)}) collective-permute-start(bf16[12,1728]{1,0:T(8,128)(2,1)S(1)} %select_n.109), channel_id=1, source_target_pairs={{0,0},{1,1},{2,4},{3,5},{4,8},{5,9},{6,12},{7,13},{8,64},{9,65},{1... | collective-permute-start | bytes 124424 | tf_op jit(solution)/shard_map/ppermute | solution.py:350
  15.5 3.7 %collective-permute-done.6 = bf16[12,1728]{1,0:T(8,128)(2,1)S(1)} collective-permute-done((bf16[12,1728]{1,0:T(8,128)(2,1)S(1)}, bf16[12,1728]{1,0:T(8,128)(2,1)S(1)}, u32[]{:S(2)}, u32[]{:S(2)}) %collective-permute-start.6) | collective-permute-done | bytes 41504 | tf_op jit(solution)/shard_map/ppermute | solution.py:350
  19.2 1.2 broadcast_in_dim.3
  20.5 3.8 %all-to-all-start = ((bf16[16,24,1728]{2,1,0:T(8,128)(2,1)}), bf16[16,24,1728]{2,1,0:T(8,128)(2,1)S(1)}, u32[]{:S(2)}, u32[]{:S(2)}) async-start(bf16[16,24,1728]{2,1,0:T(8,128)(2,1)} %broadcast_in_dim.3), calls=%async_computation | async-start | bytes 2752512 | tf_op jit(solution)/shard_map/all_to_all | solution.py:356
  24.3 1.8 %collective-permute-start = (bf16[256,384]{1,0:T(8,128)(2,1)S(1)}, bf16[256,384]{1,0:T(8,128)(2,1)S(1)}, u32[]{:S(2)}, u32[]{:S(2)}) collective-permute-start(bf16[256,384]{1,0:T(8,128)(2,1)S(1)} %copy-done.1), channel_id=1, source_target_pairs={{0,1},{1,2},{2,3},{3,4},{4,5},{5,6},{6,7},{7,8},{8,9},{9,10},{10,1... | collective-permute-start | bytes 589832 | tf_op jit(solution)/shard_map/ppermute | solution.py:358
  26.2 5.8 %collective-permute-done.x_ref = bf16[256,384]{1,0:T(8,128)(2,1)S(1)} collective-permute-done((bf16[256,384]{1,0:T(8,128)(2,1)S(1)}, bf16[256,384]{1,0:T(8,128)(2,1)S(1)}, u32[]{:S(2)}, u32[]{:S(2)}) %collective-permute-start) | collective-permute-done | bytes 196640 | tf_op jit(solution)/shard_map/ppermute | solution.py:358
  32.1 0.7 shard_map.50
  32.8 5.2 %collective-permute-start.1 = (bf16[96,256]{1,0:T(8,128)(2,1)S(1)}, bf16[96,256]{1,0:T(8,128)(2,1)S(1)}, u32[]{:S(2)}, u32[]{:S(2)}) collective-permute-start(bf16[96,256]{1,0:T(8,128)(2,1)S(1)} %get-tuple-element.21), channel_id=1, source_target_pairs={{0,0},{1,64},{2,1},{3,65},{4,4},{5,68},{6,5},{7,69},{8,8},{9,72},{... | collective-permute-start | bytes 147464 | tf_op jit(solution)/shard_map/ppermute | solution.py:362
  38.0 1.9 %collective-permute-start.2 = (bf16[96,256]{1,0:T(8,128)(2,1)S(1)}, bf16[96,256]{1,0:T(8,128)(2,1)S(1)}, u32[]{:S(2)}, u32[]{:S(2)}) collective-permute-start(bf16[96,256]{1,0:T(8,128)(2,1)S(1)} %get-tuple-element.22), channel_id=1, source_target_pairs={{0,64},{1,1},{2,65},{3,0},{4,68},{5,5},{6,69},{7,4},{8,72},{9,9},{... | collective-permute-start | bytes 147464 | tf_op jit(solution)/shard_map/ppermute | solution.py:362
  40.0 0.7 collective-permute-start.4
  40.7 30.6 %collective-permute-done.2.refs_1_ = bf16[96,256]{1,0:T(8,128)(2,1)S(1)} collective-permute-done((bf16[96,256]{1,0:T(8,128)(2,1)S(1)}, bf16[96,256]{1,0:T(8,128)(2,1)S(1)}, u32[]{:S(2)}, u32[]{:S(2)}) %collective-permute-start.2) | collective-permute-done | bytes 49184 | tf_op jit(solution)/shard_map/ppermute | solution.py:362
  71.3 0.8 shard_map.51
  72.2 6.0 %collective-permute-start.7 = (bf16[96,1024]{1,0:T(8,128)(2,1)S(1)}, bf16[96,1024]{1,0:T(8,128)(2,1)S(1)}, u32[]{:S(2)}, u32[]{:S(2)}) collective-permute-start(bf16[96,1024]{1,0:T(8,128)(2,1)S(1)} %get-tuple-element.26.a0), channel_id=1, source_target_pairs={{0,1},{1,2},{2,3},{3,0},{4,5},{5,6},{6,7},{7,4},{8,9},{9,10},{10,1... | collective-permute-start | bytes 589832 | tf_op jit(solution)/shard_map/ppermute | solution.py:74
  78.2 2.7 %collective-permute-start.8 = (bf16[96,1024]{1,0:T(8,128)(2,1)S(1)}, bf16[96,1024]{1,0:T(8,128)(2,1)S(1)}, u32[]{:S(2)}, u32[]{:S(2)}) collective-permute-start(bf16[96,1024]{1,0:T(8,128)(2,1)S(1)} %get-tuple-element.26.a0), channel_id=1, source_target_pairs={{0,2},{1,3},{2,0},{3,1},{4,6},{5,7},{6,4},{7,5},{8,10},{9,11},{10,... | collective-permute-start | bytes 589832 | tf_op jit(solution)/shard_map/ppermute | solution.py:74
  80.9 2.0 %collective-permute-start.9 = (bf16[96,1024]{1,0:T(8,128)(2,1)S(1)}, bf16[96,1024]{1,0:T(8,128)(2,1)S(1)}, u32[]{:S(2)}, u32[]{:S(2)}) collective-permute-start(bf16[96,1024]{1,0:T(8,128)(2,1)S(1)} %get-tuple-element.26.a0), channel_id=1, source_target_pairs={{0,3},{1,0},{2,1},{3,2},{4,7},{5,4},{6,5},{7,6},{8,11},{9,8},{10,9... | collective-permute-start | bytes 589832 | tf_op jit(solution)/shard_map/ppermute | solution.py:74
  82.9 5.9 %collective-permute-done.8.a2 = bf16[96,1024]{1,0:T(8,128)(2,1)S(1)} collective-permute-done((bf16[96,1024]{1,0:T(8,128)(2,1)S(1)}, bf16[96,1024]{1,0:T(8,128)(2,1)S(1)}, u32[]{:S(2)}, u32[]{:S(2)}) %collective-permute-start.8) | collective-permute-done | bytes 196640 | tf_op jit(solution)/shard_map/ppermute | solution.py:74
  88.8 2.4 %collective-permute-done.9.a3 = bf16[96,1024]{1,0:T(8,128)(2,1)S(1)} collective-permute-done((bf16[96,1024]{1,0:T(8,128)(2,1)S(1)}, bf16[96,1024]{1,0:T(8,128)(2,1)S(1)}, u32[]{:S(2)}, u32[]{:S(2)}) %collective-permute-start.9) | collective-permute-done | bytes 196640 | tf_op jit(solution)/shard_map/ppermute | solution.py:74
  91.2 2.8 %shard_map.52 = (bf16[384,1024]{1,0:T(8,128)(2,1)S(1)}, f32[96,1024]{1,0:T(8,128)S(1)}, f32[96,1024]{1,0:T(8,128)S(1)}) custom-call(s32[6]{0:T(128)S(1)} %stack.19.prm, bf16[384,1728]{1,0:T(8,128)(2,1)S(1)} %bitcast.15, bf16[96,1024]{1,0:T(8,128)(2,1)S(1)} %get-tuple-element.26.a0, bf16[96,1024]{1,0:T(8,128)(2,1)S(1)} %collective-permute-done.7.a1, ...), custom_call_target="tpu_custom_call" | custom-call | tf_op jit(solution)/shard_map/pallas_call | solution.py:324
  94.0 0.7 collective-permute-start.10
  94.7 1.3 collective-permute-done.10.got
  96.1 0.6 shard_map.53.mine
  96.7 1.7 %collective-permute-start.11 = (bf16[96,1024]{1,0:T(8,128)(2,1)S(1)}, bf16[96,1024]{1,0:T(8,128)(2,1)S(1)}, u32[]{:S(2)}, u32[]{:S(2)}) collective-permute-start(bf16[96,1024]{1,0:T(8,128)(2,1)S(1)} %shard_map.53.mine), channel_id=1, source_target_pairs={{0,128},{128,0},{1,129},{129,1},{2,130},{130,2},{3,131},{131,3},{4... | collective-permute-start | bytes 589832 | tf_op jit(solution)/shard_map/ppermute | solution.py:70
  98.4 4.2 %collective-permute-done.12.g = bf16[96,1024]{1,0:T(8,128)(2,1)S(1)} collective-permute-done((bf16[96,1024]{1,0:T(8,128)(2,1)S(1)}, bf16[96,1024]{1,0:T(8,128)(2,1)S(1)}, u32[]{:S(2)}, u32[]{:S(2)}) %collective-permute-start.12) | collective-permute-done | bytes 196640 | tf_op jit(solution)/shard_map/ppermute | solution.py:70
  102.6 4.2 %collective-permute-done.11.theirs = bf16[96,1024]{1,0:T(8,128)(2,1)S(1)} collective-permute-done((bf16[96,1024]{1,0:T(8,128)(2,1)S(1)}, bf16[96,1024]{1,0:T(8,128)(2,1)S(1)}, u32[]{:S(2)}, u32[]{:S(2)}) %collective-permute-start.11) | collective-permute-done | bytes 196640 | tf_op jit(solution)/shard_map/ppermute | solution.py:70
  106.8 1.0 shard_map.54
  107.8 1.0 collective-permute-start.13
  108.9 1.1 collective-permute-done.13.b_other
  110.0 4.2 %shard_map.58 = bf16[384,1728]{1,0:T(8,128)(2,1)} custom-call(s32[6]{0:T(128)S(1)} %stack.19.prm, bf16[384,1024]{1,0:T(8,128)(2,1)S(1)} %get-tuple-element.39.full, bf16[96,1024]{1,0:T(8,128)(2,1)S(1)} %get-tuple-element.30.b_own, bf16[96,1024]{1,0:T(8,128)(2,1)S(1)} %collective-permute-done.13.b_other), custom_call_target="tpu_custom_call" | custom-call | tf_op jit(solution)/shard_map/pallas_call | solution.py:324
  114.2 4.4 %all-to-all-start.1 = ((bf16[16,24,1728]{2,1,0:T(8,128)(2,1)}), bf16[16,24,1728]{2,1,0:T(8,128)(2,1)}, u32[]{:S(2)}, u32[]{:S(2)}) async-start(bf16[16,24,1728]{2,1,0:T(8,128)(2,1)} %bitcast.6), calls=%async_computation.1 | async-start | bytes 2752512 | tf_op jit(solution)/shard_map/all_to_all | solution.py:413
  118.6 4.8 %shard_map.55 = (f32[96,1024]{1,0:T(8,128)S(1)}, bf16[96,1024]{1,0:T(8,128)(2,1)S(1)}, bf16[96,1024]{1,0:T(8,128)(2,1)S(1)}, bf16[96,1024]{1,0:T(8,128)(2,1)S(1)}) custom-call(s32[6]{0:T(128)S(1)} %stack.19.prm, bf16[384,1728]{1,0:T(8,128)(2,1)S(1)} %bitcast.16, bf16[96,1024]{1,0:T(8,128)(2,1)S(1)} %get-tuple-element.30.b_own, ...), custom_call_target="tpu_custom_call" | custom-call | tf_op jit(solution)/shard_map/pallas_call | solution.py:324
  123.4 1.2 collective-permute-start.14
  124.5 1.0 collective-permute-start.15
  125.8 3.6 %collective-permute-done.14.r1 = bf16[96,1024]{1,0:T(8,128)(2,1)S(1)} collective-permute-done((bf16[96,1024]{1,0:T(8,128)(2,1)S(1)}, bf16[96,1024]{1,0:T(8,128)(2,1)S(1)}, u32[]{:S(2)}, u32[]{:S(2)}) %collective-permute-start.14) | collective-permute-done | bytes 196640 | tf_op jit(solution)/shard_map/ppermute | solution.py:74
  129.4 4.8 %collective-permute-done.15.r2 = bf16[96,1024]{1,0:T(8,128)(2,1)S(1)} collective-permute-done((bf16[96,1024]{1,0:T(8,128)(2,1)S(1)}, bf16[96,1024]{1,0:T(8,128)(2,1)S(1)}, u32[]{:S(2)}, u32[]{:S(2)}) %collective-permute-start.15) | collective-permute-done | bytes 196640 | tf_op jit(solution)/shard_map/ppermute | solution.py:74
  134.2 1.0 collective-permute-done.16.r3
  135.3 0.8 shard_map.56
  136.0 2.8 %collective-permute-start.17 = (bf16[96,256]{1,0:T(8,128)(2,1)S(1)}, bf16[96,256]{1,0:T(8,128)(2,1)S(1)}, u32[]{:S(2)}, u32[]{:S(2)}) collective-permute-start(bf16[96,256]{1,0:T(8,128)(2,1)S(1)} %get-tuple-element.35), channel_id=1, source_target_pairs={{64,0},{1,1},{65,2},{4,3},{68,4},{5,5},{69,6},{8,7},{72,8},{9,9},{... | collective-permute-start | bytes 147464 | tf_op jit(solution)/shard_map/ppermute | solution.py:408
  138.9 4.1 %collective-permute-start.18 = (bf16[96,256]{1,0:T(8,128)(2,1)S(1)}, bf16[96,256]{1,0:T(8,128)(2,1)S(1)}, u32[]{:S(2)}, u32[]{:S(2)}) collective-permute-start(bf16[96,256]{1,0:T(8,128)(2,1)S(1)} %get-tuple-element.36), channel_id=1, source_target_pairs={{1,0},{65,1},{0,2},{68,3},{5,4},{69,5},{4,6},{72,7},{9,8},{73,9},{... | collective-permute-start | bytes 147464 | tf_op jit(solution)/shard_map/ppermute | solution.py:408
  142.9 0.7 collective-permute-start.19
  143.6 7.0 %collective-permute-start.20 = (bf16[96,256]{1,0:T(8,128)(2,1)S(1)}, bf16[96,256]{1,0:T(8,128)(2,1)S(1)}, u32[]{:S(2)}, u32[]{:S(2)}) collective-permute-start(bf16[96,256]{1,0:T(8,128)(2,1)S(1)} %get-tuple-element.38), channel_id=1, source_target_pairs={{0,0},{64,1},{1,2},{69,3},{4,4},{68,5},{5,6},{73,7},{8,8},{72,9},{... | collective-permute-start | bytes 147464 | tf_op jit(solution)/shard_map/ppermute | solution.py:408
  150.6 1.6 fusion
  152.2 6.4 %collective-permute-start.21 = (bf16[12,1728]{1,0:T(8,128)(2,1)S(1)}, bf16[12,1728]{1,0:T(8,128)(2,1)S(1)}, u32[]{:S(2)}, u32[]{:S(2)}) collective-permute-start(bf16[12,1728]{1,0:T(8,128)(2,1)S(1)} %get-tuple-element.56), channel_id=1, source_target_pairs={{1,0},{0,1},{5,2},{4,3},{9,4},{8,5},{13,6},{12,7},{65,8},{64,9},{6... | collective-permute-start | bytes 124424 | tf_op jit(solution)/shard_map/ppermute | solution.py:421
  158.5 4.7 %collective-permute-start.22 = (bf16[12,1728]{1,0:T(8,128)(2,1)S(1)}, bf16[12,1728]{1,0:T(8,128)(2,1)S(1)}, u32[]{:S(2)}, u32[]{:S(2)}) collective-permute-start(bf16[12,1728]{1,0:T(8,128)(2,1)S(1)} %get-tuple-element.57), channel_id=1, source_target_pairs={{0,0},{1,1},{4,2},{5,3},{8,4},{9,5},{12,6},{13,7},{64,8},{65,9},{6... | collective-permute-start | bytes 124424 | tf_op jit(solution)/shard_map/ppermute | solution.py:420
  163.2 1.4 shard_map.57
  164.6 4.8 %collective-permute-done.22 = bf16[12,1728]{1,0:T(8,128)(2,1)S(1)} collective-permute-done((bf16[12,1728]{1,0:T(8,128)(2,1)S(1)}, bf16[12,1728]{1,0:T(8,128)(2,1)S(1)}, u32[]{:S(2)}, u32[]{:S(2)}) %collective-permute-start.22) | collective-permute-done | bytes 41504 | tf_op jit(solution)/shard_map/ppermute | solution.py:420
  170.0 0.7 copy.9
  (35 shorter events, 1.4 us)
Async XLA Ops:
  2.0 13.4 %collective-permute-start.5 = (bf16[12,1728]{1,0:T(8,128)(2,1)S(1)}, bf16[12,1728]{1,0:T(8,128)(2,1)S(1)}, u32[]{:S(2)}, u32[]{:S(2)}) collective-permute-start(bf16[12,1728]{1,0:T(8,128)(2,1)S(1)} %select_n.107), channel_id=1, source_target_pairs={{0,1},{1,0},{2,5},{3,4},{4,9},{5,8},{6,13},{7,12},{8,65},{9,64},{1... | collective-permute-start | bytes 124424 | tf_op jit(solution)/shard_map/ppermute | solution.py:351
  10.3 8.9 %collective-permute-start.6 = (bf16[12,1728]{1,0:T(8,128)(2,1)S(1)}, bf16[12,1728]{1,0:T(8,128)(2,1)S(1)}, u32[]{:S(2)}, u32[]{:S(2)}) collective-permute-start(bf16[12,1728]{1,0:T(8,128)(2,1)S(1)} %select_n.109), channel_id=1, source_target_pairs={{0,0},{1,1},{2,4},{3,5},{4,8},{5,9},{6,12},{7,13},{8,64},{9,65},{1... | collective-permute-start | bytes 124424 | tf_op jit(solution)/shard_map/ppermute | solution.py:350
  20.5 3.8 %copy-start.1 = (bf16[256,384]{1,0:T(8,128)(2,1)S(1)}, bf16[256,384]{1,0:T(8,128)(2,1)}, u32[]{:S(2)}) copy-start(bf16[256,384]{1,0:T(8,128)(2,1)} %param.3) | copy-start | bytes 589828
  20.5 5.7 %copy-start = (s32[2,2]{1,0:T(2,128)S(1)}, s32[2,2]{1,0:T(2,128)}, u32[]{:S(2)}) copy-start(s32[2,2]{1,0:T(2,128)} %param.5) | copy-start | bytes 52
  20.5 70.7 %all-to-all-start = ((bf16[16,24,1728]{2,1,0:T(8,128)(2,1)}), bf16[16,24,1728]{2,1,0:T(8,128)(2,1)S(1)}, u32[]{:S(2)}, u32[]{:S(2)}) async-start(bf16[16,24,1728]{2,1,0:T(8,128)(2,1)} %broadcast_in_dim.3), calls=%async_computation | async-start | bytes 2752512 | tf_op jit(solution)/shard_map/all_to_all | solution.py:356
  24.3 7.8 %collective-permute-start = (bf16[256,384]{1,0:T(8,128)(2,1)S(1)}, bf16[256,384]{1,0:T(8,128)(2,1)S(1)}, u32[]{:S(2)}, u32[]{:S(2)}) collective-permute-start(bf16[256,384]{1,0:T(8,128)(2,1)S(1)} %copy-done.1), channel_id=1, source_target_pairs={{0,1},{1,2},{2,3},{3,4},{4,5},{5,6},{6,7},{7,8},{8,9},{9,10},{10,1... | collective-permute-start | bytes 589832 | tf_op jit(solution)/shard_map/ppermute | solution.py:358
  32.8 7.9 %collective-permute-start.1 = (bf16[96,256]{1,0:T(8,128)(2,1)S(1)}, bf16[96,256]{1,0:T(8,128)(2,1)S(1)}, u32[]{:S(2)}, u32[]{:S(2)}) collective-permute-start(bf16[96,256]{1,0:T(8,128)(2,1)S(1)} %get-tuple-element.21), channel_id=1, source_target_pairs={{0,0},{1,64},{2,1},{3,65},{4,4},{5,68},{6,5},{7,69},{8,8},{9,72},{... | collective-permute-start | bytes 147464 | tf_op jit(solution)/shard_map/ppermute | solution.py:362
  38.0 33.3 %collective-permute-start.2 = (bf16[96,256]{1,0:T(8,128)(2,1)S(1)}, bf16[96,256]{1,0:T(8,128)(2,1)S(1)}, u32[]{:S(2)}, u32[]{:S(2)}) collective-permute-start(bf16[96,256]{1,0:T(8,128)(2,1)S(1)} %get-tuple-element.22), channel_id=1, source_target_pairs={{0,64},{1,1},{2,65},{3,0},{4,68},{5,5},{6,69},{7,4},{8,72},{9,9},{... | collective-permute-start | bytes 147464 | tf_op jit(solution)/shard_map/ppermute | solution.py:362
  39.9 31.4 %collective-permute-start.3 = (bf16[96,256]{1,0:T(8,128)(2,1)S(1)}, bf16[96,256]{1,0:T(8,128)(2,1)S(1)}, u32[]{:S(2)}, u32[]{:S(2)}) collective-permute-start(bf16[96,256]{1,0:T(8,128)(2,1)S(1)} %get-tuple-element.23), channel_id=1, source_target_pairs={{0,1},{1,65},{2,0},{3,64},{4,5},{5,69},{6,4},{7,68},{8,9},{9,73},{... | collective-permute-start | bytes 147464 | tf_op jit(solution)/shard_map/ppermute | solution.py:362
  40.0 31.3 %collective-permute-start.4 = (bf16[96,256]{1,0:T(8,128)(2,1)S(1)}, bf16[96,256]{1,0:T(8,128)(2,1)S(1)}, u32[]{:S(2)}, u32[]{:S(2)}) collective-permute-start(bf16[96,256]{1,0:T(8,128)(2,1)S(1)} %get-tuple-element.24), channel_id=1, source_target_pairs={{0,65},{1,0},{2,64},{3,1},{4,69},{5,4},{6,68},{7,5},{8,73},{9,8},{... | collective-permute-start | bytes 147464 | tf_op jit(solution)/shard_map/ppermute | solution.py:362
  72.2 10.7 %collective-permute-start.7 = (bf16[96,1024]{1,0:T(8,128)(2,1)S(1)}, bf16[96,1024]{1,0:T(8,128)(2,1)S(1)}, u32[]{:S(2)}, u32[]{:S(2)}) collective-permute-start(bf16[96,1024]{1,0:T(8,128)(2,1)S(1)} %get-tuple-element.26.a0), channel_id=1, source_target_pairs={{0,1},{1,2},{2,3},{3,0},{4,5},{5,6},{6,7},{7,4},{8,9},{9,10},{10,1... | collective-permute-start | bytes 589832 | tf_op jit(solution)/shard_map/ppermute | solution.py:74
  78.2 10.6 %collective-permute-start.8 = (bf16[96,1024]{1,0:T(8,128)(2,1)S(1)}, bf16[96,1024]{1,0:T(8,128)(2,1)S(1)}, u32[]{:S(2)}, u32[]{:S(2)}) collective-permute-start(bf16[96,1024]{1,0:T(8,128)(2,1)S(1)} %get-tuple-element.26.a0), channel_id=1, source_target_pairs={{0,2},{1,3},{2,0},{3,1},{4,6},{5,7},{6,4},{7,5},{8,10},{9,11},{10,... | collective-permute-start | bytes 589832 | tf_op jit(solution)/shard_map/ppermute | solution.py:74
  80.9 10.3 %collective-permute-start.9 = (bf16[96,1024]{1,0:T(8,128)(2,1)S(1)}, bf16[96,1024]{1,0:T(8,128)(2,1)S(1)}, u32[]{:S(2)}, u32[]{:S(2)}) collective-permute-start(bf16[96,1024]{1,0:T(8,128)(2,1)S(1)} %get-tuple-element.26.a0), channel_id=1, source_target_pairs={{0,3},{1,0},{2,1},{3,2},{4,7},{5,4},{6,5},{7,6},{8,11},{9,8},{10,9... | collective-permute-start | bytes 589832 | tf_op jit(solution)/shard_map/ppermute | solution.py:74
  94.0 2.1 %collective-permute-start.10 = (f32[96,1024]{1,0:T(8,128)S(1)}, f32[96,1024]{1,0:T(8,128)S(1)}, u32[]{:S(2)}, u32[]{:S(2)}) collective-permute-start(f32[96,1024]{1,0:T(8,128)S(1)} %get-tuple-element.28), channel_id=1, source_target_pairs={{0,64},{64,0},{1,65},{65,1},{2,66},{66,2},{3,67},{67,3},{4,68},{68... | collective-permute-start | bytes 1179656 | tf_op jit(solution)/shard_map/ppermute | solution.py:70
  94.7 7.9 %collective-permute-start.12 = (bf16[96,1024]{1,0:T(8,128)(2,1)S(1)}, bf16[96,1024]{1,0:T(8,128)(2,1)S(1)}, u32[]{:S(2)}, u32[]{:S(2)}) collective-permute-start(bf16[96,1024]{1,0:T(8,128)(2,1)S(1)} %get-tuple-element.25.x), channel_id=1, source_target_pairs={{0,128},{128,0},{1,129},{129,1},{2,130},{130,2},{3,131},{131,3},{4... | collective-permute-start | bytes 589832 | tf_op jit(solution)/shard_map/ppermute | solution.py:70
  96.7 10.1 %collective-permute-start.11 = (bf16[96,1024]{1,0:T(8,128)(2,1)S(1)}, bf16[96,1024]{1,0:T(8,128)(2,1)S(1)}, u32[]{:S(2)}, u32[]{:S(2)}) collective-permute-start(bf16[96,1024]{1,0:T(8,128)(2,1)S(1)} %shard_map.53.mine), channel_id=1, source_target_pairs={{0,128},{128,0},{1,129},{129,1},{2,130},{130,2},{3,131},{131,3},{4... | collective-permute-start | bytes 589832 | tf_op jit(solution)/shard_map/ppermute | solution.py:70
  107.8 2.1 %collective-permute-start.13 = (bf16[96,1024]{1,0:T(8,128)(2,1)S(1)}, bf16[96,1024]{1,0:T(8,128)(2,1)S(1)}, u32[]{:S(2)}, u32[]{:S(2)}) collective-permute-start(bf16[96,1024]{1,0:T(8,128)(2,1)S(1)} %get-tuple-element.30.b_own), channel_id=1, source_target_pairs={{0,64},{64,0},{1,65},{65,1},{2,66},{66,2},{3,67},{67,3},{4,68},{68... | collective-permute-start | bytes 589832 | tf_op jit(solution)/shard_map/ppermute | solution.py:70
  114.2 36.3 %all-to-all-start.1 = ((bf16[16,24,1728]{2,1,0:T(8,128)(2,1)}), bf16[16,24,1728]{2,1,0:T(8,128)(2,1)}, u32[]{:S(2)}, u32[]{:S(2)}) async-start(bf16[16,24,1728]{2,1,0:T(8,128)(2,1)} %bitcast.6), calls=%async_computation.1 | async-start | bytes 2752512 | tf_op jit(solution)/shard_map/all_to_all | solution.py:413
  123.4 6.1 %collective-permute-start.14 = (bf16[96,1024]{1,0:T(8,128)(2,1)S(1)}, bf16[96,1024]{1,0:T(8,128)(2,1)S(1)}, u32[]{:S(2)}, u32[]{:S(2)}) collective-permute-start(bf16[96,1024]{1,0:T(8,128)(2,1)S(1)} %get-tuple-element.32), channel_id=1, source_target_pairs={{0,1},{1,2},{2,3},{3,0},{4,5},{5,6},{6,7},{7,4},{8,9},{9,10},{10,1... | collective-permute-start | bytes 589832 | tf_op jit(solution)/shard_map/ppermute | solution.py:74
  124.5 9.7 %collective-permute-start.15 = (bf16[96,1024]{1,0:T(8,128)(2,1)S(1)}, bf16[96,1024]{1,0:T(8,128)(2,1)S(1)}, u32[]{:S(2)}, u32[]{:S(2)}) collective-permute-start(bf16[96,1024]{1,0:T(8,128)(2,1)S(1)} %get-tuple-element.33), channel_id=1, source_target_pairs={{0,2},{1,3},{2,0},{3,1},{4,6},{5,7},{6,4},{7,5},{8,10},{9,11},{10,... | collective-permute-start | bytes 589832 | tf_op jit(solution)/shard_map/ppermute | solution.py:74
  125.6 9.7 %collective-permute-start.16 = (bf16[96,1024]{1,0:T(8,128)(2,1)S(1)}, bf16[96,1024]{1,0:T(8,128)(2,1)S(1)}, u32[]{:S(2)}, u32[]{:S(2)}) collective-permute-start(bf16[96,1024]{1,0:T(8,128)(2,1)S(1)} %get-tuple-element.34), channel_id=1, source_target_pairs={{0,3},{1,0},{2,1},{3,2},{4,7},{5,4},{6,5},{7,6},{8,11},{9,8},{10,9... | collective-permute-start | bytes 589832 | tf_op jit(solution)/shard_map/ppermute | solution.py:74
  136.0 22.5 %collective-permute-start.17 = (bf16[96,256]{1,0:T(8,128)(2,1)S(1)}, bf16[96,256]{1,0:T(8,128)(2,1)S(1)}, u32[]{:S(2)}, u32[]{:S(2)}) collective-permute-start(bf16[96,256]{1,0:T(8,128)(2,1)S(1)} %get-tuple-element.35), channel_id=1, source_target_pairs={{64,0},{1,1},{65,2},{4,3},{68,4},{5,5},{69,6},{8,7},{72,8},{9,9},{... | collective-permute-start | bytes 147464 | tf_op jit(solution)/shard_map/ppermute | solution.py:408
  138.9 24.3 %collective-permute-start.18 = (bf16[96,256]{1,0:T(8,128)(2,1)S(1)}, bf16[96,256]{1,0:T(8,128)(2,1)S(1)}, u32[]{:S(2)}, u32[]{:S(2)}) collective-permute-start(bf16[96,256]{1,0:T(8,128)(2,1)S(1)} %get-tuple-element.36), channel_id=1, source_target_pairs={{1,0},{65,1},{0,2},{68,3},{5,4},{69,5},{4,6},{72,7},{9,8},{73,9},{... | collective-permute-start | bytes 147464 | tf_op jit(solution)/shard_map/ppermute | solution.py:408
  142.9 20.3 %collective-permute-start.19 = (bf16[96,256]{1,0:T(8,128)(2,1)S(1)}, bf16[96,256]{1,0:T(8,128)(2,1)S(1)}, u32[]{:S(2)}, u32[]{:S(2)}) collective-permute-start(bf16[96,256]{1,0:T(8,128)(2,1)S(1)} %get-tuple-element.37), channel_id=1, source_target_pairs={{65,0},{0,1},{64,2},{5,3},{69,4},{4,5},{68,6},{9,7},{73,8},{8,9},{... | collective-permute-start | bytes 147464 | tf_op jit(solution)/shard_map/ppermute | solution.py:408
  143.6 19.6 %collective-permute-start.20 = (bf16[96,256]{1,0:T(8,128)(2,1)S(1)}, bf16[96,256]{1,0:T(8,128)(2,1)S(1)}, u32[]{:S(2)}, u32[]{:S(2)}) collective-permute-start(bf16[96,256]{1,0:T(8,128)(2,1)S(1)} %get-tuple-element.38), channel_id=1, source_target_pairs={{0,0},{64,1},{1,2},{69,3},{4,4},{68,5},{5,6},{73,7},{8,8},{72,9},{... | collective-permute-start | bytes 147464 | tf_op jit(solution)/shard_map/ppermute | solution.py:408
  152.2 12.4 %collective-permute-start.21 = (bf16[12,1728]{1,0:T(8,128)(2,1)S(1)}, bf16[12,1728]{1,0:T(8,128)(2,1)S(1)}, u32[]{:S(2)}, u32[]{:S(2)}) collective-permute-start(bf16[12,1728]{1,0:T(8,128)(2,1)S(1)} %get-tuple-element.56), channel_id=1, source_target_pairs={{1,0},{0,1},{5,2},{4,3},{9,4},{8,5},{13,6},{12,7},{65,8},{64,9},{6... | collective-permute-start | bytes 124424 | tf_op jit(solution)/shard_map/ppermute | solution.py:421
  158.5 10.9 %collective-permute-start.22 = (bf16[12,1728]{1,0:T(8,128)(2,1)S(1)}, bf16[12,1728]{1,0:T(8,128)(2,1)S(1)}, u32[]{:S(2)}, u32[]{:S(2)}) collective-permute-start(bf16[12,1728]{1,0:T(8,128)(2,1)S(1)} %get-tuple-element.57), channel_id=1, source_target_pairs={{0,0},{1,1},{4,2},{5,3},{8,4},{9,5},{12,6},{13,7},{64,8},{65,9},{6... | collective-permute-start | bytes 124424 | tf_op jit(solution)/shard_map/ppermute | solution.py:420
